TPU v7x, 256 devices: a whole 4x4x8 slice. The times are simulated.
256 devices in a mesh: seq: 32 (over z, x), chan: 8 (over y, core).
Axes of the slice: x: 4, y: 4, z: 8, core: 2. Of those that a mesh axis runs over, the one named last changes fastest.
Arguments:
- tokens: int32 [8192], P('seq'), may hold values from 0 to 255
- embed_table: bfloat16 [256, 2048], P(None, 'chan'), may hold values from -6 to 6
- short_conv: float32 [3, 2048], P(None, 'chan'), may hold values from -4 to 4
- query_branch: bfloat16 [8192, 2048], P('seq', 'chan'), may hold values from -6 to 6
- key_branch: bfloat16 [8192, 2048], P('seq', 'chan'), may hold values from -6 to 6
- decay_rate: float32 [2048], P('chan'), may hold values from 1.2207031e-05 to 0.1, as said below
- weight_first: float32 [33, 64], replicated, may hold values from -1 to 1
- weight_second: float32 [64, 64], replicated, may hold values from -0.75 to 0.75
- weight_third: float32 [64, 2048], P(None, 'chan'), may hold values from -0.75 to 0.75
- skip_gain: float32 [2048], P('chan'), may hold values from -4 to 4
- cotangent: bfloat16 [8192, 2048], P('seq', 'chan'), may hold values from -6 to 6
Outputs:
- operator_out: bfloat16 [8192, 2048], P('seq', 'chan')
- grad_query: bfloat16 [8192, 2048], P('seq', 'chan')
- grad_key: bfloat16 [8192, 2048], P('seq', 'chan')
- grad_embed: float32 [256, 2048], P('seq', 'chan')
- grad_short: float32 [3, 2048], P(None, 'chan')
- grad_skip: float32 [2048], P('chan')
- grad_first: float32 [33, 64], replicated
- grad_second: float32 [64, 64], replicated
- grad_third: float32 [64, 2048], P(None, 'chan')
Inputs may be any that keep to these rules, and one draw needn't show every extreme that they name: `decay_rate`: each channel's decay rate is either slow, log-uniform from 0.1 / 8192 to 2 / 8192, or fast, log-uniform from 0.02 to 0.1, clipped to the stated range.
All inputs are finite; a program needn't handle non-finite values.
Results may differ from a plain program's by a relative error of at most 0.0014.
Values sent between devices are 32-bit elements; how exact they have to be, the bound alone decides.
No kernel may reach another device: no remote copies, remote signals or barrier semaphores. Data moves between devices by JAX's collectives and lax.ppermute only.
A program may use at most 64 MiB of HBM per device.

v0:
```python
import math

import jax
import jax.numpy as jnp
from jax import lax
from jax.sharding import PartitionSpec as P

BANDS = 16


highest = lax.Precision.HIGHEST
two_pi = 2.0 * math.pi


def from_partner(block, axis, bit):
    count = lax.axis_size(axis)
    route = []
    for low in range(count):
        high = low | 1 << bit
        if high != low and high < count:
            route += [(low, high), (high, low)]
    return lax.ppermute(block, axis, route)


def from_behind(value, axis, steps):
    count = lax.axis_size(axis)
    leading, last = (max(0, -steps), min(count, count - steps))
    return lax.ppermute(value, axis, [(source, source + steps) for source in range(leading, last)])


def features(positions, length):
    frequency = 2 ** jnp.arange(BANDS, dtype=jnp.int32) + 1
    phases = positions[:, None] * frequency[None, :] % length
    angles = phases.astype(jnp.float32) * (two_pi / length)
    ramp_col = positions.astype(jnp.float32)[:, None] / length
    return jnp.concatenate([ramp_col, jnp.cos(angles), jnp.sin(angles)], axis=1)


def filter_forward(positions, length, weight_first, weight_second, weight_third, decay_rate):
    embedding = features(positions, length)
    pre_one = jnp.dot(
        embedding, weight_first, precision=highest, preferred_element_type=jnp.float32
    )
    act_one = jnp.sin(pre_one)
    pre_two = jnp.dot(act_one, weight_second, precision=highest, preferred_element_type=jnp.float32)
    act_two = jnp.sin(pre_two)
    shaped = jnp.dot(act_two, weight_third, precision=highest, preferred_element_type=jnp.float32)
    scaling = jnp.sqrt(jnp.expm1(-2.0 * decay_rate) / jnp.expm1(-2.0 * length * decay_rate))
    window = scaling[None, :] * jnp.exp(
        -decay_rate[None, :] * positions.astype(jnp.float32)[:, None]
    )
    return (shaped * window, (window, embedding, pre_one, act_one, pre_two, act_two))


def filter_head(grad_filter, saved_acts, weight_third):
    window, embedding, pre_one, act_one, pre_two, act_two = saved_acts
    grad_shaped = grad_filter * window
    grad_third = jnp.dot(
        act_two.T, grad_shaped, precision=highest, preferred_element_type=jnp.float32
    )
    grad_act_two = jnp.dot(
        grad_shaped, weight_third.T, precision=highest, preferred_element_type=jnp.float32
    )
    return (grad_third, grad_act_two)


def filter_tail(grad_act_two, saved_acts, weight_second):
    window, embedding, pre_one, act_one, pre_two, act_two = saved_acts
    grad_pre_two = grad_act_two * jnp.cos(pre_two)
    grad_second = jnp.dot(
        act_one.T, grad_pre_two, precision=highest, preferred_element_type=jnp.float32
    )
    grad_act_one = jnp.dot(
        grad_pre_two, weight_second.T, precision=highest, preferred_element_type=jnp.float32
    )
    grad_pre_one = grad_act_one * jnp.cos(pre_one)
    grad_first = jnp.dot(
        embedding.T, grad_pre_one, precision=highest, preferred_element_type=jnp.float32
    )
    return (grad_first, grad_second)


def rotation(first_index, second_index, modulus):
    phases = first_index * second_index % modulus
    angles = phases.astype(jnp.float32) * (two_pi / modulus)
    return (jnp.cos(angles), jnp.sin(angles))


def rotate(complex_state, cosine_part, sine_part, sign_flip):
    real_part = complex_state[0] * cosine_part + sign_flip * (complex_state[1] * sine_part)
    imag_part = complex_state[1] * cosine_part - sign_flip * (complex_state[0] * sine_part)
    return jnp.stack([real_part, imag_part])


def scaled(factor, complex_state):
    real_part = factor[0] * complex_state[0] - factor[1] * complex_state[1]
    imag_part = factor[0] * complex_state[1] + factor[1] * complex_state[0]
    return jnp.stack([real_part, imag_part])


def block_dft(complex_state, sign_flip):
    points_in = complex_state.shape[2]
    grid_index = jnp.arange(points_in, dtype=jnp.int32)
    cosine_part, sine_part = rotation(grid_index[:, None], grid_index[None, :], points_in)
    tables = jnp.concatenate([cosine_part, sine_part], axis=0)
    both_parts = jnp.einsum("kn,ranc->rakc", tables, complex_state, precision=highest)
    real_part = both_parts[0, :, :points_in] + sign_flip * both_parts[1, :, points_in:]
    imag_part = both_parts[1, :, :points_in] - sign_flip * both_parts[0, :, points_in:]
    return jnp.stack([real_part, imag_part])


def spectrum_section(complex_state, kappa_index, points):
    depth_rows = complex_state.shape[2]
    lane_index = 2 * kappa_index + jnp.arange(2, dtype=jnp.int32)
    cosine_part, sine_part = rotation(
        lane_index[:, None], jnp.arange(depth_rows, dtype=jnp.int32)[None, :], points
    )
    turned = rotate(complex_state, cosine_part[:, :, None], sine_part[:, :, None], 1.0)
    return block_dft(turned, 1.0)


def unspectrum_section(complex_state, kappa_index, points):
    depth_rows = complex_state.shape[2]
    lane_index = 2 * kappa_index + jnp.arange(2, dtype=jnp.int32)
    local_state = block_dft(complex_state, -1.0)
    cosine_part, sine_part = rotation(
        lane_index[:, None], jnp.arange(depth_rows, dtype=jnp.int32)[None, :], points
    )
    return rotate(local_state, cosine_part[:, :, None], sine_part[:, :, None], -1.0)


def forward_factors(upper_half, angle):
    cosine_val = jnp.cos(angle)
    sine_val = jnp.sin(angle)
    first_factor = (jnp.where(upper_half, -cosine_val, 1.0), jnp.where(upper_half, -sine_val, 0.0))
    second_factor = (jnp.where(upper_half, cosine_val, 1.0), jnp.where(upper_half, sine_val, 0.0))
    return (first_factor, second_factor)


def inverse_factors(upper_half, angle):
    cosine_val = jnp.cos(angle)
    sine_val = jnp.sin(angle)
    first_factor = (jnp.where(upper_half, -cosine_val, 1.0), jnp.where(upper_half, -sine_val, 0.0))
    second_factor = (jnp.where(upper_half, 1.0, cosine_val), jnp.where(upper_half, 0.0, sine_val))
    return (first_factor, second_factor)


def reversed_index(seq_index, levels):
    total_index = jnp.zeros((), jnp.int32)
    for bit_number in range(levels):
        total_index = total_index + seq_index // 2**bit_number % 2 * 2 ** (levels - 1 - bit_number)
    return total_index


def butterfly_forward(signals, seq_index, seq_count, points):
    levels = seq_count.bit_length() - 1
    half_count = seq_count // 2
    partners = from_partner((signals[0], signals[1], signals[2]), "seq", levels - 1)
    other_index = jnp.bitwise_xor(seq_index, half_count)
    upper_half = seq_index // half_count % 2 == 1
    twist = -two_pi * (seq_index % half_count).astype(jnp.float32) / (2 * half_count)
    first_factor, second_factor = forward_factors(upper_half, twist)
    branch_ids = jnp.arange(2, dtype=jnp.float32)
    own_angle = -math.pi * branch_ids * seq_index.astype(jnp.float32) / seq_count
    far_angle = -math.pi * branch_ids * other_index.astype(jnp.float32) / seq_count
    own_factor = scaled(first_factor, (jnp.cos(own_angle), jnp.sin(own_angle)))
    far_factor = scaled(second_factor, (jnp.cos(far_angle), jnp.sin(far_angle)))
    states = tuple(
        (
            own_factor[:, :, None, None] * own_rows[None, None]
            + far_factor[:, :, None, None] * theirs[None, None]
            for own_rows, theirs in zip(signals, partners)
        )
    )
    for bit_number in range(levels - 2, -1, -1):
        span_size = 2**bit_number
        received = from_partner((states[0], states[1], states[2]), "seq", bit_number)
        upper_half = seq_index // span_size % 2 == 1
        twist = -two_pi * (seq_index % span_size).astype(jnp.float32) / (2 * span_size)
        first_factor, second_factor = forward_factors(upper_half, twist)
        states = tuple(
            (
                scaled(first_factor, own_state) + scaled(second_factor, far_state)
                for own_state, far_state in zip(states, received)
            )
        )
    kappa_index = reversed_index(seq_index, levels)
    return tuple((spectrum_section(own_state, kappa_index, points) for own_state in states))


def butterfly_inverse(spectra, seq_index, seq_count, points):
    levels = seq_count.bit_length() - 1
    kappa_index = reversed_index(seq_index, levels)
    states = tuple((unspectrum_section(own_state, kappa_index, points) for own_state in spectra))
    for bit_number in range(levels):
        span_size = 2**bit_number
        received = from_partner((states[0], states[1], states[2]), "seq", bit_number)
        upper_half = seq_index // span_size % 2 == 1
        twist = two_pi * (seq_index % span_size).astype(jnp.float32) / (2 * span_size)
        first_factor, second_factor = inverse_factors(upper_half, twist)
        states = tuple(
            (
                scaled(first_factor, own_state) + scaled(second_factor, far_state)
                for own_state, far_state in zip(states, received)
            )
        )
    branch_ids = jnp.arange(2, dtype=jnp.float32)
    turn_angle = math.pi * branch_ids * seq_index.astype(jnp.float32) / seq_count
    cosine_val = jnp.cos(turn_angle)[:, None, None]
    sine_val = jnp.sin(turn_angle)[:, None, None]
    return tuple(
        (
            jnp.sum(own_state[0] * cosine_val - own_state[1] * sine_val, axis=0) / points
            for own_state in states
        )
    )


def pointwise(spectra):
    keyed_spec, filter_spec, grad_spec = spectra
    conv_spec = jnp.stack(
        [
            keyed_spec[0] * filter_spec[0] - keyed_spec[1] * filter_spec[1],
            keyed_spec[0] * filter_spec[1] + keyed_spec[1] * filter_spec[0],
        ]
    )
    back_spec = jnp.stack(
        [
            filter_spec[0] * grad_spec[0] + filter_spec[1] * grad_spec[1],
            filter_spec[0] * grad_spec[1] - filter_spec[1] * grad_spec[0],
        ]
    )
    shape_spec = jnp.stack(
        [
            keyed_spec[0] * grad_spec[0] + keyed_spec[1] * grad_spec[1],
            keyed_spec[0] * grad_spec[1] - keyed_spec[1] * grad_spec[0],
        ]
    )
    return (conv_spec, back_spec, shape_spec)


def per_device(
    tokens,
    embed_table,
    short_conv,
    query_branch,
    key_branch,
    decay_rate,
    weight_first,
    weight_second,
    weight_third,
    skip_gain,
    cotangent,
):
    seq_count = lax.axis_size("seq")
    seq_index = lax.axis_index("seq")
    row_count = query_branch.shape[0]
    length = row_count * seq_count
    points = 2 * length
    inv_root = 1.0 / math.sqrt(length)
    vocab_size = embed_table.shape[0]
    earlier = from_behind(tokens[row_count - 2 :], "seq", 1)
    window_ids = jnp.concatenate([earlier, tokens])
    row_start = seq_index * row_count
    window_pos = row_start + jnp.arange(row_count + 2, dtype=jnp.int32) - 2
    present = window_pos >= 0
    vocab_ids = jnp.arange(vocab_size, dtype=jnp.int32)
    lookup = ((window_ids[:, None] == vocab_ids[None, :]) & present[:, None]).astype(jnp.bfloat16)
    embedded = jnp.dot(lookup, embed_table, preferred_element_type=jnp.float32)
    value_branch = (
        short_conv[0] * embedded[2:]
        + short_conv[1] * embedded[1:-1]
        + short_conv[2] * embedded[:-2]
    )
    key_rows = key_branch.astype(jnp.float32)
    keyed_value = key_rows * value_branch
    query_rows = query_branch.astype(jnp.float32)
    grad_out = cotangent.astype(jnp.float32)
    grad_z = grad_out * query_rows
    positions = row_start + jnp.arange(row_count, dtype=jnp.int32)
    filter_rows, tail_acts = filter_forward(
        positions, length, weight_first, weight_second, weight_third, decay_rate
    )
    spectra = butterfly_forward((keyed_value, filter_rows, grad_z), seq_index, seq_count, points)
    returned = butterfly_inverse(pointwise(spectra), seq_index, seq_count, points)
    convolved, back_keyed, grad_filter = returned
    third_part, act_two_part = filter_head(grad_filter, tail_acts, weight_third)
    inner_sum = convolved + skip_gain * keyed_value
    operator_out = (query_rows * inner_sum).astype(jnp.bfloat16)
    grad_query = (grad_out * inner_sum).astype(jnp.bfloat16)
    grad_keyed = back_keyed + skip_gain * grad_z
    grad_key = (grad_keyed * value_branch).astype(jnp.bfloat16)
    grad_value = grad_keyed * key_rows
    short_part = jnp.stack(
        [
            jnp.sum(grad_value * embedded[2 - offset : 2 - offset + row_count], axis=0)
            for offset in range(3)
        ]
    )
    skip_part = jnp.sum(grad_z * keyed_value, axis=0)
    ids_stacked = jnp.concatenate([window_ids[2:], window_ids[1:-1], window_ids[:-2]])
    live_stacked = jnp.concatenate([present[2:], present[1:-1], present[:-2]])
    weighted = jnp.concatenate([short_conv[offset] * grad_value for offset in range(3)], axis=0)
    vocab_rows = jnp.arange(vocab_size // seq_count * lax.axis_size("seq"), dtype=jnp.int32)
    matches = ((vocab_rows[:, None] == ids_stacked[None, :]) & live_stacked[None, :]).astype(
        jnp.float32
    )
    grad_embed = (
        lax.psum_scatter(
            jnp.dot(matches, weighted, precision=highest, preferred_element_type=jnp.float32),
            "seq",
            scatter_dimension=0,
            tiled=True,
        )
        * inv_root
    )
    grad_act_two = lax.psum(act_two_part, "chan")
    first_part, second_part = filter_tail(grad_act_two, tail_acts, weight_second)
    grad_short, grad_skip, grad_third, grad_first, grad_second = lax.psum(
        (short_part, skip_part, third_part, first_part, second_part), "seq"
    )
    return (
        operator_out,
        grad_query,
        grad_key,
        grad_embed,
        grad_short * inv_root,
        grad_skip * inv_root,
        grad_first * inv_root,
        grad_second * inv_root,
        grad_third * inv_root,
    )


def solution(mesh):
    in_specs = (
        P("seq"),
        P(None, "chan"),
        P(None, "chan"),
        P("seq", "chan"),
        P("seq", "chan"),
        P("chan"),
        P(),
        P(),
        P(None, "chan"),
        P("chan"),
        P("seq", "chan"),
    )
    out_specs = (
        P("seq", "chan"),
        P("seq", "chan"),
        P("seq", "chan"),
        P("seq", "chan"),
        P(None, "chan"),
        P("chan"),
        P(),
        P(),
        P(None, "chan"),
    )
    return jax.shard_map(
        per_device, mesh=mesh, in_specs=in_specs, out_specs=out_specs, check_vma=False
    )
```

profile of v0, /device:TPU:1, one launch (start us, length us, event | category | flops | bytes accessed | tf_op | source)
XLA Modules:
  0.0 1267.4 jit_solution(2836227527595112904)
XLA Ops:
  13.2 7.8 collective-permute-start.6
  21.8 3.1 collective-permute-start
  33.0 3.7 collective-permute-start.16
  38.7 8.5 collective-permute-done.1
  48.2 9.7 collective-permute-done.16
  62.6 87.1 %collective-permute-done.2 = f32[2,2,256,256]{2,3,1,0:T(8,128)S(1)} collective-permute-done((f32[2,2,256,256]{2,3,1,0:T(8,128)S(1)}, f32[2,2,256,256]{2,3,1,0:T(8,128)S(1)}, u32[]{:S(2)}, u32[]{:S(2)}) %collective-permute-start.2) | collective-permute-done | bytes 1048608 | tf_op jit(solution)/shard_map/ppermute | solution.py:22
  151.5 20.7 %collective-permute-done.7 = f32[2,2,256,256]{2,3,1,0:T(8,128)S(1)} collective-permute-done((f32[2,2,256,256]{2,3,1,0:T(8,128)S(1)}, f32[2,2,256,256]{2,3,1,0:T(8,128)S(1)}, u32[]{:S(2)}, u32[]{:S(2)}) %collective-permute-start.7) | collective-permute-done | bytes 1048608 | tf_op jit(solution)/shard_map/ppermute | solution.py:22
  174.0 20.7 %collective-permute-done.17 = f32[2,2,256,256]{2,3,1,0:T(8,128)S(1)} collective-permute-done((f32[2,2,256,256]{2,3,1,0:T(8,128)S(1)}, f32[2,2,256,256]{2,3,1,0:T(8,128)S(1)}, u32[]{:S(2)}, u32[]{:S(2)}) %collective-permute-start.17) | collective-permute-done | bytes 1048608 | tf_op jit(solution)/shard_map/ppermute | solution.py:22
  196.8 23.6 %collective-permute-done.3 = f32[2,2,256,256]{2,3,1,0:T(8,128)S(1)} collective-permute-done((f32[2,2,256,256]{2,3,1,0:T(8,128)S(1)}, f32[2,2,256,256]{2,3,1,0:T(8,128)S(1)}, u32[]{:S(2)}, u32[]{:S(2)}) %collective-permute-start.3) | collective-permute-done | bytes 1048608 | tf_op jit(solution)/shard_map/ppermute | solution.py:22
  220.7 2.9 collective-permute-start.4
  223.6 19.3 %collective-permute-done.8 = f32[2,2,256,256]{2,3,1,0:T(8,128)S(1)} collective-permute-done((f32[2,2,256,256]{2,3,1,0:T(8,128)S(1)}, f32[2,2,256,256]{2,3,1,0:T(8,128)S(1)}, u32[]{:S(2)}, u32[]{:S(2)}) %collective-permute-start.8) | collective-permute-done | bytes 1048608 | tf_op jit(solution)/shard_map/ppermute | solution.py:22
  243.2 2.7 collective-permute-start.9
  246.1 19.2 %collective-permute-done.18 = f32[2,2,256,256]{2,3,1,0:T(8,128)S(1)} collective-permute-done((f32[2,2,256,256]{2,3,1,0:T(8,128)S(1)}, f32[2,2,256,256]{2,3,1,0:T(8,128)S(1)}, u32[]{:S(2)}, u32[]{:S(2)}) %collective-permute-start.18) | collective-permute-done | bytes 1048608 | tf_op jit(solution)/shard_map/ppermute | solution.py:22
  265.6 2.7 collective-permute-start.19
  271.2 20.6 %collective-permute-done.19 = f32[2,2,256,256]{2,3,1,0:T(8,128)S(1)} collective-permute-done((f32[2,2,256,256]{2,3,1,0:T(8,128)S(1)}, f32[2,2,256,256]{2,3,1,0:T(8,128)S(1)}, u32[]{:S(2)}, u32[]{:S(2)}) %collective-permute-start.19) | collective-permute-done | bytes 1048608 | tf_op jit(solution)/shard_map/ppermute | solution.py:22
  294.2 21.4 %collective-permute-done.5 = f32[2,2,256,256]{2,3,1,0:T(8,128)S(1)} collective-permute-done((f32[2,2,256,256]{2,3,1,0:T(8,128)S(1)}, f32[2,2,256,256]{2,3,1,0:T(8,128)S(1)}, u32[]{:S(2)}, u32[]{:S(2)}) %collective-permute-start.5) | collective-permute-done | bytes 1048608 | tf_op jit(solution)/shard_map/ppermute | solution.py:22
  315.9 22.2 %collective-permute-done.10 = f32[2,2,256,256]{2,3,1,0:T(8,128)S(1)} collective-permute-done((f32[2,2,256,256]{2,3,1,0:T(8,128)S(1)}, f32[2,2,256,256]{2,3,1,0:T(8,128)S(1)}, u32[]{:S(2)}, u32[]{:S(2)}) %collective-permute-start.10) | collective-permute-done | bytes 1048608 | tf_op jit(solution)/shard_map/ppermute | solution.py:22
  338.4 22.2 %collective-permute-done.20 = f32[2,2,256,256]{2,3,1,0:T(8,128)S(1)} collective-permute-done((f32[2,2,256,256]{2,3,1,0:T(8,128)S(1)}, f32[2,2,256,256]{2,3,1,0:T(8,128)S(1)}, u32[]{:S(2)}, u32[]{:S(2)}) %collective-permute-start.20) | collective-permute-done | bytes 1048608 | tf_op jit(solution)/shard_map/ppermute | solution.py:22
  376.6 21.5 %collective-permute-done.11 = f32[2,2,256,256]{2,3,1,0:T(8,128)S(1)} collective-permute-done((f32[2,2,256,256]{2,3,1,0:T(8,128)S(1)}, f32[2,2,256,256]{2,3,1,0:T(8,128)S(1)}, u32[]{:S(2)}, u32[]{:S(2)}) %collective-permute-start.11) | collective-permute-done | bytes 1048608 | tf_op jit(solution)/shard_map/ppermute | solution.py:22
  399.2 21.3 %collective-permute-done.21 = f32[2,2,256,256]{2,3,1,0:T(8,128)S(1)} collective-permute-done((f32[2,2,256,256]{2,3,1,0:T(8,128)S(1)}, f32[2,2,256,256]{2,3,1,0:T(8,128)S(1)}, u32[]{:S(2)}, u32[]{:S(2)}) %collective-permute-start.21) | collective-permute-done | bytes 1048608 | tf_op jit(solution)/shard_map/ppermute | solution.py:22
  421.7 21.3 %collective-permute-done.26 = f32[2,2,256,256]{2,3,1,0:T(8,128)S(1)} collective-permute-done((f32[2,2,256,256]{2,3,1,0:T(8,128)S(1)}, f32[2,2,256,256]{2,3,1,0:T(8,128)S(1)}, u32[]{:S(2)}, u32[]{:S(2)}) %collective-permute-start.26) | collective-permute-done | bytes 1048608 | tf_op jit(solution)/shard_map/ppermute | solution.py:22
  444.6 20.6 %collective-permute-done.12 = f32[2,2,256,256]{2,3,1,0:T(8,128)S(1)} collective-permute-done((f32[2,2,256,256]{2,3,1,0:T(8,128)S(1)}, f32[2,2,256,256]{2,3,1,0:T(8,128)S(1)}, u32[]{:S(2)}, u32[]{:S(2)}) %collective-permute-start.12) | collective-permute-done | bytes 1048608 | tf_op jit(solution)/shard_map/ppermute | solution.py:22
  465.5 22.1 %collective-permute-done.22 = f32[2,2,256,256]{2,3,1,0:T(8,128)S(1)} collective-permute-done((f32[2,2,256,256]{2,3,1,0:T(8,128)S(1)}, f32[2,2,256,256]{2,3,1,0:T(8,128)S(1)}, u32[]{:S(2)}, u32[]{:S(2)}) %collective-permute-start.22) | collective-permute-done | bytes 1048608 | tf_op jit(solution)/shard_map/ppermute | solution.py:22
  488.0 22.1 %collective-permute-done.27 = f32[2,2,256,256]{2,3,1,0:T(8,128)S(1)} collective-permute-done((f32[2,2,256,256]{2,3,1,0:T(8,128)S(1)}, f32[2,2,256,256]{2,3,1,0:T(8,128)S(1)}, u32[]{:S(2)}, u32[]{:S(2)}) %collective-permute-start.27) | collective-permute-done | bytes 1048608 | tf_op jit(solution)/shard_map/ppermute | solution.py:22
  514.0 40.3 %collective-permute-done.28 = f32[2,2,256,256]{2,3,1,0:T(8,128)S(1)} collective-permute-done((f32[2,2,256,256]{2,3,1,0:T(8,128)S(1)}, f32[2,2,256,256]{2,3,1,0:T(8,128)S(1)}, u32[]{:S(2)}, u32[]{:S(2)}) %collective-permute-start.28) | collective-permute-done | bytes 1048608 | tf_op jit(solution)/shard_map/ppermute | solution.py:22
  557.9 101.4 %collective-permute-done.24 = f32[2,2,256,256]{2,3,1,0:T(8,128)S(1)} collective-permute-done((f32[2,2,256,256]{2,3,1,0:T(8,128)S(1)}, f32[2,2,256,256]{2,3,1,0:T(8,128)S(1)}, u32[]{:S(2)}, u32[]{:S(2)}) %collective-permute-start.24) | collective-permute-done | bytes 1048608 | tf_op jit(solution)/shard_map/ppermute | solution.py:22
  660.9 44.2 %collective-permute-done.29 = f32[2,2,256,256]{2,3,1,0:T(8,128)S(1)} collective-permute-done((f32[2,2,256,256]{2,3,1,0:T(8,128)S(1)}, f32[2,2,256,256]{2,3,1,0:T(8,128)S(1)}, u32[]{:S(2)}, u32[]{:S(2)}) %collective-permute-start.29) | collective-permute-done | bytes 1048608 | tf_op jit(solution)/shard_map/ppermute | solution.py:22
  707.6 79.8 %collective-permute-done.30 = f32[2,2,256,256]{2,3,1,0:T(8,128)S(1)} collective-permute-done((f32[2,2,256,256]{2,3,1,0:T(8,128)S(1)}, f32[2,2,256,256]{2,3,1,0:T(8,128)S(1)}, u32[]{:S(2)}, u32[]{:S(2)}) %collective-permute-start.30) | collective-permute-done | bytes 1048608 | tf_op jit(solution)/shard_map/ppermute | solution.py:22
  793.8 106.9 %all-reduce.4.cloned.1.call-done = f32[256,64]{0,1:T(8,128)} async-done(((f32[256,64]{0,1:T(8,128)}), f32[256,64]{0,1:T(8,128)}) %all-reduce.4.cloned.1.call-update) | async-done | bytes 65552 | tf_op jit(solution)/shard_map/psum | solution.py:317
  903.6 115.7 %all-reduce = (f32[3,256]{1,0:T(4,128)S(1)}, f32[256]{0:T(256)S(1)}, f32[33,64]{1,0:T(8,128)S(1)}, f32[64,64]{1,0:T(8,128)S(1)}) all-reduce(f32[3,256]{1,0:T(4,128)S(1)} %pad_maximum_fusion.6, f32[256]{0:T(256)S(1)} %copy-done.20, f32[33,64]{1,0:T(8,128)S(1)} %fusion.71, ...), channel_id=1, replica_groups=mesh['seq'=32,'chan'=8] {'seq'}, use_global_device_ids=true, to_apply=%region_6.7 | all-reduce | flops 7232 | bytes 57856 | tf_op jit(solution)/shard_map/psum | solution.py:319
  1021.6 20.8 %all-reduce.6.cloned.1.call-done = f32[64,256]{1,0:T(8,128)} async-done(((f32[64,256]{1,0:T(8,128)}), f32[64,256]{1,0:T(8,128)}) %all-reduce.6.cloned.1.call-update) | async-done | bytes 65552 | tf_op jit(solution)/shard_map/psum | solution.py:319
  1044.0 215.4 %reduce-scatter.2.cloned.1.call-done = f32[8,256]{1,0:T(8,128)} async-done(((f32[256,256]{1,0:T(8,128)}), f32[8,256]{1,0:T(8,128)}) %reduce-scatter.2.cloned.1.call-update) | async-done | bytes 8208 | tf_op jit(solution)/shard_map/reduce_scatter | solution.py:309
  (255 shorter events, 78.8 us)
Async XLA Ops:
  7.2 893.5 %all-reduce.4.cloned.1.call-start = ((), (), s32[]{:S(2)}) async-start(), calls=%async_computation.2 | async-start | bytes 131072 | tf_op jit(solution)/shard_map/psum | solution.py:317
  13.2 25.3 %collective-permute-start.6 = (f32[256,256]{1,0:T(8,128)S(1)}, f32[256,256]{1,0:T(8,128)S(1)}, u32[]{:S(2)}, u32[]{:S(2)}) collective-permute-start(f32[256,256]{1,0:T(8,128)S(1)} %convolution_multiply_fusion), channel_id=1, source_target_pairs={{0,128},{128,0},{8,136},{136,8},{16,144},{144,16},{24,152},{152,24... | collective-permute-start | bytes 786440 | tf_op jit(solution)/shard_map/ppermute | solution.py:22
  33.0 24.9 %collective-permute-start.16 = (f32[256,256]{1,0:T(8,128)S(1)}, f32[256,256]{1,0:T(8,128)}, u32[]{:S(2)}, u32[]{:S(2)}) collective-permute-start(f32[256,256]{1,0:T(8,128)S(1)} %get-tuple-element.163), channel_id=1, source_target_pairs={{0,128},{128,0},{8,136},{136,8},{16,144},{144,16},{24,152},{152,24... | collective-permute-start | bytes 786440 | tf_op jit(solution)/shard_map/ppermute | solution.py:22
  59.5 90.2 %collective-permute-start.2 = (f32[2,2,256,256]{2,3,1,0:T(8,128)S(1)}, f32[2,2,256,256]{2,3,1,0:T(8,128)S(1)}, u32[]{:S(2)}, u32[]{:S(2)}) collective-permute-start(f32[2,2,256,256]{2,3,1,0:T(8,128)S(1)} %get-tuple-element.181), channel_id=1, source_target_pairs={{0,64},{64,0},{8,72},{72,8},{16,80},{80,16},{24,88},{88,24},{32,96... | collective-permute-start | bytes 3145736 | tf_op jit(solution)/shard_map/ppermute | solution.py:22
  59.7 112.5 %collective-permute-start.7 = (f32[2,2,256,256]{2,3,1,0:T(8,128)S(1)}, f32[2,2,256,256]{2,3,1,0:T(8,128)S(1)}, u32[]{:S(2)}, u32[]{:S(2)}) collective-permute-start(f32[2,2,256,256]{2,3,1,0:T(8,128)S(1)} %get-tuple-element.180), channel_id=1, source_target_pairs={{0,64},{64,0},{8,72},{72,8},{16,80},{80,16},{24,88},{88,24},{32,96... | collective-permute-start | bytes 3145736 | tf_op jit(solution)/shard_map/ppermute | solution.py:22
  62.2 132.5 %collective-permute-start.17 = (f32[2,2,256,256]{2,3,1,0:T(8,128)S(1)}, f32[2,2,256,256]{2,3,1,0:T(8,128)S(1)}, u32[]{:S(2)}, u32[]{:S(2)}) collective-permute-start(f32[2,2,256,256]{2,3,1,0:T(8,128)S(1)} %get-tuple-element.179), channel_id=1, source_target_pairs={{0,64},{64,0},{8,72},{72,8},{16,80},{80,16},{24,88},{88,24},{32,96... | collective-permute-start | bytes 3145736 | tf_op jit(solution)/shard_map/ppermute | solution.py:22
  150.0 70.4 %collective-permute-start.3 = (f32[2,2,256,256]{2,3,1,0:T(8,128)S(1)}, f32[2,2,256,256]{2,3,1,0:T(8,128)S(1)}, u32[]{:S(2)}, u32[]{:S(2)}) collective-permute-start(f32[2,2,256,256]{2,3,1,0:T(8,128)S(1)} %maximum_add_fusion), channel_id=1, source_target_pairs={{0,32},{32,0},{8,40},{40,8},{16,48},{48,16},{24,56},{56,24},{64,96... | collective-permute-start | bytes 3145736 | tf_op jit(solution)/shard_map/ppermute | solution.py:22
  172.5 70.4 %collective-permute-start.8 = (f32[2,2,256,256]{2,3,1,0:T(8,128)S(1)}, f32[2,2,256,256]{2,3,1,0:T(8,128)S(1)}, u32[]{:S(2)}, u32[]{:S(2)}) collective-permute-start(f32[2,2,256,256]{2,3,1,0:T(8,128)S(1)} %maximum_add_fusion.4), channel_id=1, source_target_pairs={{0,32},{32,0},{8,40},{40,8},{16,48},{48,16},{24,56},{56,24},{64,96... | collective-permute-start | bytes 3145736 | tf_op jit(solution)/shard_map/ppermute | solution.py:22
  195.0 70.4 %collective-permute-start.18 = (f32[2,2,256,256]{2,3,1,0:T(8,128)S(1)}, f32[2,2,256,256]{2,3,1,0:T(8,128)S(1)}, u32[]{:S(2)}, u32[]{:S(2)}) collective-permute-start(f32[2,2,256,256]{2,3,1,0:T(8,128)S(1)} %maximum_add_fusion.13), channel_id=1, source_target_pairs={{0,32},{32,0},{8,40},{40,8},{16,48},{48,16},{24,56},{56,24},{64,96... | collective-permute-start | bytes 3145736 | tf_op jit(solution)/shard_map/ppermute | solution.py:22
  220.7 47.8 %collective-permute-start.4 = (f32[2,2,256,256]{2,3,1,0:T(8,128)S(1)}, f32[2,2,256,256]{2,3,1,0:T(8,128)S(1)}, u32[]{:S(2)}, u32[]{:S(2)}) collective-permute-start(f32[2,2,256,256]{2,3,1,0:T(8,128)S(1)} %maximum_add_fusion.1), channel_id=1, source_target_pairs={{0,16},{16,0},{8,24},{24,8},{32,48},{48,32},{40,56},{56,40},{64,80... | collective-permute-start | bytes 3145736 | tf_op jit(solution)/shard_map/ppermute | solution.py:22
  243.2 27.6 %collective-permute-start.9 = (f32[2,2,256,256]{2,3,1,0:T(8,128)S(1)}, f32[2,2,256,256]{2,3,1,0:T(8,128)S(1)}, u32[]{:S(2)}, u32[]{:S(2)}) collective-permute-start(f32[2,2,256,256]{2,3,1,0:T(8,128)S(1)} %maximum_add_fusion.5), channel_id=1, source_target_pairs={{0,16},{16,0},{8,24},{24,8},{32,48},{48,32},{40,56},{56,40},{64,80... | collective-permute-start | bytes 3145736 | tf_op jit(solution)/shard_map/ppermute | solution.py:22
  265.6 26.1 %collective-permute-start.19 = (f32[2,2,256,256]{2,3,1,0:T(8,128)S(1)}, f32[2,2,256,256]{2,3,1,0:T(8,128)S(1)}, u32[]{:S(2)}, u32[]{:S(2)}) collective-permute-start(f32[2,2,256,256]{2,3,1,0:T(8,128)S(1)} %maximum_add_fusion.14), channel_id=1, source_target_pairs={{0,16},{16,0},{8,24},{24,8},{32,48},{48,32},{40,56},{56,40},{64,80... | collective-permute-start | bytes 3145736 | tf_op jit(solution)/shard_map/ppermute | solution.py:22
  268.8 46.9 %collective-permute-start.5 = (f32[2,2,256,256]{2,3,1,0:T(8,128)S(1)}, f32[2,2,256,256]{2,3,1,0:T(8,128)S(1)}, u32[]{:S(2)}, u32[]{:S(2)}) collective-permute-start(f32[2,2,256,256]{2,3,1,0:T(8,128)S(1)} %maximum_add_fusion.2), channel_id=1, source_target_pairs={{0,8},{8,0},{16,24},{24,16},{32,40},{40,32},{48,56},{56,48},{64,72... | collective-permute-start | bytes 3145736 | tf_op jit(solution)/shard_map/ppermute | solution.py:22
  271.0 67.1 %collective-permute-start.10 = (f32[2,2,256,256]{2,3,1,0:T(8,128)S(1)}, f32[2,2,256,256]{2,3,1,0:T(8,128)S(1)}, u32[]{:S(2)}, u32[]{:S(2)}) collective-permute-start(f32[2,2,256,256]{2,3,1,0:T(8,128)S(1)} %maximum_add_fusion.6), channel_id=1, source_target_pairs={{0,8},{8,0},{16,24},{24,16},{32,40},{40,32},{48,56},{56,48},{64,72... | collective-permute-start | bytes 3145736 | tf_op jit(solution)/shard_map/ppermute | solution.py:22
  292.1 68.6 %collective-permute-start.20 = (f32[2,2,256,256]{2,3,1,0:T(8,128)S(1)}, f32[2,2,256,256]{2,3,1,0:T(8,128)S(1)}, u32[]{:S(2)}, u32[]{:S(2)}) collective-permute-start(f32[2,2,256,256]{2,3,1,0:T(8,128)S(1)} %maximum_add_fusion.15), channel_id=1, source_target_pairs={{0,8},{8,0},{16,24},{24,16},{32,40},{40,32},{48,56},{56,48},{64,72... | collective-permute-start | bytes 3145736 | tf_op jit(solution)/shard_map/ppermute | solution.py:22
  374.5 23.6 %collective-permute-start.11 = (f32[2,2,256,256]{2,3,1,0:T(8,128)S(1)}, f32[2,2,256,256]{2,3,1,0:T(8,128)S(1)}, u32[]{:S(2)}, u32[]{:S(2)}) collective-permute-start(f32[2,2,256,256]{2,3,1,0:T(8,128)S(1)} %pad_maximum_fusion), channel_id=1, source_target_pairs={{0,8},{8,0},{16,24},{24,16},{32,40},{40,32},{48,56},{56,48},{64,72... | collective-permute-start | bytes 3145736 | tf_op jit(solution)/shard_map/ppermute | solution.py:22
  374.7 45.9 %collective-permute-start.21 = (f32[2,2,256,256]{2,3,1,0:T(8,128)S(1)}, f32[2,2,256,256]{2,3,1,0:T(8,128)S(1)}, u32[]{:S(2)}, u32[]{:S(2)}) collective-permute-start(f32[2,2,256,256]{2,3,1,0:T(8,128)S(1)} %pad_maximum_fusion.1), channel_id=1, source_target_pairs={{0,8},{8,0},{16,24},{24,16},{32,40},{40,32},{48,56},{56,48},{64,72... | collective-permute-start | bytes 3145736 | tf_op jit(solution)/shard_map/ppermute | solution.py:22
  376.3 66.7 %collective-permute-start.26 = (f32[2,2,256,256]{2,3,1,0:T(8,128)S(1)}, f32[2,2,256,256]{2,3,1,0:T(8,128)S(1)}, u32[]{:S(2)}, u32[]{:S(2)}) collective-permute-start(f32[2,2,256,256]{2,3,1,0:T(8,128)S(1)} %pad_maximum_fusion.2), channel_id=1, source_target_pairs={{0,8},{8,0},{16,24},{24,16},{32,40},{40,32},{48,56},{56,48},{64,72... | collective-permute-start | bytes 3145736 | tf_op jit(solution)/shard_map/ppermute | solution.py:22
  398.3 66.8 %collective-permute-start.12 = (f32[2,2,256,256]{2,3,1,0:T(8,128)S(1)}, f32[2,2,256,256]{2,3,1,0:T(8,128)S(1)}, u32[]{:S(2)}, u32[]{:S(2)}) collective-permute-start(f32[2,2,256,256]{2,3,1,0:T(8,128)S(1)} %maximum_add_fusion.8), channel_id=1, source_target_pairs={{0,16},{16,0},{8,24},{24,8},{32,48},{48,32},{40,56},{56,40},{64,80... | collective-permute-start | bytes 3145736 | tf_op jit(solution)/shard_map/ppermute | solution.py:22
  420.8 66.8 %collective-permute-start.22 = (f32[2,2,256,256]{2,3,1,0:T(8,128)S(1)}, f32[2,2,256,256]{2,3,1,0:T(8,128)S(1)}, u32[]{:S(2)}, u32[]{:S(2)}) collective-permute-start(f32[2,2,256,256]{2,3,1,0:T(8,128)S(1)} %maximum_add_fusion.17), channel_id=1, source_target_pairs={{0,16},{16,0},{8,24},{24,8},{32,48},{48,32},{40,56},{56,40},{64,80... | collective-permute-start | bytes 3145736 | tf_op jit(solution)/shard_map/ppermute | solution.py:22
  443.3 66.8 %collective-permute-start.27 = (f32[2,2,256,256]{2,3,1,0:T(8,128)S(1)}, f32[2,2,256,256]{2,3,1,0:T(8,128)S(1)}, u32[]{:S(2)}, u32[]{:S(2)}) collective-permute-start(f32[2,2,256,256]{2,3,1,0:T(8,128)S(1)} %maximum_add_fusion.22), channel_id=1, source_target_pairs={{0,16},{16,0},{8,24},{24,8},{32,48},{48,32},{40,56},{56,40},{64,80... | collective-permute-start | bytes 3145736 | tf_op jit(solution)/shard_map/ppermute | solution.py:22
  465.4 45.4 %collective-permute-start.13 = (f32[2,2,256,256]{2,3,1,0:T(8,128)S(1)}, f32[2,2,256,256]{2,3,1,0:T(8,128)S(1)}, u32[]{:S(2)}, u32[]{:S(2)}) collective-permute-start(f32[2,2,256,256]{2,3,1,0:T(8,128)S(1)} %maximum_add_fusion.9), channel_id=1, source_target_pairs={{0,32},{32,0},{8,40},{40,8},{16,48},{48,16},{24,56},{56,24},{64,96... | collective-permute-start | bytes 3145736 | tf_op jit(solution)/shard_map/ppermute | solution.py:22
  487.9 24.7 %collective-permute-start.23 = (f32[2,2,256,256]{2,3,1,0:T(8,128)S(1)}, f32[2,2,256,256]{2,3,1,0:T(8,128)S(1)}, u32[]{:S(2)}, u32[]{:S(2)}) collective-permute-start(f32[2,2,256,256]{2,3,1,0:T(8,128)S(1)} %maximum_add_fusion.18), channel_id=1, source_target_pairs={{0,32},{32,0},{8,40},{40,8},{16,48},{48,16},{24,56},{56,24},{64,96... | collective-permute-start | bytes 3145736 | tf_op jit(solution)/shard_map/ppermute | solution.py:22
  510.4 43.9 %collective-permute-start.28 = (f32[2,2,256,256]{2,3,1,0:T(8,128)S(1)}, f32[2,2,256,256]{2,3,1,0:T(8,128)S(1)}, u32[]{:S(2)}, u32[]{:S(2)}) collective-permute-start(f32[2,2,256,256]{2,3,1,0:T(8,128)S(1)} %maximum_add_fusion.23), channel_id=1, source_target_pairs={{0,32},{32,0},{8,40},{40,8},{16,48},{48,16},{24,56},{56,24},{64,96... | collective-permute-start | bytes 3145736 | tf_op jit(solution)/shard_map/ppermute | solution.py:22
  511.1 44.1 %collective-permute-start.14 = (f32[2,2,256,256]{2,3,1,0:T(8,128)S(1)}, f32[2,2,256,256]{2,3,1,0:T(8,128)S(1)}, u32[]{:S(2)}, u32[]{:S(2)}) collective-permute-start(f32[2,2,256,256]{2,3,1,0:T(8,128)S(1)} %maximum_add_fusion.10), channel_id=1, source_target_pairs={{0,64},{64,0},{8,72},{72,8},{16,80},{80,16},{24,88},{88,24},{32,96... | collective-permute-start | bytes 3145736 | tf_op jit(solution)/shard_map/ppermute | solution.py:22
  512.8 146.5 %collective-permute-start.24 = (f32[2,2,256,256]{2,3,1,0:T(8,128)S(1)}, f32[2,2,256,256]{2,3,1,0:T(8,128)S(1)}, u32[]{:S(2)}, u32[]{:S(2)}) collective-permute-start(f32[2,2,256,256]{2,3,1,0:T(8,128)S(1)} %maximum_add_fusion.19), channel_id=1, source_target_pairs={{0,64},{64,0},{8,72},{72,8},{16,80},{80,16},{24,88},{88,24},{32,96... | collective-permute-start | bytes 3145736 | tf_op jit(solution)/shard_map/ppermute | solution.py:22
  554.6 150.5 %collective-permute-start.29 = (f32[2,2,256,256]{2,3,1,0:T(8,128)S(1)}, f32[2,2,256,256]{2,3,1,0:T(8,128)S(1)}, u32[]{:S(2)}, u32[]{:S(2)}) collective-permute-start(f32[2,2,256,256]{2,3,1,0:T(8,128)S(1)} %maximum_add_fusion.24), channel_id=1, source_target_pairs={{0,64},{64,0},{8,72},{72,8},{16,80},{80,16},{24,88},{88,24},{32,96... | collective-permute-start | bytes 3145736 | tf_op jit(solution)/shard_map/ppermute | solution.py:22
  555.6 151.5 %collective-permute-start.15 = (f32[2,2,256,256]{2,3,1,0:T(8,128)S(1)}, f32[2,2,256,256]{2,3,1,0:T(8,128)S(1)}, u32[]{:S(2)}, u32[]{:S(2)}) collective-permute-start(f32[2,2,256,256]{2,3,1,0:T(8,128)S(1)} %maximum_add_fusion.11), channel_id=1, source_target_pairs={{0,128},{128,0},{8,136},{136,8},{16,144},{144,16},{24,152},{152,24... | collective-permute-start | bytes 3145736 | tf_op jit(solution)/shard_map/ppermute | solution.py:22
  659.6 47.8 %collective-permute-start.25 = (f32[2,2,256,256]{2,3,1,0:T(8,128)S(1)}, f32[2,2,256,256]{2,3,1,0:T(8,128)S(1)}, u32[]{:S(2)}, u32[]{:S(2)}) collective-permute-start(f32[2,2,256,256]{2,3,1,0:T(8,128)S(1)} %maximum_add_fusion.20), channel_id=1, source_target_pairs={{0,128},{128,0},{8,136},{136,8},{16,144},{144,16},{24,152},{152,24... | collective-permute-start | bytes 3145736 | tf_op jit(solution)/shard_map/ppermute | solution.py:22
  705.3 82.1 %collective-permute-start.30 = (f32[2,2,256,256]{2,3,1,0:T(8,128)S(1)}, f32[2,2,256,256]{2,3,1,0:T(8,128)S(1)}, u32[]{:S(2)}, u32[]{:S(2)}) collective-permute-start(f32[2,2,256,256]{2,3,1,0:T(8,128)S(1)} %maximum_add_fusion.25), channel_id=1, source_target_pairs={{0,128},{128,0},{8,136},{136,8},{16,144},{144,16},{24,152},{152,24... | collective-permute-start | bytes 3145736 | tf_op jit(solution)/shard_map/ppermute | solution.py:22
  790.2 252.3 %all-reduce.6.cloned.1.call-start = ((), (), s32[]{:S(2)}) async-start(), calls=%async_computation.3 | async-start | bytes 131072 | tf_op jit(solution)/shard_map/psum | solution.py:319
  792.4 467.0 %reduce-scatter.2.cloned.1.call-start = ((), (), s32[]{:S(2)}) async-start(), calls=%async_computation.1 | async-start | bytes 270336 | tf_op jit(solution)/shard_map/reduce_scatter | solution.py:309
  (36 other events, 1412.9 us)
Sparse Core Ops, SparseCore 0:
  790.3 110.3 all-reduce.3
  904.1 138.2 all-reduce.5
  1046.3 213.0 reduce-scatter.1
where the time goes:
time: 1280 us; the launch traced here: 1270 us
  waiting for transfers between devices  1030 us (80%)
  blocking collectives  116 us (9%)
  starting transfers between devices  48.3 us (4%)
  other arithmetic  25 us (2%)
  matrix products  22.3 us (2%)
  between operations  16.8 us (1%)
    ppermute x30, waiting for transfers between devices, from_partner(): return lax.ppermute(block, axis, route)  690 us
    reduce_scatter x1, waiting for transfers between devices, per_device(): lax.psum_scatter(jnp.dot(matches, weighted, precision=highest, preferred_...  215 us
    psum x1, blocking collectives, per_device(): lax.psum((short_part, skip_part, third_part, first_part, second_part), 's...  116 us
    psum x1, waiting for transfers between devices, per_device(): grad_act_two = lax.psum(act_two_part, 'chan')  107 us
    ppermute x30, starting transfers between devices, from_partner(): return lax.ppermute(block, axis, route)  45.1 us
  transfers between devices with their start and end apart: 34, of which 25 were waited for; matrix products, arithmetic and copies ran while one was open for 2% of the time, Pallas kernels for 0%

commit v1 on v0

v1 whole, which is shorter than its diff:
```python
import math

import jax
import jax.numpy as jnp
import numpy as np
from jax import lax
from jax.sharding import PartitionSpec as P

BANDS = 16

high = lax.Precision.HIGH
highest = lax.Precision.HIGHEST
two_pi = 2.0 * math.pi


def transform_tables(parts, rows, lanes):
    length = parts * rows
    freq = 4 * np.arange(parts, dtype=np.int64) + 1
    phase = freq[:, None] * np.arange(parts, dtype=np.int64)[None, :] % (4 * parts)
    angle = two_pi * phase / (4 * parts)
    stage = np.concatenate([np.cos(angle), -np.sin(angle)], axis=0)
    first = np.kron(stage, np.eye(lanes))
    turn = freq[:, None] * np.arange(rows, dtype=np.int64)[None, :] % (4 * length)
    turn = two_pi * turn / (4 * length)
    inner = np.arange(rows, dtype=np.int64)
    inner = two_pi * (inner[:, None] * inner[None, :] % rows) / rows
    single = lambda table: np.asarray(table, np.float32)
    return (
        single(first),
        single(np.cos(turn)),
        single(np.sin(turn)),
        single(np.concatenate([np.cos(inner), np.sin(inner)], axis=1)),
    )


def feature_table(length):
    positions = np.arange(length, dtype=np.int64)
    frequency = 2 ** np.arange(BANDS, dtype=np.int64) + 1
    phases = frequency[:, None] * positions[None, :] % length
    angles = two_pi * phases / length
    table = np.concatenate([positions[None, :] / length, np.cos(angles), np.sin(angles)], axis=0)
    return np.asarray(table, np.float32)


def dot3(left, right):
    return jnp.dot(left, right, precision=high, preferred_element_type=jnp.float32)


def shift_back(block, lanes, steps):
    before = jnp.concatenate([jnp.zeros_like(block[:lanes]), block[:-lanes]], axis=0)
    return jnp.concatenate([before[:, -steps:], block[:, :-steps]], axis=1)


def shift_ahead(block, lanes, steps):
    after = jnp.concatenate([block[lanes:], jnp.zeros_like(block[:lanes])], axis=0)
    return jnp.concatenate([block[:, steps:], after[:, :steps]], axis=1)


def per_device(
    tokens,
    embed_table,
    short_conv,
    query_branch,
    key_branch,
    decay_rate,
    weight_first,
    weight_second,
    weight_third,
    skip_gain,
    cotangent,
):
    parts = lax.axis_size("seq")
    groups = lax.axis_size("chan")
    seq_index = lax.axis_index("seq")
    rows, width = query_branch.shape
    lanes = width // parts
    length = rows * parts
    inv_root = 1.0 / math.sqrt(length)
    vocab_size = embed_table.shape[0]
    hidden = weight_first.shape[1]
    own = seq_index * lanes

    query_rows = query_branch.astype(jnp.float32)
    key_rows = key_branch.astype(jnp.float32)
    grad_out = cotangent.astype(jnp.float32)
    key_cols = key_rows.T.reshape(parts, lanes, rows)
    grad_cols = (grad_out * query_rows).T.reshape(parts, lanes, rows)
    token_cols = jnp.broadcast_to(tokens.astype(jnp.float32)[None, None, :], (parts, 1, rows))
    packed = jnp.concatenate([key_cols, grad_cols, token_cols], axis=1)
    packed = lax.all_to_all(packed, "seq", 0, 0, tiled=True)
    key_all = packed[:, :lanes].reshape(parts * lanes, rows)
    grad_z = packed[:, lanes : 2 * lanes].reshape(parts * lanes, rows)
    token_all = packed[:, 2 * lanes].astype(jnp.int32)

    embed_own = lax.dynamic_slice_in_dim(embed_table, own, lanes, axis=1)
    short_own = lax.dynamic_slice_in_dim(short_conv, own, lanes, axis=1)
    decay_own = lax.dynamic_slice_in_dim(decay_rate, own, lanes, axis=0)
    skip_own = lax.dynamic_slice_in_dim(skip_gain, own, lanes, axis=0)
    third_own = lax.dynamic_slice_in_dim(weight_third, own, lanes, axis=1)
    by_row = lambda values: jnp.tile(values, parts)[:, None]

    vocab_ids = jnp.arange(vocab_size, dtype=jnp.int32)
    match = token_all[None] == vocab_ids[:, None, None]
    embedded = jnp.einsum(
        "wc,wsp->scp", embed_own, match.astype(jnp.bfloat16), preferred_element_type=jnp.float32
    ).reshape(parts * lanes, rows)
    lagged = [embedded, shift_back(embedded, lanes, 1), shift_back(embedded, lanes, 2)]
    value = sum(by_row(short_own[lag]) * lagged[lag] for lag in range(3))
    keyed = key_all * value

    features = jnp.asarray(feature_table(length))
    pre_one = dot3(weight_first.T, features)
    act_one = jnp.sin(pre_one)
    pre_two = dot3(weight_second.T, act_one)
    act_two = jnp.sin(pre_two)
    shaped = dot3(third_own.T, act_two)
    scaling = jnp.sqrt(jnp.expm1(-2.0 * decay_own) / jnp.expm1(-2.0 * length * decay_own))
    positions = jnp.arange(length, dtype=jnp.int32).astype(jnp.float32)
    window = scaling[:, None] * jnp.exp(-decay_own[:, None] * positions[None, :])
    filter_flat = shaped * window
    filter_rows = (
        filter_flat.reshape(lanes, parts, rows).transpose(1, 0, 2).reshape(parts * lanes, rows)
    )

    first, turn_cos, turn_sin, inner = (
        jnp.asarray(table) for table in transform_tables(parts, rows, lanes)
    )
    half = parts * lanes
    turn_cos = jnp.repeat(turn_cos, lanes, axis=0)
    turn_sin = jnp.repeat(turn_sin, lanes, axis=0)

    def forward(block):
        stage = dot3(first, block)
        real, imag = stage[:half], stage[half:]
        turned = jnp.concatenate(
            [real * turn_cos + imag * turn_sin, imag * turn_cos - real * turn_sin], axis=0
        )
        both = dot3(turned, inner)
        return (
            both[:half, :rows] + both[half:, rows:],
            both[half:, :rows] - both[:half, rows:],
        )

    def inverse(spectrum):
        both = dot3(jnp.concatenate(spectrum, axis=0), inner)
        real = both[:half, :rows] - both[half:, rows:]
        imag = both[half:, :rows] + both[:half, rows:]
        turned = jnp.concatenate(
            [real * turn_cos - imag * turn_sin, imag * turn_cos + real * turn_sin], axis=0
        )
        return dot3(first.T, turned) * (1.0 / length)

    keyed_spec, filter_spec, grad_spec = forward(keyed), forward(filter_rows), forward(grad_z)

    def times(left, right):
        return (left[0] * right[0] - left[1] * right[1], left[0] * right[1] + left[1] * right[0])

    def against(left, right):
        return (left[0] * right[0] + left[1] * right[1], left[0] * right[1] - left[1] * right[0])

    convolved = inverse(times(keyed_spec, filter_spec))
    back_keyed = inverse(against(filter_spec, grad_spec))
    grad_filter = inverse(against(keyed_spec, grad_spec))

    skip_rows = by_row(skip_own)
    inner_sum = convolved + skip_rows * keyed
    grad_keyed = back_keyed + skip_rows * grad_z
    grad_value = grad_keyed * key_all

    def per_channel(block):
        return jnp.sum(block.reshape(parts, lanes, rows), axis=(0, 2))

    short_part = jnp.stack([per_channel(grad_value * lagged[lag]) for lag in range(3)])
    skip_part = per_channel(grad_z * keyed)
    scattered = (
        by_row(short_own[0]) * grad_value
        + by_row(short_own[1]) * shift_ahead(grad_value, lanes, 1)
        + by_row(short_own[2]) * shift_ahead(grad_value, lanes, 2)
    )
    upper = lax.reduce_precision(scattered, 8, 7)
    lower = (scattered - upper).astype(jnp.bfloat16)
    upper = upper.astype(jnp.bfloat16)
    both = jnp.concatenate(
        [upper.reshape(parts, lanes, rows), lower.reshape(parts, lanes, rows)], axis=1
    )
    embed_part = jnp.einsum(
        "wsp,scp->wc", match.astype(jnp.bfloat16), both, preferred_element_type=jnp.float32
    )
    embed_part = embed_part[:, :lanes] + embed_part[:, lanes:]

    grad_flat = grad_filter.reshape(parts, lanes, rows).transpose(1, 0, 2).reshape(lanes, length)
    grad_shaped = grad_flat * window
    dot_last = lambda left, right: lax.dot_general(
        left, right, (((1,), (1,)), ((), ())), precision=high, preferred_element_type=jnp.float32
    )
    third_part = dot_last(act_two, grad_shaped)
    grad_pre_two = dot3(third_own, grad_shaped) * jnp.cos(pre_two)
    second_part = dot_last(act_one, grad_pre_two)
    grad_pre_one = dot3(weight_second, grad_pre_two) * jnp.cos(pre_one)
    first_part = dot_last(features, grad_pre_one)

    summed = jnp.concatenate([second_part.reshape(-1), first_part.reshape(-1)])
    share = -(-summed.shape[0] // parts)
    summed = jnp.pad(summed, (0, share * parts - summed.shape[0])).reshape(parts, share)
    spread = lambda values: jnp.broadcast_to(values.reshape(1, -1), (parts, values.size))
    small = jnp.concatenate(
        [
            embed_part.reshape(parts, -1),
            spread(short_part),
            spread(skip_part),
            spread(third_part),
            summed,
        ],
        axis=1,
    )
    small_rows = -(-small.shape[1] // rows)
    small = jnp.pad(small, ((0, 0), (0, small_rows * rows - small.shape[1])))
    packed = jnp.concatenate(
        [
            inner_sum.reshape(parts, lanes, rows),
            grad_keyed.reshape(parts, lanes, rows),
            small.reshape(parts, small_rows, rows),
        ],
        axis=1,
    )
    packed = lax.all_to_all(packed, "seq", 0, 0, tiled=True)
    inner_own = packed[:, :lanes].reshape(width, rows).T
    grad_own = packed[:, lanes : 2 * lanes].reshape(width, rows).T
    small = packed[:, 2 * lanes :].reshape(parts, -1)

    own_vocab = vocab_size // parts
    cut = np.cumsum([own_vocab * lanes, 3 * lanes, lanes, hidden * lanes, share])
    grad_embed = small[:, : cut[0]].reshape(parts, own_vocab, lanes).transpose(1, 0, 2)
    grad_embed = grad_embed.reshape(own_vocab, width) * inv_root
    grad_short = small[:, cut[0] : cut[1]].reshape(parts, 3, lanes).transpose(1, 0, 2)
    grad_short = grad_short.reshape(3, width) * inv_root
    grad_skip = small[:, cut[1] : cut[2]].reshape(width) * inv_root
    grad_third = small[:, cut[2] : cut[3]].reshape(parts, hidden, lanes).transpose(1, 0, 2)
    grad_third = grad_third.reshape(hidden, width) * inv_root

    partial = jnp.sum(small[:, cut[3] : cut[4]], axis=0)
    padded = -(-share // 128) * 128
    partial = jnp.pad(partial, (0, padded - share)).reshape(1, padded // 128, 128)
    partial = jnp.broadcast_to(partial, (parts * groups,) + partial.shape[1:])
    partial = lax.all_to_all(partial, ("seq", "chan"), 0, 0, tiled=True)
    total = jnp.sum(partial.reshape(parts, groups, padded), axis=1)[:, :share].reshape(-1)
    count = hidden * hidden
    grad_second = total[:count].reshape(hidden, hidden) * inv_root
    grad_first = total[count : count + first_part.size].reshape(first_part.shape) * inv_root

    lookup_ids = token_all.reshape(-1)
    start = seq_index * rows
    padded_ids = jnp.concatenate([jnp.full((2,), -1, jnp.int32), lookup_ids])
    window_ids = lax.dynamic_slice_in_dim(padded_ids, start, rows + 2)
    lookup = (window_ids[:, None] == vocab_ids[None, :]).astype(jnp.bfloat16)
    embedded = jnp.dot(lookup, embed_table, preferred_element_type=jnp.float32)
    value_rows = (
        short_conv[0] * embedded[2:]
        + short_conv[1] * embedded[1:-1]
        + short_conv[2] * embedded[:-2]
    )
    operator_out = (query_rows * inner_own).astype(jnp.bfloat16)
    grad_query = (grad_out * inner_own).astype(jnp.bfloat16)
    grad_key = (grad_own * value_rows).astype(jnp.bfloat16)
    return (
        operator_out,
        grad_query,
        grad_key,
        grad_embed,
        grad_short,
        grad_skip,
        grad_first,
        grad_second,
        grad_third,
    )


def solution(mesh):
    in_specs = (
        P("seq"),
        P(None, "chan"),
        P(None, "chan"),
        P("seq", "chan"),
        P("seq", "chan"),
        P("chan"),
        P(),
        P(),
        P(None, "chan"),
        P("chan"),
        P("seq", "chan"),
    )
    out_specs = (
        P("seq", "chan"),
        P("seq", "chan"),
        P("seq", "chan"),
        P("seq", "chan"),
        P(None, "chan"),
        P("chan"),
        P(),
        P(),
        P(None, "chan"),
    )
    return jax.shard_map(
        per_device, mesh=mesh, in_specs=in_specs, out_specs=out_specs, check_vma=False
    )
```

time: 1280 us -> 161 us (0.13)
  waiting for transfers between devices: 1030 us -> 30 us
  blocking collectives: 116 us -> 0 us
  matrix products: 22.3 us -> 57.5 us
  local copies, waits for them, and re-layouts: 6.06 us -> 24.3 us
  starting transfers between devices: 48.3 us -> 32.1 us
  between operations: 16.8 us -> 1.88 us
    ppermute x31 -> x0, waiting for transfers between devices: 690 us -> none  [the longest x30 690 us: from_partner(): return lax.ppermute(block, axis, route)]
    reduce_scatter x1 -> x0, waiting for transfers between devices: 215 us -> none  [per_device(): lax.psum_scatter(jnp.dot(matches, weighted, precision=highest, preferred_...]
    psum x2 -> x0, waiting for transfers between devices: 128 us -> none  [the longest x1 107 us: per_device(): grad_act_two = lax.psum(act_two_part, 'chan')]
    psum x1 -> x0, blocking collectives: 116 us -> none  [per_device(): lax.psum((short_part, skip_part, third_part, first_part, second_part), 's...]
    ppermute x31 -> x0, starting transfers between devices: 48.2 us -> none  [the longest x30 45.1 us: from_partner(): return lax.ppermute(block, axis, route)]
    dot_general x15 -> x25, matrix products: 22.1 us -> 57.3 us  [the longest x20 50.5 us: dot3(): jnp.dot(left, right, precision=high, preferred_element_type=jnp.float32)]
    all_to_all x0 -> x3, starting transfers between devices: none -> 32.1 us  [the longest x2 21.2 us: per_device(): packed = lax.all_to_all(packed, 'seq', 0, 0, tiled=True)]
    all_to_all x0 -> x3, waiting for transfers between devices: none -> 30 us  [the longest x2 20.6 us: per_device(): packed = lax.all_to_all(packed, 'seq', 0, 0, tiled=True)]
  transfers between devices with their start and end apart: 34 -> 3, of which waited for: 25 -> 2; matrix products, arithmetic and copies ran while one was open for 2% -> 18% of each run, Pallas kernels for 0% -> 0%
where the time goes in v1:
time: 161 us; the launch traced here: 160 us
  matrix products  57.5 us (36%)
  starting transfers between devices  32.1 us (20%)
  waiting for transfers between devices  30 us (19%)
  local copies, waits for them, and re-layouts  24.3 us (15%)
  other arithmetic  13.9 us (9%)
  between operations  1.88 us (1%)
    dot_general x20, matrix products, dot3(): jnp.dot(left, right, precision=high, preferred_element_type=jnp.float32)  50.5 us
    all_to_all x2, starting transfers between devices, per_device(): packed = lax.all_to_all(packed, 'seq', 0, 0, tiled=True)  21.2 us
    all_to_all x2, waiting for transfers between devices, per_device(): packed = lax.all_to_all(packed, 'seq', 0, 0, tiled=True)  20.6 us
    all_to_all x1, starting transfers between devices, per_device(): partial = lax.all_to_all(partial, ('seq', 'chan'), 0, 0, tiled=True)  10.9 us
    all_to_all x1, waiting for transfers between devices, per_device(): partial = lax.all_to_all(partial, ('seq', 'chan'), 0, 0, tiled=True)  9.4 us
    unnamed x134, local copies, waits for them, and re-layouts  7.74 us
  transfers between devices with their start and end apart: 3, of which 2 were waited for; matrix products, arithmetic and copies ran while one was open for 18% of the time, Pallas kernels for 0%

profile of v1, /device:TPU:1, one launch (start us, length us, event | category | flops | bytes accessed | tf_op | source)
XLA Modules:
  0.0 159.7 jit_solution(18143335809773615900)
XLA Ops:
  1.4 1.0 copy.46
  2.4 1.1 copy.48
  3.5 1.0 convert_bitcast_fusion
  4.7 1.0 pad_maximum_fusion
  5.6 11.9 %all-to-all-start = ((f32[32,17,256]{2,1,0:T(8,128)}), f32[32,17,256]{2,1,0:T(8,128)S(1)}, u32[]{:S(2)}, u32[]{:S(2)}) async-start(f32[32,17,256]{2,1,0:T(8,128)} %pad_maximum_fusion), calls=%async_computation | async-start | bytes 1572864 | tf_op jit(solution)/shard_map/all_to_all | solution.py:90
  17.6 9.9 %fusion.124 = (f32[8192,64]{0,1:T(8,128)S(1)}, f32[8192,64]{0,1:T(8,128)}) fusion(f32[33,8192]{1,0:T(8,128)} %constant.14.clone, f32[33,64]{1,0:T(8,128)S(1)} %copy-done.41), kind=kOutput, calls=%fused_computation.219 | convolution fusion | flops 103809024 | bytes 5284096 | tf_op jit(solution)/shard_map/dot_general | solution.py:46
  28.2 9.1 %fusion.125 = (f32[8192,64]{0,1:T(8,128)S(1)}, f32[8192,64]{0,1:T(8,128)}) fusion(f32[8192,64]{0,1:T(8,128)S(1)} %get-tuple-element.73, f32[64,64]{1,0:T(8,128)S(1)} %copy-done.36), kind=kOutput, calls=%fused_computation.220 | convolution fusion | flops 201326592 | bytes 6307840 | tf_op jit(solution)/shard_map/dot_general | solution.py:46
  37.3 1.3 copy-done.1
  38.6 0.8 convolution_multiply_fusion.2
  39.5 2.3 %fusion.127 = f32[512,256]{1,0:T(8,128)} fusion(f32[512,256]{1,0:T(8,128)} %constant.60, f32[256,256]{1,0:T(8,128)S(1)} %reshape.206), kind=kOutput, calls=%fused_computation.222 | convolution fusion | flops 201326592 | bytes 1310720 | tf_op jit(solution)/shard_map/dot_general | solution.py:46
  42.5 1.6 fusion.1
  48.3 1.4 fusion.77
  52.5 0.8 multiply_add_fusion
  53.4 0.9 multiply_add_fusion.1
  55.3 2.9 %multiply_reduce_fusion.2 = (f32[256]{0:T(256)}, f32[256]{0:T(256)}, f32[256]{0:T(256)}, f32[256,256]{1,0:T(8,128)S(1)}, f32[256,256]{1,0:T(8,128)}) fusion(f32[32,256,8]{1,2,0:T(8,128)S(1)} %fusion.1, f32[256,254]{1,0:T(8,128)S(1)} %get-tuple-element.54, f32[256,2]{1,0:T(8,128)S(1)} %get-tuple-element.58, f32[256,255]{1,0:T(8,128)S(1)} %get-tuple-element.56, ...), kind=kOutput, calls=%fused_computation.144 | convolution fusion | flops 101842176 | bytes 3477504 | tf_op jit(solution)/shard_map/dot_general | solution.py:46
  62.0 1.4 reduce_sum.82
  63.9 1.2 reduce_sum.83
  67.8 1.4 fusion.86
  69.2 2.1 %fusion.12 = f32[256,16]{0,1:T(8,128)S(1)} fusion(s32[32,256]{1,0:T(8,128)} %bitcast.248, bf16[32,8,256]{2,1,0:T(8,128)(2,1)S(1)} %fusion.85, bf16[32,8,256]{2,1,0:T(8,128)(2,1)S(1)} %get-tuple-element.39), kind=kOutput, calls=%fused_computation.43 | convolution fusion | flops 69730304 | bytes 311296 | tf_op jit(solution)/shard_map/wsp,scp->wc/dot_general | solution.py:186
  72.1 1.0 reshape.195
  73.2 1.7 %fusion.21 = f32[512,512]{1,0:T(8,128)S(1)} fusion(f32[256,512]{1,0:T(8,128)S(1)} %copy-done.3, f32[256,256]{1,0:T(8,128)} %get-tuple-element.51, f32[256,256]{1,0:T(8,128)} %get-tuple-element.30), kind=kOutput, calls=%fused_computation.54 | convolution fusion | flops 402784256 | bytes 2097152 | tf_op jit(solution)/shard_map/dot_general | solution.py:46
  75.3 1.1 fusion.10
  78.2 1.0 fusion.82
  79.2 7.5 %convolution_multiply_fusion = f32[64,8192]{1,0:T(8,128)S(1)} fusion(f32[8192,64]{0,1:T(8,128)S(1)} %copy-done.5, f32[8,8192]{1,0:T(8,128)S(1)} %bitcast.235, f32[8192]{0:T(1024)S(1)} %copy-done.31, f32[8]{0:T(128)S(1)} %copy-done.50, f32[8]{0:T(128)S(1)} %copy-done.48, f32[64,256]{1,0:T(8,128)S(1)} %copy-done.39, s32[]{:T(128)S(6)} %select_n.4), kind=kOutput, calls=%fused_computation | convolution fusion | flops 25886720 | bytes 4523012 | tf_op jit(solution)/shard_map/dot_general | solution.py:46
  86.8 1.0 fusion.128
  88.4 8.7 %convolution_multiply_fusion.1 = f32[8192,64]{0,1:T(8,128)S(1)} fusion(f32[64,8192]{1,0:T(8,128)S(1)} %convolution_multiply_fusion, f32[64,64]{1,0:T(8,128)S(1)} %copy-done.37, f32[8192,64]{0,1:T(8,128)S(1)} %copy-done.4), kind=kOutput, calls=%fused_computation.1 | convolution fusion | flops 201850880 | bytes 6307840 | tf_op jit(solution)/shard_map/dot_general | solution.py:46
  97.2 1.0 fusion.129
  99.3 1.0 pad_maximum_fusion.1
  100.3 9.3 %all-to-all-start.1 = ((f32[32,20,256]{2,1,0:T(8,128)}), f32[32,20,256]{2,1,0:T(8,128)S(1)}, u32[]{:S(2)}, u32[]{:S(2)}) async-start(f32[32,20,256]{2,1,0:T(8,128)} %pad_maximum_fusion.1), calls=%async_computation.1 | async-start | bytes 1572864 | tf_op jit(solution)/shard_map/all_to_all | solution.py:226
  110.0 20.6 %all-to-all-done.1 = f32[32,20,256]{2,1,0:T(8,128)S(1)} async-done(((f32[32,20,256]{2,1,0:T(8,128)}), f32[32,20,256]{2,1,0:T(8,128)S(1)}, u32[]{:S(2)}, u32[]{:S(2)}) %all-to-all-start.1) | async-done | bytes 655392 | tf_op jit(solution)/shard_map/all_to_all | solution.py:226
  131.8 10.9 %all-to-all-start.2 = ((f32[256,2,128]{2,1,0:T(2,128)}), f32[256,2,128]{2,1,0:T(2,128)S(1)}, u32[]{:S(2)}, u32[]{:S(2)}) async-start(f32[256,2,128]{2,1,0:T(2,128)} %broadcast_in_dim.54), calls=%async_computation.2 | async-start | bytes 524288 | tf_op jit(solution)/shard_map/all_to_all | solution.py:245
  148.6 9.4 %all-to-all-done.2 = f32[256,2,128]{2,1,0:T(2,128)S(1)} async-done(((f32[256,2,128]{2,1,0:T(2,128)}), f32[256,2,128]{2,1,0:T(2,128)S(1)}, u32[]{:S(2)}, u32[]{:S(2)}) %all-to-all-start.2) | async-done | bytes 262176 | tf_op jit(solution)/shard_map/all_to_all | solution.py:245
  (224 shorter events, 30.6 us)
Async XLA Ops:
  0.6 41.9 %copy-start = (bf16[256,256]{1,0:T(8,128)(2,1)S(1)}, bf16[256,256]{1,0:T(8,128)(2,1)}, u32[]{:S(2)}) copy-start(bf16[256,256]{1,0:T(8,128)(2,1)} %param.17) | copy-start | bytes 393220
  2.4 3.2 %copy-start.20 = (bf16[256,256]{0,1:T(8,128)(2,1)}, bf16[256,256]{0,1:T(8,128)(2,1)S(1)}, u32[]{:S(2)}) copy-start(bf16[256,256]{0,1:T(8,128)(2,1)S(1)} %copy.46) | copy-start | bytes 393220
  4.4 13.1 %copy-start.51 = (f32[3,256]{1,0:T(4,128)S(1)}, f32[3,256]{1,0:T(4,128)}, u32[]{:S(2)}) copy-start(f32[3,256]{1,0:T(4,128)} %param.18) | copy-start | bytes 9220
  4.4 13.1 %copy-start.41 = (f32[33,64]{1,0:T(8,128)S(1)}, f32[33,64]{1,0:T(8,128)}, u32[]{:S(2)}) copy-start(f32[33,64]{1,0:T(8,128)} %param.22) | copy-start | bytes 25348
  5.6 36.2 %all-to-all-start = ((f32[32,17,256]{2,1,0:T(8,128)}), f32[32,17,256]{2,1,0:T(8,128)S(1)}, u32[]{:S(2)}, u32[]{:S(2)}) async-start(f32[32,17,256]{2,1,0:T(8,128)} %pad_maximum_fusion), calls=%async_computation | async-start | bytes 1572864 | tf_op jit(solution)/shard_map/all_to_all | solution.py:90
  17.6 10.2 %copy-start.53 = (f32[8]{0:T(128)}, f32[8]{0:T(128)S(1)}, u32[]{:S(2)}) copy-start(f32[8]{0:T(128)S(1)} %get-tuple-element.68) | copy-start | bytes 100
  17.6 10.3 %copy-start.55 = (f32[8]{0:T(128)}, f32[8]{0:T(128)S(1)}, u32[]{:S(2)}) copy-start(f32[8]{0:T(128)S(1)} %get-tuple-element.69) | copy-start | bytes 100
  17.6 10.5 %copy-start.57 = (f32[8]{0:T(128)}, f32[8]{0:T(128)S(1)}, u32[]{:S(2)}) copy-start(f32[8]{0:T(128)S(1)} %get-tuple-element.70) | copy-start | bytes 100
  17.6 9.9 %copy-start.60 = (f32[256]{0:T(256)S(1)}, f32[256]{0:T(256)}, u32[]{:S(2)}) copy-start(f32[256]{0:T(256)} %param.21) | copy-start | bytes 3076
  17.6 10.0 %copy-start.61 = (f32[256]{0:T(256)S(1)}, f32[256]{0:T(256)}, u32[]{:S(2)}) copy-start(f32[256]{0:T(256)} %param.25) | copy-start | bytes 3076
  17.6 10.6 %copy-start.36 = (f32[64,64]{1,0:T(8,128)S(1)}, f32[64,64]{1,0:T(8,128)}, u32[]{:S(2)}) copy-start(f32[64,64]{1,0:T(8,128)} %param.23) | copy-start | bytes 49156
  27.6 9.7 %copy-start.47 = (f32[8]{0:T(128)}, f32[8]{0:T(128)S(1)}, u32[]{:S(2)}) copy-start(f32[8]{0:T(128)S(1)} %get-tuple-element.71) | copy-start | bytes 100
  27.6 9.7 %copy-start.49 = (f32[8]{0:T(128)}, f32[8]{0:T(128)S(1)}, u32[]{:S(2)}) copy-start(f32[8]{0:T(128)S(1)} %get-tuple-element.72) | copy-start | bytes 100
  27.8 27.5 %copy-start.42 = (f32[256]{0:T(256)}, f32[256]{0:T(256)S(1)}, u32[]{:S(2)}) copy-start(f32[256]{0:T(256)S(1)} %mul.418) | copy-start | bytes 3076
  27.9 19.3 %copy-start.44 = (f32[256]{0:T(256)}, f32[256]{0:T(256)S(1)}, u32[]{:S(2)}) copy-start(f32[256]{0:T(256)S(1)} %mul.382) | copy-start | bytes 3076
  28.0 19.1 %copy-start.45 = (f32[256]{0:T(256)}, f32[256]{0:T(256)S(1)}, u32[]{:S(2)}) copy-start(f32[256]{0:T(256)S(1)} %mul.388) | copy-start | bytes 3076
  28.2 19.0 %copy-start.46 = (f32[256]{0:T(256)}, f32[256]{0:T(256)S(1)}, u32[]{:S(2)}) copy-start(f32[256]{0:T(256)S(1)} %mul.385) | copy-start | bytes 3076
  28.2 9.1 %copy-start.30 = (f32[8192]{0:T(1024)}, f32[8192]{0:T(1024)S(1)}, u32[]{:S(2)}) copy-start(f32[8192]{0:T(1024)S(1)} %iota_convert_fusion) | copy-start | bytes 98308
  28.2 10.4 %copy-start.38 = (f32[64,256]{1,0:T(8,128)S(1)}, f32[64,256]{1,0:T(8,128)}, u32[]{:S(2)}) copy-start(f32[64,256]{1,0:T(8,128)} %param.24) | copy-start | bytes 196612
  41.8 5.7 %copy-start.6 = (f32[32,17,256]{2,1,0:T(8,128)}, f32[32,17,256]{2,1,0:T(8,128)S(1)}, u32[]{:S(2)}) copy-start(f32[32,17,256]{2,1,0:T(8,128)S(1)} %all-to-all-done) | copy-start | bytes 1671172
  42.5 3.9 %copy-start.40 = (s32[32,1,256]{2,0,1:T(8,128)}, s32[32,1,256]{2,0,1:T(8,128)S(1)}, u32[]{:S(2)}) copy-start(s32[32,1,256]{2,0,1:T(8,128)S(1)} %copy.70) | copy-start | bytes 98308
  44.1 3.5 %copy-start.15 = (f32[512,256]{1,0:T(8,128)S(1)}, f32[512,256]{1,0:T(8,128)}, u32[]{:S(2)}) copy-start(f32[512,256]{1,0:T(8,128)} %constant.15.clone) | copy-start | bytes 1572868
  71.3 4.0 %copy-start.11 = (f32[256,256]{1,0:T(8,128)S(1)}, f32[256,256]{1,0:T(8,128)}, u32[]{:S(2)}) copy-start(f32[256,256]{1,0:T(8,128)} %copy-done.10) | copy-start | bytes 786436
  73.2 3.3 %copy-start.26 = (f32[256,256]{1,0:T(8,128)S(1)}, f32[256,256]{1,0:T(8,128)}, u32[]{:S(2)}) copy-start(f32[256,256]{1,0:T(8,128)} %get-tuple-element.35) | copy-start | bytes 786436
  73.2 3.3 %copy-start.27 = (f32[256,256]{1,0:T(8,128)S(1)}, f32[256,256]{1,0:T(8,128)}, u32[]{:S(2)}) copy-start(f32[256,256]{1,0:T(8,128)} %get-tuple-element.52) | copy-start | bytes 786436
  88.4 8.7 %copy-start.8 = (f32[33,8192]{1,0:T(8,128)S(1)}, f32[33,8192]{1,0:T(8,128)}, u32[]{:S(2)}) copy-start(f32[33,8192]{1,0:T(8,128)} %constant.14.clone) | copy-start | bytes 3244036
  99.0 10.6 %copy-start.52 = (f32[3,256]{1,0:T(4,128)S(1)}, f32[3,256]{1,0:T(4,128)}, u32[]{:S(2)}) copy-start(f32[3,256]{1,0:T(4,128)} %param.18) | copy-start | bytes 9220
  99.1 10.7 %copy-start.35 = (s32[32,1,256]{2,1,0:T(1,128)S(1)}, s32[32,1,256]{2,1,0:T(1,128)}, u32[]{:S(2)}) copy-start(s32[32,1,256]{2,1,0:T(1,128)} %copy-done.34) | copy-start | bytes 98308
  100.3 42.4 %copy-start.21 = (bf16[256,256]{0,1:T(8,128)(2,1)S(1)}, bf16[256,256]{0,1:T(8,128)(2,1)}, u32[]{:S(2)}) copy-start(bf16[256,256]{0,1:T(8,128)(2,1)} %copy-done.20) | copy-start | bytes 393220
  100.3 42.4 %copy-start.23 = (bf16[256,256]{0,1:T(8,128)(2,1)S(1)}, bf16[256,256]{0,1:T(8,128)(2,1)}, u32[]{:S(2)}) copy-start(bf16[256,256]{0,1:T(8,128)(2,1)} %copy-done.22) | copy-start | bytes 393220
  100.3 30.3 %all-to-all-start.1 = ((f32[32,20,256]{2,1,0:T(8,128)}), f32[32,20,256]{2,1,0:T(8,128)S(1)}, u32[]{:S(2)}, u32[]{:S(2)}) async-start(f32[32,20,256]{2,1,0:T(8,128)} %pad_maximum_fusion.1), calls=%async_computation.1 | async-start | bytes 1572864 | tf_op jit(solution)/shard_map/all_to_all | solution.py:226
  131.8 26.2 %all-to-all-start.2 = ((f32[256,2,128]{2,1,0:T(2,128)}), f32[256,2,128]{2,1,0:T(2,128)S(1)}, u32[]{:S(2)}, u32[]{:S(2)}) async-start(f32[256,2,128]{2,1,0:T(2,128)} %broadcast_in_dim.54), calls=%async_computation.2 | async-start | bytes 524288 | tf_op jit(solution)/shard_map/all_to_all | solution.py:245
  (33 other events, 54.4 us)

commit v2 on v1

v2 whole, which is shorter than its diff:
```python
import math

import jax
import jax.numpy as jnp
import numpy as np
from jax import lax
from jax.experimental import pallas as pl
from jax.experimental.pallas import tpu as pltpu
from jax.sharding import PartitionSpec as P

BANDS = 16
STEPS = 4

two_pi = 2.0 * math.pi
f32 = jnp.float32
bf16 = jnp.bfloat16


def halves(table):
    upper = np.asarray(np.asarray(table, np.float32), bf16)
    lower = np.asarray(np.asarray(table, np.float32) - np.asarray(upper, np.float32), bf16)
    return upper, lower


def transform_tables(parts, rows, lanes):
    length = parts * rows
    freq = 4 * np.arange(parts, dtype=np.int64) + 1
    phase = freq[:, None] * np.arange(parts, dtype=np.int64)[None, :] % (4 * parts)
    angle = two_pi * phase / (4 * parts)
    stage = np.concatenate([np.cos(angle), -np.sin(angle)], axis=0)
    first = np.kron(stage, np.eye(lanes))
    turn = freq[:, None] * np.arange(rows, dtype=np.int64)[None, :] % (4 * length)
    turn = two_pi * turn / (4 * length)
    inner = np.arange(rows, dtype=np.int64)
    inner = two_pi * (inner[:, None] * inner[None, :] % rows) / rows
    inner = np.concatenate([np.cos(inner), np.sin(inner)], axis=1)
    turns = np.stack([np.cos(turn), np.sin(turn)]).astype(np.float32)
    return halves(first) + halves(first.T) + halves(inner), turns


def feature_table(length):
    positions = np.arange(length, dtype=np.int64)
    frequency = 2 ** np.arange(BANDS, dtype=np.int64) + 1
    phases = frequency[:, None] * positions[None, :] % length
    angles = two_pi * phases / length
    table = np.concatenate([positions[None, :] / length, np.cos(angles), np.sin(angles)], axis=0)
    spare = -table.shape[0] % 8
    return np.asarray(np.pad(table, ((0, spare), (0, 0))), np.float32)


def split(block):
    upper = block.astype(bf16)
    return upper, (block - upper.astype(f32)).astype(bf16)


def dot(left, right):
    return jnp.dot(left, right, preferred_element_type=f32)


def dot_last(left, right):
    return lax.dot_general(left, right, (((1,), (1,)), ((), ())), preferred_element_type=f32)


def product(left, right, by=dot):
    return by(left[0], right[0]) + (by(left[1], right[0]) + by(left[0], right[1]))


def product_last(left, right):
    return product(left, right, dot_last)


def sine_cosine(angle):
    turns = jnp.floor(angle * (2.0 / math.pi) + 0.5)
    rest = angle - turns * 1.5703125
    rest = rest - turns * 4.837512969970703125e-4
    rest = rest - turns * 7.54978995489188216e-8
    square = rest * rest
    sine = ((-1.9515295891e-4 * square + 8.3321608736e-3) * square - 1.6666654611e-1) * square
    sine = sine * rest + rest
    cosine = (2.443315711809948e-5 * square - 1.388731625493765e-3) * square
    cosine = (cosine + 4.166664568298827e-2) * square * square - 0.5 * square + 1.0
    quarter = turns.astype(jnp.int32)
    odd = (quarter & 1) == 1
    sine, cosine = jnp.where(odd, cosine, sine), jnp.where(odd, sine, cosine)
    sine = jnp.where((quarter & 2) == 2, -sine, sine)
    cosine = jnp.where(((quarter + 1) & 2) == 2, -cosine, cosine)
    return sine, cosine


def spread_turns(turn_ref, lanes):
    def one(table):
        parts, rows = table.shape
        wide = jnp.broadcast_to(table[:, None, :], (parts, lanes, rows))
        return wide.reshape(parts * lanes, rows)

    return one(turn_ref[0]), one(turn_ref[1])


def forward(block, first, inner, turns):
    half, rows = block.shape
    stage = product(first, split(block))
    real, imag = stage[:half], stage[half:]
    turned_real = real * turns[0] + imag * turns[1]
    turned_imag = imag * turns[0] - real * turns[1]
    along = product(split(turned_real), inner)
    across = product(split(turned_imag), inner)
    return along[:, :rows] + across[:, rows:], across[:, :rows] - along[:, rows:]


def inverse(spectrum, first_back, inner, turns, length):
    half, rows = spectrum[0].shape
    along = product(split(spectrum[0]), inner)
    across = product(split(spectrum[1]), inner)
    real = along[:, :rows] - across[:, rows:]
    imag = across[:, :rows] + along[:, rows:]
    turned_real = real * turns[0] - imag * turns[1]
    turned_imag = imag * turns[0] + real * turns[1]
    turned = jnp.concatenate([turned_real, turned_imag], axis=0)
    return product(first_back, split(turned)) * (1.0 / length)


def times(left, right):
    return left[0] * right[0] - left[1] * right[1], left[0] * right[1] + left[1] * right[0]


def against(left, right):
    return left[0] * right[0] + left[1] * right[1], left[0] * right[1] - left[1] * right[0]


def shift_back(block, lanes, steps):
    rolled = pltpu.roll(block, steps, 1)
    before = jnp.concatenate([jnp.zeros_like(rolled[:lanes]), rolled[:-lanes]], axis=0)
    column = lax.broadcasted_iota(jnp.int32, block.shape, 1)
    return jnp.where(column < steps, before, rolled)


def shift_ahead(block, lanes, steps):
    width = block.shape[1]
    rolled = pltpu.roll(block, width - steps, 1)
    after = jnp.concatenate([rolled[lanes:], jnp.zeros_like(rolled[:lanes])], axis=0)
    column = lax.broadcasted_iota(jnp.int32, block.shape, 1)
    return jnp.where(column >= width - steps, after, rolled)


def pack_kernel(key_ref, query_ref, cotangent_ref, token_ref, out_ref):
    parts = out_ref.shape[0]
    rows = key_ref.shape[0]
    lanes = key_ref.shape[1] // parts
    key_cols = key_ref[...].astype(f32).T
    grad_cols = (cotangent_ref[...].astype(f32) * query_ref[...].astype(f32)).T
    place = 0
    for block in (key_cols, grad_cols):
        for start in range(0, rows, 128):
            piece = block[:, start : start + 128].reshape(parts, lanes, 128)
            out_ref[:, place : place + lanes, :] = piece
            place += lanes
    ids = token_ref[...].astype(f32)
    out_ref[:, place : place + lanes, :] = jnp.broadcast_to(ids[None], (parts, lanes, 128))


def front_kernel(
    feature_ref,
    first_ref,
    second_ref,
    third_ref,
    param_ref,
    fwd_hi,
    fwd_lo,
    in_hi,
    in_lo,
    turn_ref,
    act_one_ref,
    cos_one_ref,
    act_two_ref,
    cos_two_ref,
    window_ref,
    spec_ref,
    filter_ref,
):
    step = pl.program_id(0)
    lanes = third_ref.shape[0]
    half, rows = window_ref.shape
    length = half // lanes * rows
    block = feature_ref.shape[1]
    pre_one = product(split(first_ref[...]), split(feature_ref[...]))
    act_one, cos_one = sine_cosine(pre_one)
    act_one_ref[...] = act_one
    cos_one_ref[...] = cos_one
    pre_two = product(split(second_ref[...]), split(act_one))
    act_two, cos_two = sine_cosine(pre_two)
    act_two_ref[...] = act_two
    cos_two_ref[...] = cos_two
    shaped = product(split(third_ref[...]), split(act_two))
    count = block // rows
    for part in range(count):
        place = pl.multiple_of((step * count + part) * lanes, lanes)
        filter_ref[pl.ds(place, lanes), :] = shaped[:, part * rows : (part + 1) * rows]

    @pl.when(step == STEPS - 1)
    def _():
        row = lax.broadcasted_iota(jnp.int32, (half, rows), 0)
        column = lax.broadcasted_iota(jnp.int32, (half, rows), 1)
        position = (row // lanes * rows + column).astype(f32)
        window = param_ref[:, 1:2] * jnp.exp(-param_ref[:, 0:1] * position)
        window_ref[...] = window
        first = (fwd_hi[...], fwd_lo[...])
        inner = (in_hi[...], in_lo[...])
        turns = spread_turns(turn_ref, lanes)
        real, imag = forward(filter_ref[...] * window, first, inner, turns)
        spec_ref[0] = real
        spec_ref[1] = imag


def middle_kernel(
    packed_ref,
    embed_ref,
    param_ref,
    window_ref,
    spec_ref,
    fwd_hi,
    fwd_lo,
    back_hi,
    back_lo,
    in_hi,
    in_lo,
    turn_ref,
    feature_ref,
    act_one_ref,
    cos_one_ref,
    act_two_ref,
    cos_two_ref,
    second_ref,
    third_ref,
    out_ref,
    embedded_ref,
    shaped_ref,
    pieces_ref,
    small_ref,
    third_acc,
    second_acc,
    first_acc,
):
    step = pl.program_id(0)
    parts = packed_ref.shape[0]
    half, rows = window_ref.shape
    lanes = half // parts
    length = parts * rows
    vocab = embed_ref.shape[1]
    hidden = second_ref.shape[0]

    @pl.when(step == 0)
    def _():
        third_acc[...] = jnp.zeros_like(third_acc)
        second_acc[...] = jnp.zeros_like(second_acc)
        first_acc[...] = jnp.zeros_like(first_acc)
        small_ref[...] = jnp.zeros_like(small_ref)
        names = lax.broadcasted_iota(jnp.int32, (vocab, rows), 0).astype(f32)
        table = embed_ref[...]

        def matches(part):
            ids = packed_ref[part, 4 * lanes : 4 * lanes + 2, :]
            ids = jnp.concatenate([ids[0:1], ids[1:2]], axis=1)
            return jnp.where(names == ids, 1.0, 0.0).astype(bf16)

        def look_up(part, carry):
            place = pl.multiple_of(part * lanes, lanes)
            embedded_ref[pl.ds(place, lanes), :] = dot(table, matches(part))
            return carry

        lax.fori_loop(0, parts, look_up, 0, unroll=4)

        def received(place):
            pair = [
                packed_ref[:, place + off * lanes : place + (off + 1) * lanes, :].reshape(half, 128)
                for off in range(2)
            ]
            return jnp.concatenate(pair, axis=1)

        key_all = received(0)
        grad_z = received(2 * lanes)
        embedded = embedded_ref[...]
        lagged = [embedded, shift_back(embedded, lanes, 1), shift_back(embedded, lanes, 2)]
        gains = [param_ref[:, 3 + lag : 4 + lag] for lag in range(3)]
        value = gains[0] * lagged[0] + gains[1] * lagged[1] + gains[2] * lagged[2]
        keyed = key_all * value
        first = (fwd_hi[...], fwd_lo[...])
        first_back = (back_hi[...], back_lo[...])
        inner = (in_hi[...], in_lo[...])
        turns = spread_turns(turn_ref, lanes)
        keyed_spec = forward(keyed, first, inner, turns)
        grad_spec = forward(grad_z, first, inner, turns)
        filter_spec = (spec_ref[0], spec_ref[1])
        back = lambda spectrum: inverse(spectrum, first_back, inner, turns, length)
        shaped_ref[...] = back(against(keyed_spec, grad_spec)) * window_ref[...]
        skip_gain = param_ref[:, 2:3]
        inner_sum = back(times(keyed_spec, filter_spec)) + skip_gain * keyed
        grad_keyed = back(against(filter_spec, grad_spec)) + skip_gain * grad_z
        place = 0
        for block in (inner_sum, grad_keyed):
            for start in range(0, rows, 128):
                piece = block[:, start : start + 128].reshape(parts, lanes, 128)
                out_ref[:, place : place + lanes, :] = piece
                place += lanes
        grad_value = grad_keyed * key_all

        def per_channel(block):
            return jnp.sum(jnp.sum(block.reshape(parts, lanes, rows), axis=0), axis=1, keepdims=True)

        for lag in range(3):
            small_ref[:, 16 + lag : 17 + lag] = per_channel(grad_value * lagged[lag])
        small_ref[:, 19:20] = per_channel(grad_z * keyed)
        scattered = gains[0] * grad_value
        for lag in (1, 2):
            scattered = scattered + gains[lag] * shift_ahead(grad_value, lanes, lag)
        upper, lower = split(scattered)
        both = (upper.reshape(parts, lanes, rows), lower.reshape(parts, lanes, rows))
        pieces_ref[...] = jnp.concatenate(both, axis=1)

        def collect(part, total):
            return total + dot_last(pieces_ref[part], matches(part))

        total = lax.fori_loop(0, parts, collect, jnp.zeros((2 * lanes, vocab), f32), unroll=4)
        embed_part = total[:lanes] + total[lanes:]
        share = vocab // parts
        out_ref[:, 4 * lanes :, :] = jnp.zeros((parts, lanes, 128), f32)
        for part in range(parts):
            own = embed_part[:, part * share : (part + 1) * share]
            out_ref[part, 4 * lanes :, 0:share] = own

    block = feature_ref.shape[1]
    count = block // rows
    pieces = []
    for part in range(count):
        place = pl.multiple_of((step * count + part) * lanes, lanes)
        pieces.append(shaped_ref[pl.ds(place, lanes), :])
    grad_shaped = split(jnp.concatenate(pieces, axis=1))
    act_two = split(act_two_ref[...])
    third_acc[...] += product_last(grad_shaped, act_two)
    grad_pre_two = product(split(third_ref[...]), grad_shaped) * cos_two_ref[...]
    grad_pre_two = split(grad_pre_two)
    second_acc[...] += product_last(split(act_one_ref[...]), grad_pre_two)
    grad_pre_one = product(split(second_ref[...]), grad_pre_two) * cos_one_ref[...]
    first_acc[...] += product_last(split(grad_pre_one), split(feature_ref[...]))

    @pl.when(step == STEPS - 1)
    def _():
        spare = jnp.zeros((hidden, hidden - first_acc.shape[1]), f32)
        joined = (second_acc[...], first_acc[...], spare)
        hidden_part = jnp.concatenate(joined, axis=1)
        cut = 2 * hidden // 4
        stacked = [hidden_part[:, cut * i : cut * (i + 1)] for i in range(4)]
        stacked = jnp.concatenate(stacked, axis=0)
        low = 4 * lanes
        out_ref[:, low:, cut : 2 * cut] = stacked.reshape(parts, lanes, cut)
        third_part = jnp.broadcast_to(third_acc[...][None], (parts, lanes, hidden))
        out_ref[:, low:, 128 - hidden : 128] = third_part
        tail = jnp.broadcast_to(small_ref[:, 16:20][None], (parts, lanes, 4))
        out_ref[:, low:, 16:20] = tail


def finish_kernel(
    packed_ref,
    query_ref,
    cotangent_ref,
    value_ref,
    out_ref,
    grad_query_ref,
    grad_key_ref,
    embed_ref,
    short_ref,
    skip_ref,
    third_ref,
):
    parts = packed_ref.shape[0]
    width = query_ref.shape[1]
    rows = query_ref.shape[0]
    lanes = width // parts
    inv_root = 1.0 / math.sqrt(parts * rows)

    def received(place):
        tile = lambda at: packed_ref[:, at : at + lanes, :].reshape(width, 128)
        return jnp.concatenate([tile(place).T, tile(place + lanes).T], axis=0)

    inner_sum = received(0)
    out_ref[...] = (query_ref[...].astype(f32) * inner_sum).astype(bf16)
    grad_query_ref[...] = (cotangent_ref[...].astype(f32) * inner_sum).astype(bf16)
    grad_key_ref[...] = (received(2 * lanes) * value_ref[...]).astype(bf16)
    small = packed_ref[:, 4 * lanes :, :].reshape(width, 128).T * inv_root
    embed_ref[...] = small[0 : embed_ref.shape[0]]
    short_ref[...] = small[16:19]
    skip_ref[...] = small[19:20]
    third_ref[...] = small[128 - third_ref.shape[0] :]


def per_device(
    tokens,
    embed_table,
    short_conv,
    query_branch,
    key_branch,
    decay_rate,
    weight_first,
    weight_second,
    weight_third,
    skip_gain,
    cotangent,
):
    parts = lax.axis_size("seq")
    groups = lax.axis_size("chan")
    seq_index = lax.axis_index("seq")
    rows, width = query_branch.shape
    lanes = width // parts
    half = parts * lanes
    length = rows * parts
    inv_root = 1.0 / math.sqrt(length)
    vocab_size = embed_table.shape[0]
    hidden = weight_first.shape[1]
    own = seq_index * lanes
    shape = jax.ShapeDtypeStruct
    chunk = (parts, 5 * lanes, 128)
    whole = pl.BlockSpec(memory_space=pltpu.VMEM)

    packed = pl.pallas_call(
        pack_kernel,
        out_shape=shape(chunk, f32),
        in_specs=[whole] * 4,
        out_specs=whole,
        name="pack",
    )(key_branch, query_branch, cotangent, jnp.pad(tokens.reshape(2, 128), ((0, lanes - 2), (0, 0))))
    packed = lax.all_to_all(packed, "seq", 0, 0, tiled=True)

    embed_own = lax.dynamic_slice_in_dim(embed_table, own, lanes, axis=1).T
    short_own = lax.dynamic_slice_in_dim(short_conv, own, lanes, axis=1)
    decay_own = lax.dynamic_slice_in_dim(decay_rate, own, lanes, axis=0)
    skip_own = lax.dynamic_slice_in_dim(skip_gain, own, lanes, axis=0)
    third_own = lax.dynamic_slice_in_dim(weight_third, own, lanes, axis=1)
    scaling = jnp.sqrt(jnp.expm1(-2.0 * decay_own) / jnp.expm1(-2.0 * length * decay_own))
    params = [decay_own, scaling, skip_own, short_own[0], short_own[1], short_own[2]]
    params = jnp.tile(jnp.stack(params + [skip_own, skip_own], axis=1), (parts, 1))

    (fwd_hi, fwd_lo, back_hi, back_lo, in_hi, in_lo), turns = transform_tables(parts, rows, lanes)
    features = jnp.asarray(feature_table(length))
    feats = features.shape[0]
    first_t = jnp.pad(weight_first.T, ((0, 0), (0, feats - weight_first.shape[0])))
    block = length // STEPS
    still = lambda array: pl.BlockSpec(array.shape, lambda i: (0,) * array.ndim)
    moving = lambda count: pl.BlockSpec((count, block), lambda i: (0, i))

    act = shape((hidden, length), f32)
    window_shape, spec_shape = shape((half, rows), f32), shape((2, half, rows), f32)
    second_t, third_t = weight_second.T, third_own.T
    act_one, cos_one, act_two, cos_two, window, spec = pl.pallas_call(
        front_kernel,
        out_shape=(act, act, act, act, window_shape, spec_shape),
        grid=(STEPS,),
        in_specs=[moving(feats)]
        + [still(a) for a in (first_t, second_t, third_t, params, fwd_hi, fwd_lo, in_hi, in_lo, turns)],
        out_specs=[moving(hidden)] * 4 + [still(window_shape), still(spec_shape)],
        scratch_shapes=[pltpu.VMEM((half, rows), f32)],
        name="front",
    )(features, first_t, second_t, third_t, params, fwd_hi, fwd_lo, in_hi, in_lo, turns)

    operands = (packed, embed_own, params, window, spec, fwd_hi, fwd_lo, back_hi, back_lo, in_hi, in_lo, turns)
    sent = pl.pallas_call(
        middle_kernel,
        out_shape=shape(chunk, f32),
        grid=(STEPS,),
        in_specs=[still(a) for a in operands]
        + [moving(feats)]
        + [moving(hidden)] * 4
        + [still(weight_second), still(third_own)],
        out_specs=still(shape(chunk, f32)),
        scratch_shapes=[
            pltpu.VMEM((half, rows), f32),
            pltpu.VMEM((half, rows), f32),
            pltpu.VMEM((parts, 2 * lanes, rows), bf16),
            pltpu.VMEM((lanes, 128), f32),
            pltpu.VMEM((lanes, hidden), f32),
            pltpu.VMEM((hidden, hidden), f32),
            pltpu.VMEM((hidden, feats), f32),
        ],
        name="middle",
    )(*operands, features, act_one, cos_one, act_two, cos_two, weight_second, third_own)
    got = lax.all_to_all(sent, "seq", 0, 0, tiled=True)

    cut = 2 * hidden // 4
    partial = jnp.sum(got[:, 4 * lanes :, cut : 2 * cut], axis=0).reshape(1, 2, 128)
    partial = jnp.broadcast_to(partial, (parts * groups, 2, 128))
    partial = lax.all_to_all(partial, ("seq", "chan"), 0, 0, tiled=True)
    total = jnp.sum(partial.reshape(parts, groups, 2, 128), axis=1) * inv_root
    total = total.reshape(4, hidden, cut).transpose(1, 0, 2).reshape(hidden, 2 * hidden)
    grad_second = total[:, :hidden]
    grad_first = total[:, hidden : hidden + weight_first.shape[0]].T

    vocab_ids = jnp.arange(vocab_size, dtype=jnp.int32)
    before = lax.dynamic_index_in_dim(packed, jnp.maximum(seq_index - 1, 0), 0, keepdims=False)
    before = before[4 * lanes + 1, 126:].astype(jnp.int32)
    before = jnp.where(seq_index > 0, before, -1)
    window_ids = jnp.concatenate([before, tokens])
    lookup = (window_ids[:, None] == vocab_ids[None, :]).astype(bf16)
    embedded = jnp.dot(lookup, embed_table, preferred_element_type=f32)
    value_rows = (
        short_conv[0] * embedded[2:]
        + short_conv[1] * embedded[1:-1]
        + short_conv[2] * embedded[:-2]
    )
    rows_shape = shape((rows, width), bf16)
    own_vocab = vocab_size // parts
    operator_out, grad_query, grad_key, grad_embed, grad_short, grad_skip, grad_third = pl.pallas_call(
        finish_kernel,
        out_shape=(
            rows_shape,
            rows_shape,
            rows_shape,
            shape((own_vocab, width), f32),
            shape((3, width), f32),
            shape((1, width), f32),
            shape((hidden, width), f32),
        ),
        in_specs=[whole] * 4,
        out_specs=[whole] * 7,
        name="finish",
    )(got, query_branch, cotangent, value_rows)
    return (
        operator_out,
        grad_query,
        grad_key,
        grad_embed,
        grad_short,
        grad_skip.reshape(width),
        grad_first,
        grad_second,
        grad_third,
    )


def solution(mesh):
    in_specs = (
        P("seq"),
        P(None, "chan"),
        P(None, "chan"),
        P("seq", "chan"),
        P("seq", "chan"),
        P("chan"),
        P(),
        P(),
        P(None, "chan"),
        P("chan"),
        P("seq", "chan"),
    )
    out_specs = (
        P("seq", "chan"),
        P("seq", "chan"),
        P("seq", "chan"),
        P("seq", "chan"),
        P(None, "chan"),
        P("chan"),
        P(),
        P(),
        P(None, "chan"),
    )
    return jax.shard_map(
        per_device, mesh=mesh, in_specs=in_specs, out_specs=out_specs, check_vma=False
    )
```

time: 161 us -> 110 us (0.68)
  matrix products: 57.5 us -> 0.23 us
  Pallas kernels: 0 us -> 36.4 us
  local copies, waits for them, and re-layouts: 24.3 us -> 9.88 us
  other arithmetic: 13.9 us -> 1.2 us
    dot_general x26 -> x1, matrix products: 57.5 us -> 0.23 us  [per_device(): embedded = jnp.dot(lookup, embed_table, preferred_element_type=f32)]
    pallas_call x0 -> x4, Pallas kernels: none -> 36.4 us  [the longest x1 18.5 us: per_device(): pl.pallas_call(middle_kernel, out_shape=shape(chunk, f32), grid=(STEPS,),...]
    all_to_all x2 -> x1, waiting for transfers between devices: 20.6 us -> 0.41 us  [per_device(): packed = lax.all_to_all(packed, 'seq', 0, 0, tiled=True)]
    all_to_all x0 -> x1, waiting for transfers between devices: none -> 17.2 us  [per_device(): got = lax.all_to_all(sent, 'seq', 0, 0, tiled=True)]
    all_to_all x2 -> x1, starting transfers between devices: 21.2 us -> 11.9 us  [per_device(): packed = lax.all_to_all(packed, 'seq', 0, 0, tiled=True)]
    all_to_all x0 -> x1, starting transfers between devices: none -> 8.84 us  [per_device(): got = lax.all_to_all(sent, 'seq', 0, 0, tiled=True)]
    unnamed x134 -> x24, local copies, waits for them, and re-layouts: 7.74 us -> 3.1 us
    slice x11 -> x1, local copies, waits for them, and re-layouts: 3.38 us -> 0.01 us  [per_device(): grad_second = total[:, :hidden]]
  transfers between devices with their start and end apart: 3 -> 3, of which waited for: 2 -> 3; matrix products, arithmetic and copies ran while one was open for 18% -> 6% of each run, Pallas kernels for 0% -> 14%
where the time goes in v2:
time: 110 us
  Pallas kernels  36.4 us (33%)
  starting transfers between devices  31.7 us (29%)
  waiting for transfers between devices  29.6 us (27%)
  local copies, waits for them, and re-layouts  9.88 us (9%)
  other arithmetic  1.2 us (1%)
    pallas_call x1, Pallas kernels, per_device(): pl.pallas_call(middle_kernel, out_shape=shape(chunk, f32), grid=(STEPS,),...  18.5 us
    all_to_all x1, waiting for transfers between devices, per_device(): got = lax.all_to_all(sent, 'seq', 0, 0, tiled=True)  17.2 us
    pallas_call x1, Pallas kernels, per_device(): pl.pallas_call(front_kernel, out_shape=(act, act, act, act, window_shape,...  13.7 us
    all_to_all x1, waiting for transfers between devices, per_device(): partial = lax.all_to_all(partial, ('seq', 'chan'), 0, 0, tiled=True)  12 us
    all_to_all x1, starting transfers between devices, per_device(): packed = lax.all_to_all(packed, 'seq', 0, 0, tiled=True)  11.9 us
    all_to_all x1, starting transfers between devices, per_device(): partial = lax.all_to_all(partial, ('seq', 'chan'), 0, 0, tiled=True)  11 us
    all_to_all x1, starting transfers between devices, per_device(): got = lax.all_to_all(sent, 'seq', 0, 0, tiled=True)  8.84 us
    unnamed x24, local copies, waits for them, and re-layouts  3.1 us
  transfers between devices with their start and end apart: 3, of which 3 were waited for; matrix products, arithmetic and copies ran while one was open for 6% of the time, Pallas kernels for 14%

profile of v2, /device:TPU:1, one launch (start us, length us, event | category | flops | bytes accessed | tf_op | source)
XLA Modules:
  0.0 109.8 jit_solution(1012135161223175305)
XLA Ops:
  0.7 1.4 %pad.8.token_ref = s32[8,128]{1,0:T(8,128)} pad(s32[2,128]{1,0:T(2,128)} %bitcast.44, s32[]{:T(128)} %constant.18.clone.1), padding=0_6x0_0 | pad | bytes 5124 | tf_op jit(solution)/shard_map/jit(_pad)/pad | solution.py:429
  2.1 2.1 %pack.1 = f32[32,40,128]{2,1,0:T(8,128)} custom-call(bf16[256,256]{1,0:T(8,128)(2,1)} %key_ref.1, bf16[256,256]{1,0:T(8,128)(2,1)} %query_ref.3, bf16[256,256]{1,0:T(8,128)(2,1)} %cotangent_ref.3, s32[8,128]{1,0:T(8,128)} %pad.8.token_ref), custom_call_target="tpu_custom_call" | custom-call | tf_op jit(solution)/shard_map/pack/pallas_call | solution.py:423
  4.2 11.9 %all-to-all-start = ((f32[32,40,128]{2,1,0:T(8,128)}), f32[32,40,128]{2,1,0:T(8,128)S(1)}, u32[]{:S(2)}, u32[]{:S(2)}) async-start(f32[32,40,128]{2,1,0:T(8,128)} %pack.1), calls=%async_computation | async-start | bytes 1310720 | tf_op jit(solution)/shard_map/all_to_all | solution.py:430
  16.1 0.1 constant_dynamic-slice_fusion.2
  16.2 0.7 copy.68
  16.9 0.1 sqrt_bitcast_fusion
  17.0 0.1 constant_dynamic-slice_fusion.1
  17.1 0.1 copy.58
  17.2 0.7 copy.59
  18.0 0.7 copy.60.third_ref
  18.7 0.6 pad.9.first_ref
  19.3 0.7 broadcast_bitcast_fusion.param_ref
  20.0 13.7 %front.1 = (f32[64,8192]{1,0:T(8,128)}, f32[64,8192]{1,0:T(8,128)}, f32[64,8192]{1,0:T(8,128)}, f32[64,8192]{1,0:T(8,128)}, f32[256,256]{1,0:T(8,128)}, /*index=5*/f32[2,256,256]{2,1,0:T(8,128)}) custom-call(f32[40,8192]{1,0:T(8,128)} %constant.46.clone.feature_ref, f32[64,40]{1,0:T(8,128)} %pad.9.first_ref, f32[64,64]{1,0:T(8,128)} %bitcast.38, ...), custom_call_target="tpu_custom_call" | custom-call | tf_op jit(solution)/shard_map/front/pallas_call | solution.py:452
  33.6 0.7 constant_dynamic-slice_fusion.third_ref
  34.3 0.4 all-to-all-done.packed_ref
  34.7 0.9 copy-done.2
  35.6 18.5 %middle.1 = f32[32,40,128]{2,1,0:T(8,128)} custom-call(f32[32,40,128]{2,1,0:T(8,128)} %copy-done.2, bf16[8,256]{1,0:T(8,128)(2,1)} %bitcast.40, f32[256,8]{1,0:T(8,128)} %broadcast_bitcast_fusion.param_ref, f32[256,256]{1,0:T(8,128)} %get-tuple-element.22.window_ref, f32[2,256,256]{2,1,0:T(8,128)} %get-tuple-element.23.spec_ref, ...), custom_call_target="tpu_custom_call" | custom-call | tf_op jit(solution)/shard_map/middle/pallas_call | solution.py:464
  54.1 8.8 %all-to-all-start.1 = ((f32[32,40,128]{2,1,0:T(8,128)}), f32[32,40,128]{2,1,0:T(8,128)S(1)}, u32[]{:S(2)}, u32[]{:S(2)}) async-start(f32[32,40,128]{2,1,0:T(8,128)} %middle.1), calls=%async_computation.1 | async-start | bytes 1310720 | tf_op jit(solution)/shard_map/all_to_all | solution.py:484
  63.0 0.7 dynamic-slice_bitcast_fusion
  63.8 17.2 %all-to-all-done.1.packed_ref = f32[32,40,128]{2,1,0:T(8,128)S(1)} async-done(((f32[32,40,128]{2,1,0:T(8,128)}), f32[32,40,128]{2,1,0:T(8,128)S(1)}, u32[]{:S(2)}, u32[]{:S(2)}) %all-to-all-start.1) | async-done | bytes 655392 | tf_op jit(solution)/shard_map/all_to_all | solution.py:484
  81.0 0.1 slice_reduce_fusion
  81.1 0.1 broadcast_in_dim.14
  81.2 0.8 broadcast_in_dim.15
  81.9 11.0 %all-to-all-start.2 = ((f32[256,2,128]{2,1,0:T(2,128)}), f32[256,2,128]{2,1,0:T(2,128)S(1)}, u32[]{:S(2)}, u32[]{:S(2)}) async-start(f32[256,2,128]{2,1,0:T(2,128)} %broadcast_in_dim.15), calls=%async_computation.2 | async-start | bytes 524288 | tf_op jit(solution)/shard_map/all_to_all | solution.py:489
  93.0 0.2 fusion
  93.3 0.8 fusion.1.value_ref
  94.1 2.2 %finish.1 = (bf16[256,256]{1,0:T(8,128)(2,1)}, bf16[256,256]{1,0:T(8,128)(2,1)}, bf16[256,256]{1,0:T(8,128)(2,1)}, f32[8,256]{1,0:T(8,128)}, f32[3,256]{1,0:T(4,...) custom-call(f32[32,40,128]{2,1,0:T(8,128)} %copy-done.1, bf16[256,256]{1,0:T(8,128)(2,1)} %query_ref.3, ...), custom_call_target="tpu_custom_call" | custom-call | tf_op jit(solution)/shard_map/finish/pallas_call | solution.py:509
  96.2 12.0 %all-to-all-done.2 = f32[256,2,128]{2,1,0:T(2,128)S(1)} async-done(((f32[256,2,128]{2,1,0:T(2,128)}), f32[256,2,128]{2,1,0:T(2,128)S(1)}, u32[]{:S(2)}, u32[]{:S(2)}) %all-to-all-start.2) | async-done | bytes 262176 | tf_op jit(solution)/shard_map/all_to_all | solution.py:489
  108.3 0.1 mul.63
  108.4 0.1 copy.63
  108.5 0.6 slice_bitcast_fusion
  109.1 0.7 copy.64
  (29 shorter events, 0.5 us)
Async XLA Ops:
  0.6 15.4 %copy-start = (bf16[256,256]{1,0:T(8,128)(2,1)S(1)}, bf16[256,256]{1,0:T(8,128)(2,1)}, u32[]{:S(2)}) copy-start(bf16[256,256]{1,0:T(8,128)(2,1)} %param.20) | copy-start | bytes 393220
  0.7 16.2 %copy-start.8 = (f32[256]{0:T(256)S(1)}, f32[256]{0:T(256)}, u32[]{:S(2)}) copy-start(f32[256]{0:T(256)} %param.24) | copy-start | bytes 3076
  0.7 16.2 %copy-start.9 = (f32[256]{0:T(256)S(1)}, f32[256]{0:T(256)}, u32[]{:S(2)}) copy-start(f32[256]{0:T(256)} %param.28) | copy-start | bytes 3076
  0.7 16.3 %copy-start.6 = (f32[3,256]{1,0:T(4,128)S(1)}, f32[3,256]{1,0:T(4,128)}, u32[]{:S(2)}) copy-start(f32[3,256]{1,0:T(4,128)} %param.21) | copy-start | bytes 9220
  0.7 16.5 %copy-start.5 = (f32[33,64]{1,0:T(8,128)S(1)}, f32[33,64]{1,0:T(8,128)}, u32[]{:S(2)}) copy-start(f32[33,64]{1,0:T(8,128)} %param.25) | copy-start | bytes 25348
  0.7 16.5 %copy-start.3 = (f32[64,64]{1,0:T(8,128)S(1)}, f32[64,64]{1,0:T(8,128)}, u32[]{:S(2)}) copy-start(f32[64,64]{1,0:T(8,128)} %second_ref.1) | copy-start | bytes 49156
  0.7 17.2 %copy-start.4 = (f32[64,256]{1,0:T(8,128)S(1)}, f32[64,256]{1,0:T(8,128)}, u32[]{:S(2)}) copy-start(f32[64,256]{1,0:T(8,128)} %param.27) | copy-start | bytes 196612
  4.2 30.5 %all-to-all-start = ((f32[32,40,128]{2,1,0:T(8,128)}), f32[32,40,128]{2,1,0:T(8,128)S(1)}, u32[]{:S(2)}, u32[]{:S(2)}) async-start(f32[32,40,128]{2,1,0:T(8,128)} %pack.1), calls=%async_computation | async-start | bytes 1310720 | tf_op jit(solution)/shard_map/all_to_all | solution.py:430
  34.7 0.9 copy-start.2
  54.1 38.8 %copy-start.7 = (s32[256]{0:T(256)S(1)}, s32[256]{0:T(256)}, u32[]{:S(2)}) copy-start(s32[256]{0:T(256)} %param.19) | copy-start | bytes 3076
  54.1 26.9 %all-to-all-start.1 = ((f32[32,40,128]{2,1,0:T(8,128)}), f32[32,40,128]{2,1,0:T(8,128)S(1)}, u32[]{:S(2)}, u32[]{:S(2)}) async-start(f32[32,40,128]{2,1,0:T(8,128)} %middle.1), calls=%async_computation.1 | async-start | bytes 1310720 | tf_op jit(solution)/shard_map/all_to_all | solution.py:484
  81.0 13.1 %copy-start.1 = (f32[32,40,128]{2,1,0:T(8,128)}, f32[32,40,128]{2,1,0:T(8,128)S(1)}, u32[]{:S(2)}) copy-start(f32[32,40,128]{2,1,0:T(8,128)S(1)} %all-to-all-done.1.packed_ref) | copy-start | bytes 1966084
  81.9 26.3 %all-to-all-start.2 = ((f32[256,2,128]{2,1,0:T(2,128)}), f32[256,2,128]{2,1,0:T(2,128)S(1)}, u32[]{:S(2)}, u32[]{:S(2)}) async-start(f32[256,2,128]{2,1,0:T(2,128)} %broadcast_in_dim.15), calls=%async_computation.2 | async-start | bytes 524288 | tf_op jit(solution)/shard_map/all_to_all | solution.py:489

commit v3 on v2

--- a/solution.py
+++ b/solution.py
@@ -10,6 +10,7 @@
 
 BANDS = 16
 STEPS = 4
+VOCAB = 256
 
 two_pi = 2.0 * math.pi
 f32 = jnp.float32
@@ -28,14 +29,14 @@
     phase = freq[:, None] * np.arange(parts, dtype=np.int64)[None, :] % (4 * parts)
     angle = two_pi * phase / (4 * parts)
     stage = np.concatenate([np.cos(angle), -np.sin(angle)], axis=0)
-    first = np.kron(stage, np.eye(lanes))
     turn = freq[:, None] * np.arange(rows, dtype=np.int64)[None, :] % (4 * length)
     turn = two_pi * turn / (4 * length)
     inner = np.arange(rows, dtype=np.int64)
     inner = two_pi * (inner[:, None] * inner[None, :] % rows) / rows
     inner = np.concatenate([np.cos(inner), np.sin(inner)], axis=1)
     turns = np.stack([np.cos(turn), np.sin(turn)]).astype(np.float32)
-    return halves(first) + halves(first.T) + halves(inner), turns
+    stages = [np.repeat(table, lanes, axis=1).astype(np.float32) for table in (stage, stage.T)]
+    return stages, halves(inner), turns
 
 
 def feature_table(length):
@@ -87,6 +88,15 @@
     return sine, cosine
 
 
+def spread_stage(table_ref, lanes):
+    table = table_ref[...]
+    count, width = table.shape
+    wide = jnp.broadcast_to(table[:, None, :], (count, lanes, width)).reshape(count * lanes, width)
+    row = lax.broadcasted_iota(jnp.int32, wide.shape, 0) & (lanes - 1)
+    column = lax.broadcasted_iota(jnp.int32, wide.shape, 1) & (lanes - 1)
+    return split(jnp.where(row == column, wide, 0.0))
+
+
 def spread_turns(turn_ref, lanes):
     def one(table):
         parts, rows = table.shape
@@ -155,6 +165,7 @@
             out_ref[:, place : place + lanes, :] = piece
             place += lanes
     ids = token_ref[...].astype(f32)
+    ids = jnp.concatenate([ids, jnp.zeros((lanes - ids.shape[0], 128), f32)], axis=0)
     out_ref[:, place : place + lanes, :] = jnp.broadcast_to(ids[None], (parts, lanes, 128))
 
 
@@ -164,8 +175,7 @@
     second_ref,
     third_ref,
     param_ref,
-    fwd_hi,
-    fwd_lo,
+    stage_ref,
     in_hi,
     in_lo,
     turn_ref,
@@ -203,7 +213,7 @@
         position = (row // lanes * rows + column).astype(f32)
         window = param_ref[:, 1:2] * jnp.exp(-param_ref[:, 0:1] * position)
         window_ref[...] = window
-        first = (fwd_hi[...], fwd_lo[...])
+        first = spread_stage(stage_ref, lanes)
         inner = (in_hi[...], in_lo[...])
         turns = spread_turns(turn_ref, lanes)
         real, imag = forward(filter_ref[...] * window, first, inner, turns)
@@ -211,16 +221,35 @@
         spec_ref[1] = imag
 
 
-def middle_kernel(
+def received(packed_ref, place, lanes):
+    parts = packed_ref.shape[0]
+    pair = [
+        packed_ref[:, at : at + lanes, :].reshape(parts * lanes, 128)
+        for at in (place, place + lanes)
+    ]
+    return jnp.concatenate(pair, axis=1)
+
+
+def matches(packed_ref, part, lanes, vocab):
+    ids = packed_ref[part, 4 * lanes : 4 * lanes + 2, :]
+    ids = jnp.concatenate([ids[0:1], ids[1:2]], axis=1)
+    names = lax.broadcasted_iota(jnp.int32, (vocab, ids.shape[1]), 0).astype(f32)
+    return jnp.where(names == ids, 1.0, 0.0).astype(bf16)
+
+
+def lagged_values(embedded, param_ref, lanes):
+    lagged = [embedded, shift_back(embedded, lanes, 1), shift_back(embedded, lanes, 2)]
+    gains = [param_ref[:, 3 + lag : 4 + lag] for lag in range(3)]
+    return lagged, gains, gains[0] * lagged[0] + gains[1] * lagged[1] + gains[2] * lagged[2]
+
+
+def filter_kernel(
     packed_ref,
     embed_ref,
     param_ref,
     window_ref,
-    spec_ref,
-    fwd_hi,
-    fwd_lo,
-    back_hi,
-    back_lo,
+    stage_ref,
+    back_ref,
     in_hi,
     in_lo,
     turn_ref,
@@ -231,12 +260,12 @@
     cos_two_ref,
     second_ref,
     third_ref,
-    out_ref,
+    hidden_ref,
+    third_acc,
     embedded_ref,
+    keyed_spec_ref,
+    grad_spec_ref,
     shaped_ref,
-    pieces_ref,
-    small_ref,
-    third_acc,
     second_acc,
     first_acc,
 ):
@@ -253,79 +282,29 @@
         third_acc[...] = jnp.zeros_like(third_acc)
         second_acc[...] = jnp.zeros_like(second_acc)
         first_acc[...] = jnp.zeros_like(first_acc)
-        small_ref[...] = jnp.zeros_like(small_ref)
-        names = lax.broadcasted_iota(jnp.int32, (vocab, rows), 0).astype(f32)
         table = embed_ref[...]
-
-        def matches(part):
-            ids = packed_ref[part, 4 * lanes : 4 * lanes + 2, :]
-            ids = jnp.concatenate([ids[0:1], ids[1:2]], axis=1)
-            return jnp.where(names == ids, 1.0, 0.0).astype(bf16)
 
         def look_up(part, carry):
             place = pl.multiple_of(part * lanes, lanes)
-            embedded_ref[pl.ds(place, lanes), :] = dot(table, matches(part))
+            found = dot(table, matches(packed_ref, part, lanes, vocab))
+            embedded_ref[pl.ds(place, lanes), :] = found
             return carry
 
         lax.fori_loop(0, parts, look_up, 0, unroll=4)
-
-        def received(place):
-            pair = [
-                packed_ref[:, place + off * lanes : place + (off + 1) * lanes, :].reshape(half, 128)
-                for off in range(2)
-            ]
-            return jnp.concatenate(pair, axis=1)
-
-        key_all = received(0)
-        grad_z = received(2 * lanes)
-        embedded = embedded_ref[...]
-        lagged = [embedded, shift_back(embedded, lanes, 1), shift_back(embedded, lanes, 2)]
-        gains = [param_ref[:, 3 + lag : 4 + lag] for lag in range(3)]
-        value = gains[0] * lagged[0] + gains[1] * lagged[1] + gains[2] * lagged[2]
-        keyed = key_all * value
-        first = (fwd_hi[...], fwd_lo[...])
-        first_back = (back_hi[...], back_lo[...])
+        key_all = received(packed_ref, 0, lanes)
+        grad_z = received(packed_ref, 2 * lanes, lanes)
+        _, _, value = lagged_values(embedded_ref[...], param_ref, lanes)
+        first = spread_stage(stage_ref, lanes)
+        first_back = spread_stage(back_ref, lanes)
         inner = (in_hi[...], in_lo[...])
         turns = spread_turns(turn_ref, lanes)
-        keyed_spec = forward(keyed, first, inner, turns)
+        keyed_spec = forward(key_all * value, first, inner, turns)
         grad_spec = forward(grad_z, first, inner, turns)
-        filter_spec = (spec_ref[0], spec_ref[1])
-        back = lambda spectrum: inverse(spectrum, first_back, inner, turns, length)
-        shaped_ref[...] = back(against(keyed_spec, grad_spec)) * window_ref[...]
-        skip_gain = param_ref[:, 2:3]
-        inner_sum = back(times(keyed_spec, filter_spec)) + skip_gain * keyed
-        grad_keyed = back(against(filter_spec, grad_spec)) + skip_gain * grad_z
-        place = 0
-        for block in (inner_sum, grad_keyed):
-            for start in range(0, rows, 128):
-                piece = block[:, start : start + 128].reshape(parts, lanes, 128)
-                out_ref[:, place : place + lanes, :] = piece
-                place += lanes
-        grad_value = grad_keyed * key_all
-
-        def per_channel(block):
-            return jnp.sum(jnp.sum(block.reshape(parts, lanes, rows), axis=0), axis=1, keepdims=True)
-
-        for lag in range(3):
-            small_ref[:, 16 + lag : 17 + lag] = per_channel(grad_value * lagged[lag])
-        small_ref[:, 19:20] = per_channel(grad_z * keyed)
-        scattered = gains[0] * grad_value
-        for lag in (1, 2):
-            scattered = scattered + gains[lag] * shift_ahead(grad_value, lanes, lag)
-        upper, lower = split(scattered)
-        both = (upper.reshape(parts, lanes, rows), lower.reshape(parts, lanes, rows))
-        pieces_ref[...] = jnp.concatenate(both, axis=1)
-
-        def collect(part, total):
-            return total + dot_last(pieces_ref[part], matches(part))
-
-        total = lax.fori_loop(0, parts, collect, jnp.zeros((2 * lanes, vocab), f32), unroll=4)
-        embed_part = total[:lanes] + total[lanes:]
-        share = vocab // parts
-        out_ref[:, 4 * lanes :, :] = jnp.zeros((parts, lanes, 128), f32)
-        for part in range(parts):
-            own = embed_part[:, part * share : (part + 1) * share]
-            out_ref[part, 4 * lanes :, 0:share] = own
+        for ref, spectrum in ((keyed_spec_ref, keyed_spec), (grad_spec_ref, grad_spec)):
+            ref[0] = spectrum[0]
+            ref[1] = spectrum[1]
+        grad_filter = inverse(against(keyed_spec, grad_spec), first_back, inner, turns, length)
+        shaped_ref[...] = grad_filter * window_ref[...]
 
     block = feature_ref.shape[1]
     count = block // rows
@@ -346,16 +325,91 @@
     def _():
         spare = jnp.zeros((hidden, hidden - first_acc.shape[1]), f32)
         joined = (second_acc[...], first_acc[...], spare)
-        hidden_part = jnp.concatenate(joined, axis=1)
-        cut = 2 * hidden // 4
-        stacked = [hidden_part[:, cut * i : cut * (i + 1)] for i in range(4)]
-        stacked = jnp.concatenate(stacked, axis=0)
-        low = 4 * lanes
-        out_ref[:, low:, cut : 2 * cut] = stacked.reshape(parts, lanes, cut)
-        third_part = jnp.broadcast_to(third_acc[...][None], (parts, lanes, hidden))
-        out_ref[:, low:, 128 - hidden : 128] = third_part
-        tail = jnp.broadcast_to(small_ref[:, 16:20][None], (parts, lanes, 4))
-        out_ref[:, low:, 16:20] = tail
+        inv_root = 1.0 / math.sqrt(length)
+        hidden_ref[...] = (jnp.concatenate(joined, axis=1) * inv_root).reshape(hidden_ref.shape)
+
+
+def back_kernel(
+    packed_ref,
+    param_ref,
+    spec_ref,
+    back_ref,
+    in_hi,
+    in_lo,
+    turn_ref,
+    embedded_ref,
+    keyed_spec_ref,
+    grad_spec_ref,
+    inner_ref,
+    grad_ref,
+):
+    parts = packed_ref.shape[0]
+    half, rows = embedded_ref.shape
+    lanes = half // parts
+    length = parts * rows
+    key_all = received(packed_ref, 0, lanes)
+    grad_z = received(packed_ref, 2 * lanes, lanes)
+    _, _, value = lagged_values(embedded_ref[...], param_ref, lanes)
+    first_back = spread_stage(back_ref, lanes)
+    inner = (in_hi[...], in_lo[...])
+    turns = spread_turns(turn_ref, lanes)
+    keyed_spec = (keyed_spec_ref[0], keyed_spec_ref[1])
+    grad_spec = (grad_spec_ref[0], grad_spec_ref[1])
+    filter_spec = (spec_ref[0], spec_ref[1])
+    back = lambda spectrum: inverse(spectrum, first_back, inner, turns, length)
+    skip_gain = param_ref[:, 2:3]
+    inner_ref[...] = back(times(keyed_spec, filter_spec)) + skip_gain * (key_all * value)
+    grad_ref[...] = back(against(filter_spec, grad_spec)) + skip_gain * grad_z
+
+
+def send_kernel(
+    packed_ref, param_ref, embedded_ref, inner_ref, grad_ref, third_ref, hidden_ref, out_ref, pieces_ref
+):
+    parts = packed_ref.shape[0]
+    half, rows = embedded_ref.shape
+    lanes = half // parts
+    hidden = third_ref.shape[1]
+    key_all = received(packed_ref, 0, lanes)
+    grad_z = received(packed_ref, 2 * lanes, lanes)
+    lagged, gains, value = lagged_values(embedded_ref[...], param_ref, lanes)
+    grad_keyed = grad_ref[...]
+    place = 0
+    for block in (inner_ref[...], grad_keyed):
+        for start in range(0, rows, 128):
+            piece = block[:, start : start + 128].reshape(parts, lanes, 128)
+            out_ref[:, place : place + lanes, :] = piece
+            place += lanes
+    grad_value = grad_keyed * key_all
+
+    def per_channel(block):
+        return jnp.sum(jnp.sum(block.reshape(parts, lanes, rows), axis=0), axis=1, keepdims=True)
+
+    tails = [per_channel(grad_value * lagged[lag]) for lag in range(3)]
+    tails.append(per_channel(grad_z * (key_all * value)))
+    scattered = gains[0] * grad_value
+    for lag in (1, 2):
+        scattered = scattered + gains[lag] * shift_ahead(grad_value, lanes, lag)
+    upper, lower = split(scattered)
+    both = (upper.reshape(parts, lanes, rows), lower.reshape(parts, lanes, rows))
+    pieces_ref[...] = jnp.concatenate(both, axis=1)
+
+    def collect(part, total):
+        return total + dot_last(pieces_ref[part], matches(packed_ref, part, lanes, VOCAB))
+
+    total = lax.fori_loop(0, parts, collect, jnp.zeros((2 * lanes, VOCAB), f32), unroll=4)
+    embed_part = total[:lanes] + total[lanes:]
+    share = VOCAB // parts
+    low, high = 4 * lanes, 5 * lanes
+    out_ref[:, low:high, :] = jnp.zeros((parts, lanes, 128), f32)
+    for part in range(parts):
+        own = embed_part[:, part * share : (part + 1) * share]
+        out_ref[part, low:high, 0:share] = own
+    third_part = jnp.broadcast_to(third_ref[...][None], (parts, lanes, hidden))
+    out_ref[:, low:high, 128 - hidden : 128] = third_part
+    for at, tail in enumerate(tails):
+        out_ref[:, low:high, 16 + at : 17 + at] = jnp.broadcast_to(tail[None], (parts, lanes, 1))
+    hidden_sum = jnp.sum(hidden_ref[...], axis=0)
+    out_ref[:, high:, :] = jnp.broadcast_to(hidden_sum[None], (parts,) + hidden_sum.shape)
 
 
 def finish_kernel(
@@ -377,15 +431,15 @@
     lanes = width // parts
     inv_root = 1.0 / math.sqrt(parts * rows)
 
-    def received(place):
+    def crossed(place):
         tile = lambda at: packed_ref[:, at : at + lanes, :].reshape(width, 128)
         return jnp.concatenate([tile(place).T, tile(place + lanes).T], axis=0)
 
-    inner_sum = received(0)
+    inner_sum = crossed(0)
     out_ref[...] = (query_ref[...].astype(f32) * inner_sum).astype(bf16)
     grad_query_ref[...] = (cotangent_ref[...].astype(f32) * inner_sum).astype(bf16)
-    grad_key_ref[...] = (received(2 * lanes) * value_ref[...]).astype(bf16)
-    small = packed_ref[:, 4 * lanes :, :].reshape(width, 128).T * inv_root
+    grad_key_ref[...] = (crossed(2 * lanes) * value_ref[...]).astype(bf16)
+    small = packed_ref[:, 4 * lanes : 5 * lanes, :].reshape(width, 128).T * inv_root
     embed_ref[...] = small[0 : embed_ref.shape[0]]
     short_ref[...] = small[16:19]
     skip_ref[...] = small[19:20]
@@ -412,7 +466,6 @@
     lanes = width // parts
     half = parts * lanes
     length = rows * parts
-    inv_root = 1.0 / math.sqrt(length)
     vocab_size = embed_table.shape[0]
     hidden = weight_first.shape[1]
     own = seq_index * lanes
@@ -426,7 +479,7 @@
         in_specs=[whole] * 4,
         out_specs=whole,
         name="pack",
-    )(key_branch, query_branch, cotangent, jnp.pad(tokens.reshape(2, 128), ((0, lanes - 2), (0, 0))))
+    )(key_branch, query_branch, cotangent, tokens.reshape(rows // 128, 128))
     packed = lax.all_to_all(packed, "seq", 0, 0, tiled=True)
 
     embed_own = lax.dynamic_slice_in_dim(embed_table, own, lanes, axis=1).T
@@ -438,7 +491,7 @@
     params = [decay_own, scaling, skip_own, short_own[0], short_own[1], short_own[2]]
     params = jnp.tile(jnp.stack(params + [skip_own, skip_own], axis=1), (parts, 1))
 
-    (fwd_hi, fwd_lo, back_hi, back_lo, in_hi, in_lo), turns = transform_tables(parts, rows, lanes)
+    (stage, stage_back), (in_hi, in_lo), turns = transform_tables(parts, rows, lanes)
     features = jnp.asarray(feature_table(length))
     feats = features.shape[0]
     first_t = jnp.pad(weight_first.T, ((0, 0), (0, feats - weight_first.shape[0])))
@@ -454,41 +507,54 @@
         out_shape=(act, act, act, act, window_shape, spec_shape),
         grid=(STEPS,),
         in_specs=[moving(feats)]
-        + [still(a) for a in (first_t, second_t, third_t, params, fwd_hi, fwd_lo, in_hi, in_lo, turns)],
+        + [still(a) for a in (first_t, second_t, third_t, params, stage, in_hi, in_lo, turns)],
         out_specs=[moving(hidden)] * 4 + [still(window_shape), still(spec_shape)],
         scratch_shapes=[pltpu.VMEM((half, rows), f32)],
         name="front",
-    )(features, first_t, second_t, third_t, params, fwd_hi, fwd_lo, in_hi, in_lo, turns)
-
-    operands = (packed, embed_own, params, window, spec, fwd_hi, fwd_lo, back_hi, back_lo, in_hi, in_lo, turns)
-    sent = pl.pallas_call(
-        middle_kernel,
-        out_shape=shape(chunk, f32),
+    )(features, first_t, second_t, third_t, params, stage, in_hi, in_lo, turns)
+
+    operands = (packed, embed_own, params, window, stage, stage_back, in_hi, in_lo, turns)
+    hidden_shape = shape((groups, hidden // groups, 128), f32)
+    third_shape = shape((lanes, hidden), f32)
+    results = (hidden_shape, third_shape, window_shape, spec_shape, spec_shape)
+    hidden_part, third_part, embedded_all, keyed_spec, grad_spec = pl.pallas_call(
+        filter_kernel,
+        out_shape=results,
         grid=(STEPS,),
         in_specs=[still(a) for a in operands]
         + [moving(feats)]
         + [moving(hidden)] * 4
         + [still(weight_second), still(third_own)],
-        out_specs=still(shape(chunk, f32)),
+        out_specs=[still(a) for a in results],
         scratch_shapes=[
             pltpu.VMEM((half, rows), f32),
-            pltpu.VMEM((half, rows), f32),
-            pltpu.VMEM((parts, 2 * lanes, rows), bf16),
-            pltpu.VMEM((lanes, 128), f32),
-            pltpu.VMEM((lanes, hidden), f32),
             pltpu.VMEM((hidden, hidden), f32),
             pltpu.VMEM((hidden, feats), f32),
         ],
-        name="middle",
+        name="filter",
     )(*operands, features, act_one, cos_one, act_two, cos_two, weight_second, third_own)
+
+    hidden_part = lax.all_to_all(hidden_part, "chan", 0, 0, tiled=True)
+    inner_sum, grad_keyed = pl.pallas_call(
+        back_kernel,
+        out_shape=(window_shape, window_shape),
+        in_specs=[whole] * 10,
+        out_specs=[whole] * 2,
+        name="back",
+    )(packed, params, spec, stage_back, in_hi, in_lo, turns, embedded_all, keyed_spec, grad_spec)
+    sent = pl.pallas_call(
+        send_kernel,
+        out_shape=shape((parts, 5 * lanes + hidden // groups, 128), f32),
+        in_specs=[whole] * 7,
+        out_specs=whole,
+        scratch_shapes=[pltpu.VMEM((parts, 2 * lanes, rows), bf16)],
+        name="send",
+    )(packed, params, embedded_all, inner_sum, grad_keyed, third_part, hidden_part)
     got = lax.all_to_all(sent, "seq", 0, 0, tiled=True)
 
-    cut = 2 * hidden // 4
-    partial = jnp.sum(got[:, 4 * lanes :, cut : 2 * cut], axis=0).reshape(1, 2, 128)
-    partial = jnp.broadcast_to(partial, (parts * groups, 2, 128))
-    partial = lax.all_to_all(partial, ("seq", "chan"), 0, 0, tiled=True)
-    total = jnp.sum(partial.reshape(parts, groups, 2, 128), axis=1) * inv_root
-    total = total.reshape(4, hidden, cut).transpose(1, 0, 2).reshape(hidden, 2 * hidden)
+    hidden_sum = jnp.sum(got[:, 5 * lanes :], axis=0)
+    spread = jnp.broadcast_to(hidden_sum[None], (groups,) + hidden_sum.shape)
+    total = lax.all_to_all(spread, "chan", 0, 0, tiled=True).reshape(hidden, 128)
     grad_second = total[:, :hidden]
     grad_first = total[:, hidden : hidden + weight_first.shape[0]].T
 

time: 110 us -> 110 us (level)
  waiting for transfers between devices: 29.6 us -> 22.2 us
  Pallas kernels: 36.4 us -> 42.2 us
  starting transfers between devices: 31.7 us -> 33.7 us
    all_to_all x1 -> x2, waiting for transfers between devices: 12 us -> 1.73 us  [the longest x1 1.73 us: per_device(): lax.all_to_all(spread, 'chan', 0, 0, tiled=True).reshape(hidden, 128)]
    pallas_call x1 -> x3, Pallas kernels: 18.5 us -> 24.2 us  [the longest x1 14.2 us: per_device(): pl.pallas_call(filter_kernel, out_shape=results, grid=(STEPS,), in_specs=...]
    all_to_all x1 -> x2, starting transfers between devices: 11 us -> 14.4 us  [the longest x1 7.44 us: per_device(): lax.all_to_all(spread, 'chan', 0, 0, tiled=True).reshape(hidden, 128)]
    all_to_all x1, waiting for transfers between devices: 17.2 us -> 19.9 us  [per_device(): got = lax.all_to_all(sent, 'seq', 0, 0, tiled=True)]
    all_to_all x1, starting transfers between devices: 8.84 us -> 7.39 us  [per_device(): got = lax.all_to_all(sent, 'seq', 0, 0, tiled=True)]
    pad x1 -> x0, local copies, waits for them, and re-layouts: 1.37 us -> none  [per_device(): jnp.pad(tokens.reshape(2, 128), ((0, lanes - 2), (0, 0)))]
    unnamed x24 -> x27, local copies, waits for them, and re-layouts: 3.1 us -> 4.35 us
  transfers between devices with their start and end apart: 3 -> 4, of which waited for: 3 -> 3; matrix products, arithmetic and copies ran while one was open for 6% -> 6% of each run, Pallas kernels for 14% -> 19%
where the time goes in v3:
time: 110 us; the launch traced here: 109 us
  Pallas kernels  42.2 us (38%)
  starting transfers between devices  33.7 us (31%)
  waiting for transfers between devices  22.2 us (20%)
  local copies, waits for them, and re-layouts  8.86 us (8%)
    all_to_all x1, waiting for transfers between devices, per_device(): got = lax.all_to_all(sent, 'seq', 0, 0, tiled=True)  19.9 us
    pallas_call x1, Pallas kernels, per_device(): pl.pallas_call(filter_kernel, out_shape=results, grid=(STEPS,), in_specs=...  14.2 us
    pallas_call x1, Pallas kernels, per_device(): pl.pallas_call(front_kernel, out_shape=(act, act, act, act, window_shape,...  13.5 us
    all_to_all x1, starting transfers between devices, per_device(): packed = lax.all_to_all(packed, 'seq', 0, 0, tiled=True)  11.9 us
    all_to_all x1, starting transfers between devices, per_device(): lax.all_to_all(spread, 'chan', 0, 0, tiled=True).reshape(hidden, 128)  7.44 us
    all_to_all x1, starting transfers between devices, per_device(): got = lax.all_to_all(sent, 'seq', 0, 0, tiled=True)  7.39 us
    all_to_all x1, starting transfers between devices, per_device(): hidden_part = lax.all_to_all(hidden_part, 'chan', 0, 0, tiled=True)  6.97 us
    pallas_call x1, Pallas kernels, per_device(): pl.pallas_call(send_kernel, out_shape=shape((parts, 5 * lanes + hidden //...  5.16 us
  transfers between devices with their start and end apart: 4, of which 3 were waited for; matrix products, arithmetic and copies ran while one was open for 6% of the time, Pallas kernels for 19%

profile of v3, /device:TPU:1, one launch (start us, length us, event | category | flops | bytes accessed | tf_op | source)
XLA Modules:
  0.0 108.9 jit_solution(7711329889385675427)
XLA Ops:
  0.7 2.2 %pack.1 = f32[32,40,128]{2,1,0:T(8,128)} custom-call(bf16[256,256]{1,0:T(8,128)(2,1)} %key_ref.1, bf16[256,256]{1,0:T(8,128)(2,1)} %query_ref.3, bf16[256,256]{1,0:T(8,128)(2,1)} %cotangent_ref.3, s32[2,128]{1,0:T(2,128)} %bitcast.38), custom_call_target="tpu_custom_call" | custom-call | tf_op jit(solution)/shard_map/pack/pallas_call | solution.py:476
  2.9 11.9 %all-to-all-start = ((f32[32,40,128]{2,1,0:T(8,128)}), f32[32,40,128]{2,1,0:T(8,128)S(1)}, u32[]{:S(2)}, u32[]{:S(2)}) async-start(f32[32,40,128]{2,1,0:T(8,128)} %pack.1), calls=%async_computation | async-start | bytes 1310720 | tf_op jit(solution)/shard_map/all_to_all | solution.py:483
  14.8 0.1 sqrt_bitcast_fusion
  14.9 0.1 constant_dynamic-slice_fusion.2
  15.2 0.7 copy.30.third_ref
  15.9 0.1 copy.28
  15.9 0.7 copy.29
  16.6 0.1 constant_dynamic-slice_fusion.1
  16.7 0.7 copy.32
  17.4 0.6 pad.4.first_ref
  18.0 0.7 broadcast_bitcast_fusion.param_ref
  18.7 13.5 %front.1 = (f32[64,8192]{1,0:T(8,128)}, f32[64,8192]{1,0:T(8,128)}, f32[64,8192]{1,0:T(8,128)}, f32[64,8192]{1,0:T(8,128)}, f32[256,256]{1,0:T(8,128)}, /*index=5*/f32[2,256,256]{2,1,0:T(8,128)}) custom-call(f32[40,8192]{1,0:T(8,128)} %constant.40.clone.feature_ref, f32[64,40]{1,0:T(8,128)} %pad.4.first_ref, f32[64,64]{1,0:T(8,128)} %bitcast.35, ...), custom_call_target="tpu_custom_call" | custom-call | tf_op jit(solution)/shard_map/front/pallas_call | solution.py:505
  32.2 0.7 constant_dynamic-slice_fusion.third_ref
  32.9 0.5 all-to-all-done.packed_ref
  33.5 0.9 copy-done.1
  34.4 14.2 %filter.1 = (f32[8,8,128]{2,1,0:T(8,128)}, f32[8,64]{1,0:T(8,128)}, f32[256,256]{1,0:T(8,128)}, f32[2,256,256]{2,1,0:T(8,128)}, f32[2,256,256]{2,1,0:T(8,128)}) custom-call(f32[32,40,128]{2,1,0:T(8,128)} %copy-done.1, bf16[8,256]{1,0:T(8,128)(2,1)} %bitcast.37, f32[256,8]{1,0:T(8,128)} %broadcast_bitcast_fusion.param_ref, ...), custom_call_target="tpu_custom_call" | custom-call | tf_op jit(solution)/shard_map/filter/pallas_call | solution.py:520
  48.6 7.0 %all-to-all-start.1 = ((f32[8,8,128]{2,1,0:T(8,128)}), f32[8,8,128]{2,1,0:T(8,128)S(1)}, u32[]{:S(2)}, u32[]{:S(2)}) async-start(f32[8,8,128]{2,1,0:T(8,128)} %get-tuple-element.41), calls=%async_computation.1 | async-start | bytes 65536 | tf_op jit(solution)/shard_map/all_to_all | solution.py:537
  55.6 4.8 %back.1 = (f32[256,256]{1,0:T(8,128)}, f32[256,256]{1,0:T(8,128)}) custom-call(f32[32,40,128]{2,1,0:T(8,128)} %copy-done.1, f32[256,8]{1,0:T(8,128)} %broadcast_bitcast_fusion.param_ref, f32[2,256,256]{2,1,0:T(8,128)} %get-tuple-element.35.spec_ref, f32[32,512]{1,0:T(8,128)} %constant.45.clone.back_ref, bf16[256,512]{1,0:T(8,128)(2,1)} %constant.42.clone.in_hi, ...), custom_call_target="tpu_custom_call" | custom-call | tf_op jit(solution)/shard_map/back/pallas_call | solution.py:538
  60.5 0.6 copy-done.4
  61.1 5.2 %send.1 = f32[32,48,128]{2,1,0:T(8,128)} custom-call(f32[32,40,128]{2,1,0:T(8,128)} %copy-done.1, f32[256,8]{1,0:T(8,128)} %broadcast_bitcast_fusion.param_ref, f32[256,256]{1,0:T(8,128)} %get-tuple-element.34.embedded_ref, f32[256,256]{1,0:T(8,128)} %get-tuple-element.38.inner_ref, f32[256,256]{1,0:T(8,128)} %get-tuple-element.39.grad_ref, ...), custom_call_target="tpu_custom_call" | custom-call | tf_op jit(solution)/shard_map/send/pallas_call | solution.py:545
  66.2 7.4 %all-to-all-start.2 = ((f32[32,48,128]{2,1,0:T(8,128)}), f32[32,48,128]{2,1,0:T(8,128)S(1)}, u32[]{:S(2)}, u32[]{:S(2)}) async-start(f32[32,48,128]{2,1,0:T(8,128)} %send.1), calls=%async_computation.2 | async-start | bytes 1572864 | tf_op jit(solution)/shard_map/all_to_all | solution.py:553
  73.6 0.7 dynamic-slice_bitcast_fusion
  74.4 0.1 fusion.4
  74.5 0.2 fusion
  74.8 19.9 %all-to-all-done.2.packed_ref = f32[32,48,128]{2,1,0:T(8,128)S(1)} async-done(((f32[32,48,128]{2,1,0:T(8,128)}), f32[32,48,128]{2,1,0:T(8,128)S(1)}, u32[]{:S(2)}, u32[]{:S(2)}) %all-to-all-start.2) | async-done | bytes 786464 | tf_op jit(solution)/shard_map/all_to_all | solution.py:553
  94.7 0.7 broadcast_in_dim.7
  95.4 7.4 %all-to-all-start.3 = ((f32[8,8,128]{2,1,0:T(8,128)}), f32[8,8,128]{2,1,0:T(8,128)S(1)}, u32[]{:S(2)}, u32[]{:S(2)}) async-start(f32[8,8,128]{2,1,0:T(8,128)} %broadcast_in_dim.7), calls=%async_computation.3 | async-start | bytes 65536 | tf_op jit(solution)/shard_map/all_to_all | solution.py:557
  102.8 0.8 fusion.1.value_ref
  103.6 2.2 %finish.1 = (bf16[256,256]{1,0:T(8,128)(2,1)}, bf16[256,256]{1,0:T(8,128)(2,1)}, bf16[256,256]{1,0:T(8,128)(2,1)}, f32[8,256]{1,0:T(8,128)}, f32[3,256]{1,0:T(4,...) custom-call(f32[32,48,128]{2,1,0:T(8,128)} %copy-done.2, bf16[256,256]{1,0:T(8,128)(2,1)} %query_ref.3, ...), custom_call_target="tpu_custom_call" | custom-call | tf_op jit(solution)/shard_map/finish/pallas_call | solution.py:575
  105.8 1.7 %all-to-all-done.3 = f32[8,8,128]{2,1,0:T(8,128)S(1)} async-done(((f32[8,8,128]{2,1,0:T(8,128)}), f32[8,8,128]{2,1,0:T(8,128)S(1)}, u32[]{:S(2)}, u32[]{:S(2)}) %all-to-all-start.3) | async-done | bytes 32800 | tf_op jit(solution)/shard_map/all_to_all | solution.py:557
  107.6 0.7 copy.31
  108.3 0.6 copy.34
  (29 shorter events, 0.4 us)
Async XLA Ops:
  0.6 16.0 %copy-start = (bf16[256,256]{1,0:T(8,128)(2,1)S(1)}, bf16[256,256]{1,0:T(8,128)(2,1)}, u32[]{:S(2)}) copy-start(bf16[256,256]{1,0:T(8,128)(2,1)} %param.18) | copy-start | bytes 393220
  0.7 14.1 %copy-start.9 = (f32[256]{0:T(256)S(1)}, f32[256]{0:T(256)}, u32[]{:S(2)}) copy-start(f32[256]{0:T(256)} %param.22) | copy-start | bytes 3076
  0.7 14.1 %copy-start.10 = (f32[256]{0:T(256)S(1)}, f32[256]{0:T(256)}, u32[]{:S(2)}) copy-start(f32[256]{0:T(256)} %param.26) | copy-start | bytes 3076
  0.7 14.2 %copy-start.7 = (f32[3,256]{1,0:T(4,128)S(1)}, f32[3,256]{1,0:T(4,128)}, u32[]{:S(2)}) copy-start(f32[3,256]{1,0:T(4,128)} %param.19) | copy-start | bytes 9220
  0.7 14.4 %copy-start.5 = (f32[64,256]{1,0:T(8,128)S(1)}, f32[64,256]{1,0:T(8,128)}, u32[]{:S(2)}) copy-start(f32[64,256]{1,0:T(8,128)} %param.25) | copy-start | bytes 196612
  0.7 15.2 %copy-start.6 = (f32[33,64]{1,0:T(8,128)S(1)}, f32[33,64]{1,0:T(8,128)}, u32[]{:S(2)}) copy-start(f32[33,64]{1,0:T(8,128)} %param.23) | copy-start | bytes 25348
  0.7 15.2 %copy-start.3 = (f32[64,64]{1,0:T(8,128)S(1)}, f32[64,64]{1,0:T(8,128)}, u32[]{:S(2)}) copy-start(f32[64,64]{1,0:T(8,128)} %second_ref.1) | copy-start | bytes 49156
  2.9 30.5 %all-to-all-start = ((f32[32,40,128]{2,1,0:T(8,128)}), f32[32,40,128]{2,1,0:T(8,128)S(1)}, u32[]{:S(2)}, u32[]{:S(2)}) async-start(f32[32,40,128]{2,1,0:T(8,128)} %pack.1), calls=%async_computation | async-start | bytes 1310720 | tf_op jit(solution)/shard_map/all_to_all | solution.py:483
  33.5 0.9 copy-start.1
  48.6 11.8 %all-to-all-start.1 = ((f32[8,8,128]{2,1,0:T(8,128)}), f32[8,8,128]{2,1,0:T(8,128)S(1)}, u32[]{:S(2)}, u32[]{:S(2)}) async-start(f32[8,8,128]{2,1,0:T(8,128)} %get-tuple-element.41), calls=%async_computation.1 | async-start | bytes 65536 | tf_op jit(solution)/shard_map/all_to_all | solution.py:537
  60.4 14.0 %copy-start.8 = (s32[256]{0:T(256)S(1)}, s32[256]{0:T(256)}, u32[]{:S(2)}) copy-start(s32[256]{0:T(256)} %param.17) | copy-start | bytes 3076
  60.4 0.6 copy-start.4
  66.2 28.4 %all-to-all-start.2 = ((f32[32,48,128]{2,1,0:T(8,128)}), f32[32,48,128]{2,1,0:T(8,128)S(1)}, u32[]{:S(2)}, u32[]{:S(2)}) async-start(f32[32,48,128]{2,1,0:T(8,128)} %send.1), calls=%async_computation.2 | async-start | bytes 1572864 | tf_op jit(solution)/shard_map/all_to_all | solution.py:553
  94.7 9.0 %copy-start.2 = (f32[32,48,128]{2,1,0:T(8,128)}, f32[32,48,128]{2,1,0:T(8,128)S(1)}, u32[]{:S(2)}) copy-start(f32[32,48,128]{2,1,0:T(8,128)S(1)} %all-to-all-done.2.packed_ref) | copy-start | bytes 2359300
  95.4 12.2 %all-to-all-start.3 = ((f32[8,8,128]{2,1,0:T(8,128)}), f32[8,8,128]{2,1,0:T(8,128)S(1)}, u32[]{:S(2)}, u32[]{:S(2)}) async-start(f32[8,8,128]{2,1,0:T(8,128)} %broadcast_in_dim.7), calls=%async_computation.3 | async-start | bytes 65536 | tf_op jit(solution)/shard_map/all_to_all | solution.py:557

commit v4 on v3

--- a/solution.py
+++ b/solution.py
@@ -233,8 +233,11 @@
 def matches(packed_ref, part, lanes, vocab):
     ids = packed_ref[part, 4 * lanes : 4 * lanes + 2, :]
     ids = jnp.concatenate([ids[0:1], ids[1:2]], axis=1)
-    names = lax.broadcasted_iota(jnp.int32, (vocab, ids.shape[1]), 0).astype(f32)
-    return jnp.where(names == ids, 1.0, 0.0).astype(bf16)
+    ids = jnp.broadcast_to(ids, (16, ids.shape[1])).astype(bf16)
+    names = lax.broadcasted_iota(jnp.int32, (vocab, ids.shape[1]), 0).astype(f32).astype(bf16)
+    names = names.reshape(vocab // 16, 16, ids.shape[1])
+    one, zero = jnp.ones((), bf16), jnp.zeros((), bf16)
+    return jnp.where(names == ids[None], one, zero).reshape(vocab, ids.shape[1])
 
 
 def lagged_values(embedded, param_ref, lanes):
@@ -260,11 +263,12 @@
     cos_two_ref,
     second_ref,
     third_ref,
+    spec_ref,
     hidden_ref,
     third_acc,
     embedded_ref,
-    keyed_spec_ref,
-    grad_spec_ref,
+    inner_ref,
+    grad_ref,
     shaped_ref,
     second_acc,
     first_acc,
@@ -294,17 +298,19 @@
         key_all = received(packed_ref, 0, lanes)
         grad_z = received(packed_ref, 2 * lanes, lanes)
         _, _, value = lagged_values(embedded_ref[...], param_ref, lanes)
+        keyed = key_all * value
         first = spread_stage(stage_ref, lanes)
         first_back = spread_stage(back_ref, lanes)
         inner = (in_hi[...], in_lo[...])
         turns = spread_turns(turn_ref, lanes)
-        keyed_spec = forward(key_all * value, first, inner, turns)
+        keyed_spec = forward(keyed, first, inner, turns)
         grad_spec = forward(grad_z, first, inner, turns)
-        for ref, spectrum in ((keyed_spec_ref, keyed_spec), (grad_spec_ref, grad_spec)):
-            ref[0] = spectrum[0]
-            ref[1] = spectrum[1]
-        grad_filter = inverse(against(keyed_spec, grad_spec), first_back, inner, turns, length)
-        shaped_ref[...] = grad_filter * window_ref[...]
+        back = lambda spectrum: inverse(spectrum, first_back, inner, turns, length)
+        shaped_ref[...] = back(against(keyed_spec, grad_spec)) * window_ref[...]
+        filter_spec = (spec_ref[0], spec_ref[1])
+        skip_gain = param_ref[:, 2:3]
+        inner_ref[...] = back(times(keyed_spec, filter_spec)) + skip_gain * keyed
+        grad_ref[...] = back(against(filter_spec, grad_spec)) + skip_gain * grad_z
 
     block = feature_ref.shape[1]
     count = block // rows
@@ -329,41 +335,8 @@
         hidden_ref[...] = (jnp.concatenate(joined, axis=1) * inv_root).reshape(hidden_ref.shape)
 
 
-def back_kernel(
-    packed_ref,
-    param_ref,
-    spec_ref,
-    back_ref,
-    in_hi,
-    in_lo,
-    turn_ref,
-    embedded_ref,
-    keyed_spec_ref,
-    grad_spec_ref,
-    inner_ref,
-    grad_ref,
-):
-    parts = packed_ref.shape[0]
-    half, rows = embedded_ref.shape
-    lanes = half // parts
-    length = parts * rows
-    key_all = received(packed_ref, 0, lanes)
-    grad_z = received(packed_ref, 2 * lanes, lanes)
-    _, _, value = lagged_values(embedded_ref[...], param_ref, lanes)
-    first_back = spread_stage(back_ref, lanes)
-    inner = (in_hi[...], in_lo[...])
-    turns = spread_turns(turn_ref, lanes)
-    keyed_spec = (keyed_spec_ref[0], keyed_spec_ref[1])
-    grad_spec = (grad_spec_ref[0], grad_spec_ref[1])
-    filter_spec = (spec_ref[0], spec_ref[1])
-    back = lambda spectrum: inverse(spectrum, first_back, inner, turns, length)
-    skip_gain = param_ref[:, 2:3]
-    inner_ref[...] = back(times(keyed_spec, filter_spec)) + skip_gain * (key_all * value)
-    grad_ref[...] = back(against(filter_spec, grad_spec)) + skip_gain * grad_z
-
-
 def send_kernel(
-    packed_ref, param_ref, embedded_ref, inner_ref, grad_ref, third_ref, hidden_ref, out_ref, pieces_ref
+    packed_ref, param_ref, embedded_ref, inner_ref, grad_ref, third_ref, out_ref, pieces_ref
 ):
     parts = packed_ref.shape[0]
     half, rows = embedded_ref.shape
@@ -408,8 +381,6 @@
     out_ref[:, low:high, 128 - hidden : 128] = third_part
     for at, tail in enumerate(tails):
         out_ref[:, low:high, 16 + at : 17 + at] = jnp.broadcast_to(tail[None], (parts, lanes, 1))
-    hidden_sum = jnp.sum(hidden_ref[...], axis=0)
-    out_ref[:, high:, :] = jnp.broadcast_to(hidden_sum[None], (parts,) + hidden_sum.shape)
 
 
 def finish_kernel(
@@ -516,15 +487,15 @@
     operands = (packed, embed_own, params, window, stage, stage_back, in_hi, in_lo, turns)
     hidden_shape = shape((groups, hidden // groups, 128), f32)
     third_shape = shape((lanes, hidden), f32)
-    results = (hidden_shape, third_shape, window_shape, spec_shape, spec_shape)
-    hidden_part, third_part, embedded_all, keyed_spec, grad_spec = pl.pallas_call(
+    results = (hidden_shape, third_shape) + (window_shape,) * 3
+    hidden_part, third_part, embedded_all, inner_sum, grad_keyed = pl.pallas_call(
         filter_kernel,
         out_shape=results,
         grid=(STEPS,),
         in_specs=[still(a) for a in operands]
         + [moving(feats)]
         + [moving(hidden)] * 4
-        + [still(weight_second), still(third_own)],
+        + [still(weight_second), still(third_own), still(spec)],
         out_specs=[still(a) for a in results],
         scratch_shapes=[
             pltpu.VMEM((half, rows), f32),
@@ -532,31 +503,20 @@
             pltpu.VMEM((hidden, feats), f32),
         ],
         name="filter",
-    )(*operands, features, act_one, cos_one, act_two, cos_two, weight_second, third_own)
+    )(*operands, features, act_one, cos_one, act_two, cos_two, weight_second, third_own, spec)
 
     hidden_part = lax.all_to_all(hidden_part, "chan", 0, 0, tiled=True)
-    inner_sum, grad_keyed = pl.pallas_call(
-        back_kernel,
-        out_shape=(window_shape, window_shape),
-        in_specs=[whole] * 10,
-        out_specs=[whole] * 2,
-        name="back",
-    )(packed, params, spec, stage_back, in_hi, in_lo, turns, embedded_all, keyed_spec, grad_spec)
     sent = pl.pallas_call(
         send_kernel,
         out_shape=shape((parts, 5 * lanes + hidden // groups, 128), f32),
-        in_specs=[whole] * 7,
+        in_specs=[whole] * 6,
         out_specs=whole,
         scratch_shapes=[pltpu.VMEM((parts, 2 * lanes, rows), bf16)],
         name="send",
-    )(packed, params, embedded_all, inner_sum, grad_keyed, third_part, hidden_part)
-    got = lax.all_to_all(sent, "seq", 0, 0, tiled=True)
-
-    hidden_sum = jnp.sum(got[:, 5 * lanes :], axis=0)
-    spread = jnp.broadcast_to(hidden_sum[None], (groups,) + hidden_sum.shape)
-    total = lax.all_to_all(spread, "chan", 0, 0, tiled=True).reshape(hidden, 128)
-    grad_second = total[:, :hidden]
-    grad_first = total[:, hidden : hidden + weight_first.shape[0]].T
+    )(packed, params, embedded_all, inner_sum, grad_keyed, third_part)
+    hidden_sum = jnp.sum(hidden_part, axis=0)
+    spread = jnp.broadcast_to(hidden_sum[None], (parts,) + hidden_sum.shape)
+    sent = lax.dynamic_update_slice(sent, spread, (0, 5 * lanes, 0))
 
     vocab_ids = jnp.arange(vocab_size, dtype=jnp.int32)
     before = lax.dynamic_index_in_dim(packed, jnp.maximum(seq_index - 1, 0), 0, keepdims=False)
@@ -570,6 +530,15 @@
         + short_conv[1] * embedded[1:-1]
         + short_conv[2] * embedded[:-2]
     )
+    sent, value_rows = lax.optimization_barrier((sent, value_rows))
+    got = lax.all_to_all(sent, "seq", 0, 0, tiled=True)
+
+    hidden_sum = jnp.sum(got[:, 5 * lanes :], axis=0)
+    spread = jnp.broadcast_to(hidden_sum[None], (groups,) + hidden_sum.shape)
+    total = lax.all_to_all(spread, "chan", 0, 0, tiled=True).reshape(hidden, 128)
+    grad_second = total[:, :hidden]
+    grad_first = total[:, hidden : hidden + weight_first.shape[0]].T
+
     rows_shape = shape((rows, width), bf16)
     own_vocab = vocab_size // parts
     operator_out, grad_query, grad_key, grad_embed, grad_short, grad_skip, grad_third = pl.pallas_call(

time: 110 us -> 108 us (0.982)
  blocking collectives: 0 us -> 29.6 us
  waiting for transfers between devices: 22.2 us -> 3.04 us
  starting transfers between devices: 33.7 us -> 25.2 us
  Pallas kernels: 42.2 us -> 38.9 us
    all_to_all x0 -> x1, blocking collectives: none -> 29.6 us  [per_device(): got = lax.all_to_all(sent, 'seq', 0, 0, tiled=True)]
    all_to_all x1 -> x0, waiting for transfers between devices: 19.9 us -> none  [per_device(): got = lax.all_to_all(sent, 'seq', 0, 0, tiled=True)]
    all_to_all x1 -> x0, starting transfers between devices: 7.39 us -> none  [per_device(): got = lax.all_to_all(sent, 'seq', 0, 0, tiled=True)]
    pallas_call x1 -> x0, Pallas kernels: 4.82 us -> none  [per_device(): pl.pallas_call(back_kernel, out_shape=(window_shape, window_shape), in_sp...]
    pallas_call x1, Pallas kernels: 14.2 us -> 15.8 us  [per_device(): pl.pallas_call(filter_kernel, out_shape=results, grid=(STEPS,), in_specs=...]
    unnamed x27 -> x25, local copies, waits for them, and re-layouts: 4.35 us -> 3.73 us
  transfers between devices with their start and end apart: 4 -> 3, of which waited for: 3 -> 2; matrix products, arithmetic and copies ran while one was open for 6% -> 6% of each run, Pallas kernels for 19% -> 15%
where the time goes in v4:
time: 108 us
  Pallas kernels  38.9 us (36%)
  blocking collectives  29.6 us (27%)
  starting transfers between devices  25.2 us (23%)
  local copies, waits for them, and re-layouts  8.91 us (8%)
  waiting for transfers between devices  3.04 us (3%)
  other arithmetic  1.08 us (1%)
    all_to_all x1, blocking collectives, per_device(): got = lax.all_to_all(sent, 'seq', 0, 0, tiled=True)  29.6 us
    pallas_call x1, Pallas kernels, per_device(): pl.pallas_call(filter_kernel, out_shape=results, grid=(STEPS,), in_specs=...  15.8 us
    pallas_call x1, Pallas kernels, per_device(): pl.pallas_call(front_kernel, out_shape=(act, act, act, act, window_shape,...  13.5 us
    all_to_all x1, starting transfers between devices, per_device(): packed = lax.all_to_all(packed, 'seq', 0, 0, tiled=True)  11.9 us
    all_to_all x1, starting transfers between devices, per_device(): hidden_part = lax.all_to_all(hidden_part, 'chan', 0, 0, tiled=True)  6.99 us
    all_to_all x1, starting transfers between devices, per_device(): lax.all_to_all(spread, 'chan', 0, 0, tiled=True).reshape(hidden, 128)  6.37 us
    pallas_call x1, Pallas kernels, per_device(): pl.pallas_call(send_kernel, out_shape=shape((parts, 5 * lanes + hidden //...  5.12 us
    unnamed x25, local copies, waits for them, and re-layouts  3.73 us
  transfers between devices with their start and end apart: 3, of which 2 were waited for; matrix products, arithmetic and copies ran while one was open for 6% of the time, Pallas kernels for 15%

profile of v4, /device:TPU:1, one launch (start us, length us, event | category | flops | bytes accessed | tf_op | source)
XLA Modules:
  0.0 107.7 jit_solution(3716797242969633289)
XLA Ops:
  0.7 2.2 %pack.1 = f32[32,40,128]{2,1,0:T(8,128)} custom-call(bf16[256,256]{1,0:T(8,128)(2,1)} %key_ref.1, bf16[256,256]{1,0:T(8,128)(2,1)} %query_ref.3, bf16[256,256]{1,0:T(8,128)(2,1)} %cotangent_ref.3, s32[2,128]{1,0:T(2,128)} %bitcast.38), custom_call_target="tpu_custom_call" | custom-call | tf_op jit(solution)/shard_map/pack/pallas_call | solution.py:447
  2.9 11.9 %all-to-all-start = ((f32[32,40,128]{2,1,0:T(8,128)}), f32[32,40,128]{2,1,0:T(8,128)S(1)}, u32[]{:S(2)}, u32[]{:S(2)}) async-start(f32[32,40,128]{2,1,0:T(8,128)} %pack.1), calls=%async_computation | async-start | bytes 1310720 | tf_op jit(solution)/shard_map/all_to_all | solution.py:454
  14.8 0.1 sqrt_bitcast_fusion
  14.9 0.1 constant_dynamic-slice_fusion.2
  15.1 0.1 fusion.7
  15.2 0.7 copy.30.third_ref
  15.8 0.1 copy.28
  15.9 0.7 copy.29
  16.6 0.1 constant_dynamic-slice_fusion.1
  16.7 0.7 copy.32
  17.4 0.6 pad.4.first_ref
  18.0 0.7 broadcast_bitcast_fusion.param_ref
  18.7 13.5 %front.1 = (f32[64,8192]{1,0:T(8,128)}, f32[64,8192]{1,0:T(8,128)}, f32[64,8192]{1,0:T(8,128)}, f32[64,8192]{1,0:T(8,128)}, f32[256,256]{1,0:T(8,128)}, /*index=5*/f32[2,256,256]{2,1,0:T(8,128)}) custom-call(f32[40,8192]{1,0:T(8,128)} %constant.42.clone.feature_ref, f32[64,40]{1,0:T(8,128)} %pad.4.first_ref, f32[64,64]{1,0:T(8,128)} %bitcast.35, ...), custom_call_target="tpu_custom_call" | custom-call | tf_op jit(solution)/shard_map/front/pallas_call | solution.py:476
  32.2 0.7 constant_dynamic-slice_fusion.third_ref
  32.9 0.5 all-to-all-done.packed_ref
  33.5 0.9 copy-done.1
  34.4 15.8 %filter.1 = (f32[8,8,128]{2,1,0:T(8,128)}, f32[8,64]{1,0:T(8,128)}, f32[256,256]{1,0:T(8,128)}, f32[256,256]{1,0:T(8,128)}, f32[256,256]{1,0:T(8,128)}) custom-call(f32[32,40,128]{2,1,0:T(8,128)} %copy-done.1, bf16[8,256]{1,0:T(8,128)(2,1)} %bitcast.37, f32[256,8]{1,0:T(8,128)} %broadcast_bitcast_fusion.param_ref, f32[256,256]{1,0:T(8,128)} %get-tuple-element.29.window_ref, ...), custom_call_target="tpu_custom_call" | custom-call | tf_op jit(solution)/shard_map/filter/pallas_call | solution.py:491
  50.2 7.0 %all-to-all-start.1 = ((f32[8,8,128]{2,1,0:T(8,128)}), f32[8,8,128]{2,1,0:T(8,128)S(1)}, u32[]{:S(2)}, u32[]{:S(2)}) async-start(f32[8,8,128]{2,1,0:T(8,128)} %get-tuple-element.39), calls=%async_computation.1 | async-start | bytes 65536 | tf_op jit(solution)/shard_map/all_to_all | solution.py:508
  57.2 0.7 dynamic-slice_bitcast_fusion
  57.9 0.1 fusion.4
  58.0 0.1 pad_add_fusion
  58.1 0.2 fusion
  58.3 0.8 fusion.1.value_ref
  59.1 5.1 %send.1 = f32[32,48,128]{2,1,0:T(8,128)} custom-call(f32[32,40,128]{2,1,0:T(8,128)} %copy-done.1, f32[256,8]{1,0:T(8,128)} %broadcast_bitcast_fusion.param_ref, f32[256,256]{1,0:T(8,128)} %get-tuple-element.35.embedded_ref, f32[256,256]{1,0:T(8,128)} %get-tuple-element.36.inner_ref, f32[256,256]{1,0:T(8,128)} %get-tuple-element.37.grad_ref, ...), custom_call_target="tpu_custom_call" | custom-call | tf_op jit(solution)/shard_map/send/pallas_call | solution.py:509
  64.3 0.7 broadcast_dynamic-update-slice_fusion
  64.9 29.6 %all_to_all.20.packed_ref = f32[32,48,128]{2,1,0:T(8,128)S(1)} all-to-all(f32[32,48,128]{2,1,0:T(8,128)} %broadcast_dynamic-update-slice_fusion), channel_id=1, replica_groups=mesh['seq'=32,'chan'=8] {'seq'}, dimensions={0} | all-to-all | bytes 1572864 | tf_op jit(solution)/shard_map/all_to_all | solution.py:534
  94.5 0.7 broadcast_in_dim.10
  95.2 6.4 %all-to-all-start.3 = ((f32[8,8,128]{2,1,0:T(8,128)}), f32[8,8,128]{2,1,0:T(8,128)S(1)}, u32[]{:S(2)}, u32[]{:S(2)}) async-start(f32[8,8,128]{2,1,0:T(8,128)} %broadcast_in_dim.10), calls=%async_computation.3 | async-start | bytes 65536 | tf_op jit(solution)/shard_map/all_to_all | solution.py:538
  101.6 2.2 %finish.1 = (bf16[256,256]{1,0:T(8,128)(2,1)}, bf16[256,256]{1,0:T(8,128)(2,1)}, bf16[256,256]{1,0:T(8,128)(2,1)}, f32[8,256]{1,0:T(8,128)}, f32[3,256]{1,0:T(4,...) custom-call(f32[32,48,128]{2,1,0:T(8,128)} %copy-done.2, bf16[256,256]{1,0:T(8,128)(2,1)} %query_ref.3, ...), custom_call_target="tpu_custom_call" | custom-call | tf_op jit(solution)/shard_map/finish/pallas_call | solution.py:544
  103.8 2.5 %all-to-all-done.3 = f32[8,8,128]{2,1,0:T(8,128)S(1)} async-done(((f32[8,8,128]{2,1,0:T(8,128)}), f32[8,8,128]{2,1,0:T(8,128)S(1)}, u32[]{:S(2)}, u32[]{:S(2)}) %all-to-all-start.3) | async-done | bytes 32800 | tf_op jit(solution)/shard_map/all_to_all | solution.py:538
  106.4 0.7 copy.31
  107.1 0.6 copy.35
  (27 shorter events, 0.3 us)
Async XLA Ops:
  0.6 16.0 %copy-start = (bf16[256,256]{1,0:T(8,128)(2,1)S(1)}, bf16[256,256]{1,0:T(8,128)(2,1)}, u32[]{:S(2)}) copy-start(bf16[256,256]{1,0:T(8,128)(2,1)} %param.18) | copy-start | bytes 393220
  0.7 14.1 %copy-start.8 = (f32[256]{0:T(256)S(1)}, f32[256]{0:T(256)}, u32[]{:S(2)}) copy-start(f32[256]{0:T(256)} %param.22) | copy-start | bytes 3076
  0.7 14.1 %copy-start.9 = (f32[256]{0:T(256)S(1)}, f32[256]{0:T(256)}, u32[]{:S(2)}) copy-start(f32[256]{0:T(256)} %param.26) | copy-start | bytes 3076
  0.7 14.2 %copy-start.6 = (f32[3,256]{1,0:T(4,128)S(1)}, f32[3,256]{1,0:T(4,128)}, u32[]{:S(2)}) copy-start(f32[3,256]{1,0:T(4,128)} %param.19) | copy-start | bytes 9220
  0.7 14.4 %copy-start.4 = (f32[64,256]{1,0:T(8,128)S(1)}, f32[64,256]{1,0:T(8,128)}, u32[]{:S(2)}) copy-start(f32[64,256]{1,0:T(8,128)} %param.25) | copy-start | bytes 196612
  0.7 15.1 %copy-start.5 = (f32[33,64]{1,0:T(8,128)S(1)}, f32[33,64]{1,0:T(8,128)}, u32[]{:S(2)}) copy-start(f32[33,64]{1,0:T(8,128)} %param.23) | copy-start | bytes 25348
  0.7 15.2 %copy-start.3 = (f32[64,64]{1,0:T(8,128)S(1)}, f32[64,64]{1,0:T(8,128)}, u32[]{:S(2)}) copy-start(f32[64,64]{1,0:T(8,128)} %second_ref.1) | copy-start | bytes 49156
  2.9 30.5 %all-to-all-start = ((f32[32,40,128]{2,1,0:T(8,128)}), f32[32,40,128]{2,1,0:T(8,128)S(1)}, u32[]{:S(2)}, u32[]{:S(2)}) async-start(f32[32,40,128]{2,1,0:T(8,128)} %pack.1), calls=%async_computation | async-start | bytes 1310720 | tf_op jit(solution)/shard_map/all_to_all | solution.py:454
  33.5 0.9 copy-start.1
  34.4 23.6 %copy-start.7 = (s32[256]{0:T(256)S(1)}, s32[256]{0:T(256)}, u32[]{:S(2)}) copy-start(s32[256]{0:T(256)} %param.17) | copy-start | bytes 3076
  50.2 14.0 %all-to-all-start.1 = ((f32[8,8,128]{2,1,0:T(8,128)}), f32[8,8,128]{2,1,0:T(8,128)S(1)}, u32[]{:S(2)}, u32[]{:S(2)}) async-start(f32[8,8,128]{2,1,0:T(8,128)} %get-tuple-element.39), calls=%async_computation.1 | async-start | bytes 65536 | tf_op jit(solution)/shard_map/all_to_all | solution.py:508
  94.5 7.1 %copy-start.2 = (f32[32,48,128]{2,1,0:T(8,128)}, f32[32,48,128]{2,1,0:T(8,128)S(1)}, u32[]{:S(2)}) copy-start(f32[32,48,128]{2,1,0:T(8,128)S(1)} %all_to_all.20.packed_ref) | copy-start | bytes 2359300
  95.2 11.1 %all-to-all-start.3 = ((f32[8,8,128]{2,1,0:T(8,128)}), f32[8,8,128]{2,1,0:T(8,128)S(1)}, u32[]{:S(2)}, u32[]{:S(2)}) async-start(f32[8,8,128]{2,1,0:T(8,128)} %broadcast_in_dim.10), calls=%async_computation.3 | async-start | bytes 65536 | tf_op jit(solution)/shard_map/all_to_all | solution.py:538

commit v5 on v4

--- a/solution.py
+++ b/solution.py
@@ -45,7 +45,7 @@
     phases = frequency[:, None] * positions[None, :] % length
     angles = two_pi * phases / length
     table = np.concatenate([positions[None, :] / length, np.cos(angles), np.sin(angles)], axis=0)
-    spare = -table.shape[0] % 8
+    spare = -table.shape[0] % 16
     return np.asarray(np.pad(table, ((0, spare), (0, 0))), np.float32)
 
 
@@ -68,6 +68,15 @@
 
 def product_last(left, right):
     return product(left, right, dot_last)
+
+
+def deep(pair):
+    return jnp.concatenate([pair[0], pair[0], pair[1]], axis=0)
+
+
+def wide(matrix):
+    upper = lax.reduce_precision(matrix, 8, 7)
+    return jnp.concatenate([upper, matrix - upper, upper], axis=1).astype(bf16)
 
 
 def sine_cosine(angle):
@@ -179,9 +188,9 @@
     in_hi,
     in_lo,
     turn_ref,
-    act_one_ref,
+    upper_ref,
+    lower_ref,
     cos_one_ref,
-    act_two_ref,
     cos_two_ref,
     window_ref,
     spec_ref,
@@ -192,15 +201,17 @@
     half, rows = window_ref.shape
     length = half // lanes * rows
     block = feature_ref.shape[1]
-    pre_one = product(split(first_ref[...]), split(feature_ref[...]))
-    act_one, cos_one = sine_cosine(pre_one)
-    act_one_ref[...] = act_one
+    feature = split(feature_ref[...])
+    act_one, cos_one = sine_cosine(dot(first_ref[...], deep(feature)))
     cos_one_ref[...] = cos_one
-    pre_two = product(split(second_ref[...]), split(act_one))
-    act_two, cos_two = sine_cosine(pre_two)
-    act_two_ref[...] = act_two
+    act_one = split(act_one)
+    act_two, cos_two = sine_cosine(dot(second_ref[...], deep(act_one)))
     cos_two_ref[...] = cos_two
-    shaped = product(split(third_ref[...]), split(act_two))
+    act_two = split(act_two)
+    shaped = dot(third_ref[...], deep(act_two))
+    for ref, half_of in ((upper_ref, 0), (lower_ref, 1)):
+        both = (act_two[half_of], act_one[half_of], feature[half_of])
+        ref[...] = jnp.concatenate(both, axis=0)
     count = block // rows
     for part in range(count):
         place = pl.multiple_of((step * count + part) * lanes, lanes)
@@ -256,22 +267,20 @@
     in_hi,
     in_lo,
     turn_ref,
-    feature_ref,
-    act_one_ref,
+    upper_ref,
+    lower_ref,
     cos_one_ref,
-    act_two_ref,
     cos_two_ref,
     second_ref,
     third_ref,
     spec_ref,
     hidden_ref,
-    third_acc,
+    third_part_ref,
     embedded_ref,
     inner_ref,
     grad_ref,
     shaped_ref,
-    second_acc,
-    first_acc,
+    acc_ref,
 ):
     step = pl.program_id(0)
     parts = packed_ref.shape[0]
@@ -283,9 +292,7 @@
 
     @pl.when(step == 0)
     def _():
-        third_acc[...] = jnp.zeros_like(third_acc)
-        second_acc[...] = jnp.zeros_like(second_acc)
-        first_acc[...] = jnp.zeros_like(first_acc)
+        acc_ref[...] = jnp.zeros_like(acc_ref)
         table = embed_ref[...]
 
         def look_up(part, carry):
@@ -312,27 +319,33 @@
         inner_ref[...] = back(times(keyed_spec, filter_spec)) + skip_gain * keyed
         grad_ref[...] = back(against(filter_spec, grad_spec)) + skip_gain * grad_z
 
-    block = feature_ref.shape[1]
+    block = upper_ref.shape[1]
     count = block // rows
     pieces = []
     for part in range(count):
         place = pl.multiple_of((step * count + part) * lanes, lanes)
         pieces.append(shaped_ref[pl.ds(place, lanes), :])
-    grad_shaped = split(jnp.concatenate(pieces, axis=1))
-    act_two = split(act_two_ref[...])
-    third_acc[...] += product_last(grad_shaped, act_two)
-    grad_pre_two = product(split(third_ref[...]), grad_shaped) * cos_two_ref[...]
-    grad_pre_two = split(grad_pre_two)
-    second_acc[...] += product_last(split(act_one_ref[...]), grad_pre_two)
-    grad_pre_one = product(split(second_ref[...]), grad_pre_two) * cos_one_ref[...]
-    first_acc[...] += product_last(split(grad_pre_one), split(feature_ref[...]))
+    grad_shaped = jnp.concatenate(pieces, axis=1)
+    grad_shaped = split(jnp.concatenate([grad_shaped, jnp.zeros_like(grad_shaped)], axis=0))
+    grad_pre_two = split(dot(third_ref[...], deep(grad_shaped)) * cos_two_ref[...])
+    grad_pre_one = split(dot(second_ref[...], deep(grad_pre_two)) * cos_one_ref[...])
+    left = [
+        jnp.concatenate([grad_shaped[i], grad_pre_two[i], grad_pre_one[i]], axis=0) for i in range(2)
+    ]
+    count = left[0].shape[0]
+    both = dot_last(jnp.concatenate(left, axis=0), upper_ref[...])
+    acc_ref[...] += both[:count] + both[count:] + dot_last(left[0], lower_ref[...])
 
     @pl.when(step == STEPS - 1)
     def _():
-        spare = jnp.zeros((hidden, hidden - first_acc.shape[1]), f32)
-        joined = (second_acc[...], first_acc[...], spare)
         inv_root = 1.0 / math.sqrt(length)
-        hidden_ref[...] = (jnp.concatenate(joined, axis=1) * inv_root).reshape(hidden_ref.shape)
+        two, one = 2 * lanes, 2 * lanes + hidden
+        third_part_ref[...] = acc_ref[0:lanes, 0:hidden]
+        second_part = acc_ref[two:one, hidden : 2 * hidden]
+        first_part = acc_ref[one:, 2 * hidden :]
+        spare = jnp.zeros((hidden, hidden - first_part.shape[1]), f32)
+        joined = jnp.concatenate([second_part, first_part, spare], axis=1) * inv_root
+        hidden_ref[...] = joined.reshape(hidden_ref.shape)
 
 
 def send_kernel(
@@ -470,21 +483,25 @@
     still = lambda array: pl.BlockSpec(array.shape, lambda i: (0,) * array.ndim)
     moving = lambda count: pl.BlockSpec((count, block), lambda i: (0, i))
 
-    act = shape((hidden, length), f32)
+    act, joint = shape((hidden, length), f32), shape((2 * hidden + feats, length), bf16)
     window_shape, spec_shape = shape((half, rows), f32), shape((2, half, rows), f32)
-    second_t, third_t = weight_second.T, third_own.T
-    act_one, cos_one, act_two, cos_two, window, spec = pl.pallas_call(
+    first_t, second_t, third_t = wide(first_t), wide(weight_second.T), wide(third_own.T)
+    upper, lower, cos_one, cos_two, window, spec = pl.pallas_call(
         front_kernel,
-        out_shape=(act, act, act, act, window_shape, spec_shape),
+        out_shape=(joint, joint, act, act, window_shape, spec_shape),
         grid=(STEPS,),
         in_specs=[moving(feats)]
         + [still(a) for a in (first_t, second_t, third_t, params, stage, in_hi, in_lo, turns)],
-        out_specs=[moving(hidden)] * 4 + [still(window_shape), still(spec_shape)],
+        out_specs=[moving(2 * hidden + feats)] * 2
+        + [moving(hidden)] * 2
+        + [still(window_shape), still(spec_shape)],
         scratch_shapes=[pltpu.VMEM((half, rows), f32)],
         name="front",
     )(features, first_t, second_t, third_t, params, stage, in_hi, in_lo, turns)
 
     operands = (packed, embed_own, params, window, stage, stage_back, in_hi, in_lo, turns)
+    second_own = wide(weight_second)
+    third_wide = wide(jnp.pad(third_own, ((0, 0), (0, lanes))))
     hidden_shape = shape((groups, hidden // groups, 128), f32)
     third_shape = shape((lanes, hidden), f32)
     results = (hidden_shape, third_shape) + (window_shape,) * 3
@@ -493,17 +510,16 @@
         out_shape=results,
         grid=(STEPS,),
         in_specs=[still(a) for a in operands]
-        + [moving(feats)]
-        + [moving(hidden)] * 4
-        + [still(weight_second), still(third_own), still(spec)],
+        + [moving(2 * hidden + feats)] * 2
+        + [moving(hidden)] * 2
+        + [still(second_own), still(third_wide), still(spec)],
         out_specs=[still(a) for a in results],
         scratch_shapes=[
             pltpu.VMEM((half, rows), f32),
-            pltpu.VMEM((hidden, hidden), f32),
-            pltpu.VMEM((hidden, feats), f32),
+            pltpu.VMEM((2 * lanes + 2 * hidden, 2 * hidden + feats), f32),
         ],
         name="filter",
-    )(*operands, features, act_one, cos_one, act_two, cos_two, weight_second, third_own, spec)
+    )(*operands, upper, lower, cos_one, cos_two, second_own, third_wide, spec)
 
     hidden_part = lax.all_to_all(hidden_part, "chan", 0, 0, tiled=True)
     sent = pl.pallas_call(
@@ -530,13 +546,12 @@
         + short_conv[1] * embedded[1:-1]
         + short_conv[2] * embedded[:-2]
     )
-    sent, value_rows = lax.optimization_barrier((sent, value_rows))
     got = lax.all_to_all(sent, "seq", 0, 0, tiled=True)
 
     hidden_sum = jnp.sum(got[:, 5 * lanes :], axis=0)
     spread = jnp.broadcast_to(hidden_sum[None], (groups,) + hidden_sum.shape)
     total = lax.all_to_all(spread, "chan", 0, 0, tiled=True).reshape(hidden, 128)
-    grad_second = total[:, :hidden]
+    grad_second = total[:, :hidden].T
     grad_first = total[:, hidden : hidden + weight_first.shape[0]].T
 
     rows_shape = shape((rows, width), bf16)

time: 108 us -> 105 us (0.972)
  blocking collectives: 29.6 us -> 0 us
  waiting for transfers between devices: 3.04 us -> 22.9 us
  starting transfers between devices: 25.2 us -> 32.9 us
  other arithmetic: 1.08 us -> 4.67 us
  Pallas kernels: 38.9 us -> 36.3 us
  local copies, waits for them, and re-layouts: 8.91 us -> 6.49 us
    all_to_all x1 -> x0, blocking collectives: 29.6 us -> none  [per_device(): got = lax.all_to_all(sent, 'seq', 0, 0, tiled=True)]
    all_to_all x0 -> x1, waiting for transfers between devices: none -> 20.2 us  [per_device(): got = lax.all_to_all(sent, 'seq', 0, 0, tiled=True)]
    all_to_all x0 -> x1, starting transfers between devices: none -> 6.98 us  [per_device(): got = lax.all_to_all(sent, 'seq', 0, 0, tiled=True)]
    concatenate x0 -> x5, other arithmetic: none -> 3.46 us  [wide(): return jnp.concatenate([upper, matrix - upper, upper], axis=1).astype(bf16)]
    pallas_call x1, Pallas kernels: 13.5 us -> 12 us  [per_device(): pl.pallas_call(front_kernel, out_shape=(joint, joint, act, act, window_sh...]
  transfers between devices with their start and end apart: 3 -> 4, of which waited for: 2 -> 3; matrix products, arithmetic and copies ran while one was open for 6% -> 7% of each run, Pallas kernels for 15% -> 14%
where the time goes in v5:
time: 105 us; the launch traced here: 104 us
  Pallas kernels  36.3 us (35%)
  starting transfers between devices  32.9 us (31%)
  waiting for transfers between devices  22.9 us (22%)
  local copies, waits for them, and re-layouts  6.49 us (6%)
  other arithmetic  4.67 us (4%)
    all_to_all x1, waiting for transfers between devices, per_device(): got = lax.all_to_all(sent, 'seq', 0, 0, tiled=True)  20.2 us
    pallas_call x1, Pallas kernels, per_device(): pl.pallas_call(filter_kernel, out_shape=results, grid=(STEPS,), in_specs=...  14.9 us
    pallas_call x1, Pallas kernels, per_device(): pl.pallas_call(front_kernel, out_shape=(joint, joint, act, act, window_sh...  12 us
    all_to_all x1, starting transfers between devices, per_device(): packed = lax.all_to_all(packed, 'seq', 0, 0, tiled=True)  11.9 us
    all_to_all x1, starting transfers between devices, per_device(): lax.all_to_all(spread, 'chan', 0, 0, tiled=True).reshape(hidden, 128)  7.1 us
    all_to_all x1, starting transfers between devices, per_device(): got = lax.all_to_all(sent, 'seq', 0, 0, tiled=True)  6.98 us
    all_to_all x1, starting transfers between devices, per_device(): hidden_part = lax.all_to_all(hidden_part, 'chan', 0, 0, tiled=True)  6.97 us
    pallas_call x1, Pallas kernels, per_device(): pl.pallas_call(send_kernel, out_shape=shape((parts, 5 * lanes + hidden //...  5.11 us
  transfers between devices with their start and end apart: 4, of which 3 were waited for; matrix products, arithmetic and copies ran while one was open for 7% of the time, Pallas kernels for 14%

profile of v5, /device:TPU:1, one launch (start us, length us, event | category | flops | bytes accessed | tf_op | source)
XLA Modules:
  0.0 104.4 jit_solution(10381524051126079188)
XLA Ops:
  0.7 2.2 %pack.1 = f32[32,40,128]{2,1,0:T(8,128)} custom-call(bf16[256,256]{1,0:T(8,128)(2,1)} %key_ref.1, bf16[256,256]{1,0:T(8,128)(2,1)} %query_ref.3, bf16[256,256]{1,0:T(8,128)(2,1)} %cotangent_ref.3, s32[2,128]{1,0:T(2,128)} %bitcast.41), custom_call_target="tpu_custom_call" | custom-call | tf_op jit(solution)/shard_map/pack/pallas_call | solution.py:460
  2.9 11.9 %all-to-all-start = ((f32[32,40,128]{2,1,0:T(8,128)}), f32[32,40,128]{2,1,0:T(8,128)S(1)}, u32[]{:S(2)}, u32[]{:S(2)}) async-start(f32[32,40,128]{2,1,0:T(8,128)} %pack.1), calls=%async_computation | async-start | bytes 1310720 | tf_op jit(solution)/shard_map/all_to_all | solution.py:467
  14.9 0.1 reduce-precision_subtract_fusion.2
  15.1 0.1 copy.49
  15.3 0.1 constant_dynamic-slice_fusion.1
  15.4 0.7 pad_maximum_fusion.4.third_ref
  16.0 0.1 sqrt_bitcast_fusion
  16.3 0.7 copy.56
  17.0 0.7 pad_maximum_fusion.first_ref
  17.7 0.7 pad_maximum_fusion.1.second_ref
  18.4 0.7 broadcast_bitcast_fusion.param_ref
  19.1 12.0 %front.1 = (bf16[176,8192]{1,0:T(8,128)(2,1)}, bf16[176,8192]{1,0:T(8,128)(2,1)}, f32[64,8192]{1,0:T(8,128)}, f32[64,8192]{1,0:T(8,128)}, f32[256,256]{1,0:T(8,128)}, /*index=5*/f32[2,256,256]{2,1,0:T(8,128)}) custom-call(f32[48,8192]{1,0:T(8,128)} %constant.42.clone.feature_ref, bf16[64,144]{1,0:T(8,128)(2,1)} %pad_maximum_fusion.first_ref, ...), custom_call_target="tpu_custom_call" | custom-call | tf_op jit(solution)/shard_map/front/pallas_call | solution.py:489
  31.1 0.7 pad_maximum_fusion.3.third_ref
  31.8 0.7 pad_maximum_fusion.2.second_ref
  32.5 1.0 all-to-all-done.packed_ref
  33.5 0.9 copy-done.1
  34.3 14.9 %filter.1 = (f32[8,8,128]{2,1,0:T(8,128)}, f32[8,64]{1,0:T(8,128)}, f32[256,256]{1,0:T(8,128)}, f32[256,256]{1,0:T(8,128)}, f32[256,256]{1,0:T(8,128)}) custom-call(f32[32,40,128]{2,1,0:T(8,128)} %copy-done.1, bf16[8,256]{1,0:T(8,128)(2,1)} %bitcast.40, f32[256,8]{1,0:T(8,128)} %broadcast_bitcast_fusion.param_ref, f32[256,256]{1,0:T(8,128)} %get-tuple-element.27.window_ref, ...), custom_call_target="tpu_custom_call" | custom-call | tf_op jit(solution)/shard_map/filter/pallas_call | solution.py:508
  49.2 7.0 %all-to-all-start.1 = ((f32[8,8,128]{2,1,0:T(8,128)}), f32[8,8,128]{2,1,0:T(8,128)S(1)}, u32[]{:S(2)}, u32[]{:S(2)}) async-start(f32[8,8,128]{2,1,0:T(8,128)} %get-tuple-element.37), calls=%async_computation.1 | async-start | bytes 65536 | tf_op jit(solution)/shard_map/all_to_all | solution.py:524
  56.2 5.1 %send.1 = f32[32,48,128]{2,1,0:T(8,128)} custom-call(f32[32,40,128]{2,1,0:T(8,128)} %copy-done.1, f32[256,8]{1,0:T(8,128)} %broadcast_bitcast_fusion.param_ref, f32[256,256]{1,0:T(8,128)} %get-tuple-element.33.embedded_ref, f32[256,256]{1,0:T(8,128)} %get-tuple-element.34.inner_ref, f32[256,256]{1,0:T(8,128)} %get-tuple-element.35.grad_ref, ...), custom_call_target="tpu_custom_call" | custom-call | tf_op jit(solution)/shard_map/send/pallas_call | solution.py:525
  61.3 0.7 broadcast_dynamic-update-slice_fusion
  62.0 7.0 %all-to-all-start.2 = ((f32[32,48,128]{2,1,0:T(8,128)}), f32[32,48,128]{2,1,0:T(8,128)S(1)}, u32[]{:S(2)}, u32[]{:S(2)}) async-start(f32[32,48,128]{2,1,0:T(8,128)} %broadcast_dynamic-update-slice_fusion), calls=%async_computation.2 | async-start | bytes 1572864 | tf_op jit(solution)/shard_map/all_to_all | solution.py:549
  69.0 0.7 dynamic-slice_bitcast_fusion
  69.7 0.1 fusion.8
  69.9 0.2 fusion
  70.1 20.2 %all-to-all-done.2.packed_ref = f32[32,48,128]{2,1,0:T(8,128)S(1)} async-done(((f32[32,48,128]{2,1,0:T(8,128)}), f32[32,48,128]{2,1,0:T(8,128)S(1)}, u32[]{:S(2)}, u32[]{:S(2)}) %all-to-all-start.2) | async-done | bytes 786464 | tf_op jit(solution)/shard_map/all_to_all | solution.py:549
  90.4 0.7 broadcast_in_dim.10
  91.1 7.1 %all-to-all-start.3 = ((f32[8,8,128]{2,1,0:T(8,128)}), f32[8,8,128]{2,1,0:T(8,128)S(1)}, u32[]{:S(2)}, u32[]{:S(2)}) async-start(f32[8,8,128]{2,1,0:T(8,128)} %broadcast_in_dim.10), calls=%async_computation.3 | async-start | bytes 65536 | tf_op jit(solution)/shard_map/all_to_all | solution.py:553
  98.2 0.8 fusion.1.value_ref
  99.0 2.2 %finish.1 = (bf16[256,256]{1,0:T(8,128)(2,1)}, bf16[256,256]{1,0:T(8,128)(2,1)}, bf16[256,256]{1,0:T(8,128)(2,1)}, f32[8,256]{1,0:T(8,128)}, f32[3,256]{1,0:T(4,...) custom-call(f32[32,48,128]{2,1,0:T(8,128)} %copy-done.2, bf16[256,256]{1,0:T(8,128)(2,1)} %query_ref.3, ...), custom_call_target="tpu_custom_call" | custom-call | tf_op jit(solution)/shard_map/finish/pallas_call | solution.py:559
  101.2 1.7 %all-to-all-done.3 = f32[8,8,128]{2,1,0:T(8,128)S(1)} async-done(((f32[8,8,128]{2,1,0:T(8,128)}), f32[8,8,128]{2,1,0:T(8,128)S(1)}, u32[]{:S(2)}, u32[]{:S(2)}) %all-to-all-start.3) | async-done | bytes 32800 | tf_op jit(solution)/shard_map/all_to_all | solution.py:553
  103.0 0.7 copy.55
  103.7 0.7 copy.54
  (38 shorter events, 0.7 us)
Async XLA Ops:
  0.6 14.6 %copy-start = (bf16[256,256]{1,0:T(8,128)(2,1)S(1)}, bf16[256,256]{1,0:T(8,128)(2,1)}, u32[]{:S(2)}) copy-start(bf16[256,256]{1,0:T(8,128)(2,1)} %param.18) | copy-start | bytes 393220
  0.7 14.1 %copy-start.6 = (f32[3,256]{1,0:T(4,128)S(1)}, f32[3,256]{1,0:T(4,128)}, u32[]{:S(2)}) copy-start(f32[3,256]{1,0:T(4,128)} %param.19) | copy-start | bytes 9220
  0.7 14.2 %copy-start.5 = (f32[64,256]{1,0:T(8,128)S(1)}, f32[64,256]{1,0:T(8,128)}, u32[]{:S(2)}) copy-start(f32[64,256]{1,0:T(8,128)} %param.25) | copy-start | bytes 196612
  0.7 14.4 %copy-start.4 = (f32[33,64]{1,0:T(8,128)S(1)}, f32[33,64]{1,0:T(8,128)}, u32[]{:S(2)}) copy-start(f32[33,64]{1,0:T(8,128)} %param.23) | copy-start | bytes 25348
  0.7 15.3 %copy-start.8 = (f32[256]{0:T(256)S(1)}, f32[256]{0:T(256)}, u32[]{:S(2)}) copy-start(f32[256]{0:T(256)} %param.22) | copy-start | bytes 3076
  0.7 15.3 %copy-start.9 = (f32[256]{0:T(256)S(1)}, f32[256]{0:T(256)}, u32[]{:S(2)}) copy-start(f32[256]{0:T(256)} %param.26) | copy-start | bytes 3076
  0.7 15.5 %copy-start.3 = (f32[64,64]{1,0:T(8,128)S(1)}, f32[64,64]{1,0:T(8,128)}, u32[]{:S(2)}) copy-start(f32[64,64]{1,0:T(8,128)} %param.24) | copy-start | bytes 49156
  2.9 30.5 %all-to-all-start = ((f32[32,40,128]{2,1,0:T(8,128)}), f32[32,40,128]{2,1,0:T(8,128)S(1)}, u32[]{:S(2)}, u32[]{:S(2)}) async-start(f32[32,40,128]{2,1,0:T(8,128)} %pack.1), calls=%async_computation | async-start | bytes 1310720 | tf_op jit(solution)/shard_map/all_to_all | solution.py:467
  33.4 0.9 copy-start.1
  49.2 12.1 %all-to-all-start.1 = ((f32[8,8,128]{2,1,0:T(8,128)}), f32[8,8,128]{2,1,0:T(8,128)S(1)}, u32[]{:S(2)}, u32[]{:S(2)}) async-start(f32[8,8,128]{2,1,0:T(8,128)} %get-tuple-element.37), calls=%async_computation.1 | async-start | bytes 65536 | tf_op jit(solution)/shard_map/all_to_all | solution.py:524
  56.2 13.7 %copy-start.7 = (s32[256]{0:T(256)S(1)}, s32[256]{0:T(256)}, u32[]{:S(2)}) copy-start(s32[256]{0:T(256)} %param.17) | copy-start | bytes 3076
  62.0 28.4 %all-to-all-start.2 = ((f32[32,48,128]{2,1,0:T(8,128)}), f32[32,48,128]{2,1,0:T(8,128)S(1)}, u32[]{:S(2)}, u32[]{:S(2)}) async-start(f32[32,48,128]{2,1,0:T(8,128)} %broadcast_dynamic-update-slice_fusion), calls=%async_computation.2 | async-start | bytes 1572864 | tf_op jit(solution)/shard_map/all_to_all | solution.py:549
  90.4 8.6 %copy-start.2 = (f32[32,48,128]{2,1,0:T(8,128)}, f32[32,48,128]{2,1,0:T(8,128)S(1)}, u32[]{:S(2)}) copy-start(f32[32,48,128]{2,1,0:T(8,128)S(1)} %all-to-all-done.2.packed_ref) | copy-start | bytes 2359300
  91.1 11.8 %all-to-all-start.3 = ((f32[8,8,128]{2,1,0:T(8,128)}), f32[8,8,128]{2,1,0:T(8,128)S(1)}, u32[]{:S(2)}, u32[]{:S(2)}) async-start(f32[8,8,128]{2,1,0:T(8,128)} %broadcast_in_dim.10), calls=%async_computation.3 | async-start | bytes 65536 | tf_op jit(solution)/shard_map/all_to_all | solution.py:553

commit v6 on v5

--- a/solution.py
+++ b/solution.py
@@ -301,7 +301,7 @@
             embedded_ref[pl.ds(place, lanes), :] = found
             return carry
 
-        lax.fori_loop(0, parts, look_up, 0, unroll=4)
+        lax.fori_loop(0, parts, look_up, 0, unroll=8)
         key_all = received(packed_ref, 0, lanes)
         grad_z = received(packed_ref, 2 * lanes, lanes)
         _, _, value = lagged_values(embedded_ref[...], param_ref, lanes)
@@ -382,7 +382,7 @@
     def collect(part, total):
         return total + dot_last(pieces_ref[part], matches(packed_ref, part, lanes, VOCAB))
 
-    total = lax.fori_loop(0, parts, collect, jnp.zeros((2 * lanes, VOCAB), f32), unroll=4)
+    total = lax.fori_loop(0, parts, collect, jnp.zeros((2 * lanes, VOCAB), f32), unroll=8)
     embed_part = total[:lanes] + total[lanes:]
     share = VOCAB // parts
     low, high = 4 * lanes, 5 * lanes

time: 105 us -> 104 us (level)
  transfers between devices with their start and end apart: 4 -> 4, of which waited for: 3 -> 4; matrix products, arithmetic and copies ran while one was open for 7% -> 7% of each run, Pallas kernels for 14% -> 14%
where the time goes in v6:
time: 104 us; the launch traced here: 103 us
  Pallas kernels  35.3 us (34%)
  starting transfers between devices  33.1 us (32%)
  waiting for transfers between devices  22.7 us (22%)
  local copies, waits for them, and re-layouts  6.49 us (6%)
  other arithmetic  4.67 us (4%)
    all_to_all x1, waiting for transfers between devices, per_device(): got = lax.all_to_all(sent, 'seq', 0, 0, tiled=True)  19.9 us
    pallas_call x1, Pallas kernels, per_device(): pl.pallas_call(filter_kernel, out_shape=results, grid=(STEPS,), in_specs=...  14.4 us
    pallas_call x1, Pallas kernels, per_device(): pl.pallas_call(front_kernel, out_shape=(joint, joint, act, act, window_sh...  12 us
    all_to_all x1, starting transfers between devices, per_device(): packed = lax.all_to_all(packed, 'seq', 0, 0, tiled=True)  11.9 us
    all_to_all x1, starting transfers between devices, per_device(): lax.all_to_all(spread, 'chan', 0, 0, tiled=True).reshape(hidden, 128)  7.32 us
    all_to_all x1, starting transfers between devices, per_device(): got = lax.all_to_all(sent, 'seq', 0, 0, tiled=True)  6.99 us
    all_to_all x1, starting transfers between devices, per_device(): hidden_part = lax.all_to_all(hidden_part, 'chan', 0, 0, tiled=True)  6.97 us
    pallas_call x1, Pallas kernels, per_device(): pl.pallas_call(send_kernel, out_shape=shape((parts, 5 * lanes + hidden //...  4.62 us
  transfers between devices with their start and end apart: 4, of which 4 were waited for; matrix products, arithmetic and copies ran while one was open for 7% of the time, Pallas kernels for 14%

profile of v6, /device:TPU:1, one launch (start us, length us, event | category | flops | bytes accessed | tf_op | source)
XLA Modules:
  0.0 103.4 jit_solution(3278964155773248691)
XLA Ops:
  0.7 2.2 %pack.1 = f32[32,40,128]{2,1,0:T(8,128)} custom-call(bf16[256,256]{1,0:T(8,128)(2,1)} %key_ref.1, bf16[256,256]{1,0:T(8,128)(2,1)} %query_ref.3, bf16[256,256]{1,0:T(8,128)(2,1)} %cotangent_ref.3, s32[2,128]{1,0:T(2,128)} %bitcast.41), custom_call_target="tpu_custom_call" | custom-call | tf_op jit(solution)/shard_map/pack/pallas_call | solution.py:460
  2.9 11.9 %all-to-all-start = ((f32[32,40,128]{2,1,0:T(8,128)}), f32[32,40,128]{2,1,0:T(8,128)S(1)}, u32[]{:S(2)}, u32[]{:S(2)}) async-start(f32[32,40,128]{2,1,0:T(8,128)} %pack.1), calls=%async_computation | async-start | bytes 1310720 | tf_op jit(solution)/shard_map/all_to_all | solution.py:467
  14.9 0.1 reduce-precision_subtract_fusion.2
  15.1 0.1 copy.49
  15.3 0.1 constant_dynamic-slice_fusion.1
  15.4 0.7 pad_maximum_fusion.4.third_ref
  16.0 0.1 sqrt_bitcast_fusion
  16.3 0.7 copy.56
  17.0 0.7 pad_maximum_fusion.first_ref
  17.7 0.7 pad_maximum_fusion.1.second_ref
  18.4 0.7 broadcast_bitcast_fusion.param_ref
  19.1 12.0 %front.1 = (bf16[176,8192]{1,0:T(8,128)(2,1)}, bf16[176,8192]{1,0:T(8,128)(2,1)}, f32[64,8192]{1,0:T(8,128)}, f32[64,8192]{1,0:T(8,128)}, f32[256,256]{1,0:T(8,128)}, /*index=5*/f32[2,256,256]{2,1,0:T(8,128)}) custom-call(f32[48,8192]{1,0:T(8,128)} %constant.42.clone.feature_ref, bf16[64,144]{1,0:T(8,128)(2,1)} %pad_maximum_fusion.first_ref, ...), custom_call_target="tpu_custom_call" | custom-call | tf_op jit(solution)/shard_map/front/pallas_call | solution.py:489
  31.1 0.7 pad_maximum_fusion.3.third_ref
  31.8 0.7 pad_maximum_fusion.2.second_ref
  32.5 1.0 all-to-all-done.packed_ref
  33.5 0.9 copy-done.1
  34.3 14.4 %filter.1 = (f32[8,8,128]{2,1,0:T(8,128)}, f32[8,64]{1,0:T(8,128)}, f32[256,256]{1,0:T(8,128)}, f32[256,256]{1,0:T(8,128)}, f32[256,256]{1,0:T(8,128)}) custom-call(f32[32,40,128]{2,1,0:T(8,128)} %copy-done.1, bf16[8,256]{1,0:T(8,128)(2,1)} %bitcast.40, f32[256,8]{1,0:T(8,128)} %broadcast_bitcast_fusion.param_ref, f32[256,256]{1,0:T(8,128)} %get-tuple-element.27.window_ref, ...), custom_call_target="tpu_custom_call" | custom-call | tf_op jit(solution)/shard_map/filter/pallas_call | solution.py:508
  48.7 7.0 %all-to-all-start.1 = ((f32[8,8,128]{2,1,0:T(8,128)}), f32[8,8,128]{2,1,0:T(8,128)S(1)}, u32[]{:S(2)}, u32[]{:S(2)}) async-start(f32[8,8,128]{2,1,0:T(8,128)} %get-tuple-element.37), calls=%async_computation.1 | async-start | bytes 65536 | tf_op jit(solution)/shard_map/all_to_all | solution.py:524
  55.7 4.6 %send.1 = f32[32,48,128]{2,1,0:T(8,128)} custom-call(f32[32,40,128]{2,1,0:T(8,128)} %copy-done.1, f32[256,8]{1,0:T(8,128)} %broadcast_bitcast_fusion.param_ref, f32[256,256]{1,0:T(8,128)} %get-tuple-element.33.embedded_ref, f32[256,256]{1,0:T(8,128)} %get-tuple-element.34.inner_ref, f32[256,256]{1,0:T(8,128)} %get-tuple-element.35.grad_ref, ...), custom_call_target="tpu_custom_call" | custom-call | tf_op jit(solution)/shard_map/send/pallas_call | solution.py:525
  60.3 0.1 all-to-all-done.1
  60.4 0.7 broadcast_dynamic-update-slice_fusion
  61.1 7.0 %all-to-all-start.2 = ((f32[32,48,128]{2,1,0:T(8,128)}), f32[32,48,128]{2,1,0:T(8,128)S(1)}, u32[]{:S(2)}, u32[]{:S(2)}) async-start(f32[32,48,128]{2,1,0:T(8,128)} %broadcast_dynamic-update-slice_fusion), calls=%async_computation.2 | async-start | bytes 1572864 | tf_op jit(solution)/shard_map/all_to_all | solution.py:549
  68.1 0.7 dynamic-slice_bitcast_fusion
  69.0 0.2 fusion
  69.3 19.9 %all-to-all-done.2.packed_ref = f32[32,48,128]{2,1,0:T(8,128)S(1)} async-done(((f32[32,48,128]{2,1,0:T(8,128)}), f32[32,48,128]{2,1,0:T(8,128)S(1)}, u32[]{:S(2)}, u32[]{:S(2)}) %all-to-all-start.2) | async-done | bytes 786464 | tf_op jit(solution)/shard_map/all_to_all | solution.py:549
  89.2 0.7 broadcast_in_dim.10
  89.9 7.3 %all-to-all-start.3 = ((f32[8,8,128]{2,1,0:T(8,128)}), f32[8,8,128]{2,1,0:T(8,128)S(1)}, u32[]{:S(2)}, u32[]{:S(2)}) async-start(f32[8,8,128]{2,1,0:T(8,128)} %broadcast_in_dim.10), calls=%async_computation.3 | async-start | bytes 65536 | tf_op jit(solution)/shard_map/all_to_all | solution.py:553
  97.2 0.8 fusion.1.value_ref
  98.0 2.2 %finish.1 = (bf16[256,256]{1,0:T(8,128)(2,1)}, bf16[256,256]{1,0:T(8,128)(2,1)}, bf16[256,256]{1,0:T(8,128)(2,1)}, f32[8,256]{1,0:T(8,128)}, f32[3,256]{1,0:T(4,...) custom-call(f32[32,48,128]{2,1,0:T(8,128)} %copy-done.2, bf16[256,256]{1,0:T(8,128)(2,1)} %query_ref.3, ...), custom_call_target="tpu_custom_call" | custom-call | tf_op jit(solution)/shard_map/finish/pallas_call | solution.py:559
  100.2 1.7 %all-to-all-done.3 = f32[8,8,128]{2,1,0:T(8,128)S(1)} async-done(((f32[8,8,128]{2,1,0:T(8,128)}), f32[8,8,128]{2,1,0:T(8,128)S(1)}, u32[]{:S(2)}, u32[]{:S(2)}) %all-to-all-start.3) | async-done | bytes 32800 | tf_op jit(solution)/shard_map/all_to_all | solution.py:553
  102.0 0.7 copy.55
  102.7 0.7 copy.54
  (38 shorter events, 0.8 us)
Async XLA Ops:
  0.6 14.6 %copy-start = (bf16[256,256]{1,0:T(8,128)(2,1)S(1)}, bf16[256,256]{1,0:T(8,128)(2,1)}, u32[]{:S(2)}) copy-start(bf16[256,256]{1,0:T(8,128)(2,1)} %param.18) | copy-start | bytes 393220
  0.7 14.1 %copy-start.6 = (f32[3,256]{1,0:T(4,128)S(1)}, f32[3,256]{1,0:T(4,128)}, u32[]{:S(2)}) copy-start(f32[3,256]{1,0:T(4,128)} %param.19) | copy-start | bytes 9220
  0.7 14.2 %copy-start.5 = (f32[64,256]{1,0:T(8,128)S(1)}, f32[64,256]{1,0:T(8,128)}, u32[]{:S(2)}) copy-start(f32[64,256]{1,0:T(8,128)} %param.25) | copy-start | bytes 196612
  0.7 14.4 %copy-start.4 = (f32[33,64]{1,0:T(8,128)S(1)}, f32[33,64]{1,0:T(8,128)}, u32[]{:S(2)}) copy-start(f32[33,64]{1,0:T(8,128)} %param.23) | copy-start | bytes 25348
  0.7 15.3 %copy-start.8 = (f32[256]{0:T(256)S(1)}, f32[256]{0:T(256)}, u32[]{:S(2)}) copy-start(f32[256]{0:T(256)} %param.22) | copy-start | bytes 3076
  0.7 15.3 %copy-start.9 = (f32[256]{0:T(256)S(1)}, f32[256]{0:T(256)}, u32[]{:S(2)}) copy-start(f32[256]{0:T(256)} %param.26) | copy-start | bytes 3076
  0.7 15.5 %copy-start.3 = (f32[64,64]{1,0:T(8,128)S(1)}, f32[64,64]{1,0:T(8,128)}, u32[]{:S(2)}) copy-start(f32[64,64]{1,0:T(8,128)} %param.24) | copy-start | bytes 49156
  2.9 30.5 %all-to-all-start = ((f32[32,40,128]{2,1,0:T(8,128)}), f32[32,40,128]{2,1,0:T(8,128)S(1)}, u32[]{:S(2)}, u32[]{:S(2)}) async-start(f32[32,40,128]{2,1,0:T(8,128)} %pack.1), calls=%async_computation | async-start | bytes 1310720 | tf_op jit(solution)/shard_map/all_to_all | solution.py:467
  33.4 0.9 copy-start.1
  48.7 11.7 %all-to-all-start.1 = ((f32[8,8,128]{2,1,0:T(8,128)}), f32[8,8,128]{2,1,0:T(8,128)S(1)}, u32[]{:S(2)}, u32[]{:S(2)}) async-start(f32[8,8,128]{2,1,0:T(8,128)} %get-tuple-element.37), calls=%async_computation.1 | async-start | bytes 65536 | tf_op jit(solution)/shard_map/all_to_all | solution.py:524
  55.7 13.3 %copy-start.7 = (s32[256]{0:T(256)S(1)}, s32[256]{0:T(256)}, u32[]{:S(2)}) copy-start(s32[256]{0:T(256)} %param.17) | copy-start | bytes 3076
  61.1 28.1 %all-to-all-start.2 = ((f32[32,48,128]{2,1,0:T(8,128)}), f32[32,48,128]{2,1,0:T(8,128)S(1)}, u32[]{:S(2)}, u32[]{:S(2)}) async-start(f32[32,48,128]{2,1,0:T(8,128)} %broadcast_dynamic-update-slice_fusion), calls=%async_computation.2 | async-start | bytes 1572864 | tf_op jit(solution)/shard_map/all_to_all | solution.py:549
  89.2 8.8 %copy-start.2 = (f32[32,48,128]{2,1,0:T(8,128)}, f32[32,48,128]{2,1,0:T(8,128)S(1)}, u32[]{:S(2)}) copy-start(f32[32,48,128]{2,1,0:T(8,128)S(1)} %all-to-all-done.2.packed_ref) | copy-start | bytes 2359300
  89.9 12.0 %all-to-all-start.3 = ((f32[8,8,128]{2,1,0:T(8,128)}), f32[8,8,128]{2,1,0:T(8,128)S(1)}, u32[]{:S(2)}, u32[]{:S(2)}) async-start(f32[8,8,128]{2,1,0:T(8,128)} %broadcast_in_dim.10), calls=%async_computation.3 | async-start | bytes 65536 | tf_op jit(solution)/shard_map/all_to_all | solution.py:553
